TPU v7x, 32 devices: a whole 2x2x4 slice. The times are simulated.
32 devices in a mesh: gx: 2 (over x), gy: 4 (over y, core), gz: 4 (over z).
Axes of the slice: x: 2, y: 2, z: 4, core: 2. Of those that a mesh axis runs over, the one named last changes fastest.
Arguments:
- positions: float32 [2, 4, 8, 3, 128], P('gx', 'gy', 'gz'), may hold values from 0 to 8, as said below
- block_fill: int32 [2, 4, 8], P('gx', 'gy', 'gz'), may hold values from 16 to 128, as said below
- noise: float32 [2, 4, 8, 8, 384], P('gx', 'gy', 'gz'), may hold values from -6 to 6
- pair_list: int32 [2, 4, 4, 3, 54], P('gx', 'gy', 'gz'), may hold values from 0 to 26, as said below
- pair_count: int32 [2, 4, 4], P('gx', 'gy', 'gz'), may hold values from 2 to 36, as said below
Outputs:
- displacement: float32 [2, 4, 8, 8, 384], P('gx', 'gy', 'gz')
Inputs may be any that keep to these rules, and one draw needn't show every extreme that they name: `positions`: each bead of cell (x, y, z) lies in the unit cube with corner (x, y, z). `block_fill`: beads of a block occupy its first slots. `pair_list`: in each device's list, the first pair_count slots hold field 0, a block index below 2; field 1, a neighbour code 9 (dx + 1) + 3 (dy + 1) + (dz + 1) with dx, dy, dz in -1..1 whose cell lies inside the grid; field 2, the owner flag. The relation is symmetric: a pair is listed on the first block's device exactly when the reverse pair is listed on the second block's device, and exactly one of the two carries owner flag 1; every block lists itself with code 13 and flag 1. Later slots hold 0, 13, 0. `pair_count`: counts the listed pairs of the device, each block's own pair included; some device lists every neighbour inside the grid of each of its blocks.
All inputs are finite; a program needn't handle non-finite values.
Results may differ from a plain program's by a relative error of at most 0.0025.
Values may be sent and summed in bfloat16 or wider, within the bound.
No kernel may reach another device: no remote copies, remote signals or barrier semaphores. Data moves between devices by JAX's collectives and lax.ppermute only.
A program may use at most 64 MiB of HBM per device.

v0:
```python
import jax
import jax.numpy as jnp
from jax import lax
from jax.sharding import PartitionSpec as P

ITERS = 3
ROOT_ITERS = 12


radius = 0.08
floor_sq = 0.0001
epsilon = 1e-06
group_pairs = 8


def padded_2(array, sides, width):
    for axis, dim in sides:
        count, length = (lax.axis_size(axis), array.shape[dim])
        up = [(i, (i + 1) % count) for i in range(count - 1)]
        down = [(j, i) for i, j in up]
        last = lax.slice_in_dim(array, length - width, length, axis=dim)
        leading = lax.slice_in_dim(array, 0, width, axis=dim)
        before = lax.ppermute(last, axis, up)
        after = lax.ppermute(leading, axis, down)
        array = jnp.concatenate([before, array, after], axis=dim)
    return array


def mobility_tiles(first_pos, second_pos):
    offset = second_pos[:, :, None, :] - first_pos[:, :, :, None]
    dist_sq = (
        offset[:, 0] * offset[:, 0] + offset[:, 1] * offset[:, 1] + offset[:, 2] * offset[:, 2]
    )
    inverse_sq = 1.0 / jnp.maximum(dist_sq, floor_sq)
    distance = jnp.sqrt(dist_sq)
    reach_ratio = radius * jnp.sqrt(inverse_sq)
    far_iso = 0.75 * reach_ratio * (1.0 + 2.0 / 3.0 * radius * radius * inverse_sq)
    far_dyad = 0.75 * reach_ratio * (1.0 - 2.0 * radius * radius * inverse_sq)
    near_iso = 1.0 - 9.0 / 32.0 * distance / radius
    near_dyad = 3.0 / 32.0 * distance / radius
    apart = dist_sq >= 4.0 * radius * radius
    isotropic = jnp.where(apart, far_iso, near_iso)
    dyadic = jnp.where(apart, far_dyad, near_dyad) * inverse_sq
    identity_three = jnp.eye(3, dtype=jnp.float32)
    offset_t = jnp.transpose(offset, (0, 2, 1, 3))
    product = offset[:, :, :, None, :] * offset_t[:, None, :, :, :]
    mobility = (
        identity_three[None, :, None, :, None] * isotropic[:, None, :, None, :]
        + dyadic[:, None, :, None, :] * product
    )
    group_size = first_pos.shape[0]
    bead_count = first_pos.shape[2]
    return mobility.reshape(group_size, 3 * bead_count, 3 * bead_count).astype(jnp.bfloat16)


def inverse_three(matrix):
    cofactor = [
        [
            matrix[(line_index + 1) % 3][(place_index + 1) % 3]
            * matrix[(line_index + 2) % 3][(place_index + 2) % 3]
            - matrix[(line_index + 1) % 3][(place_index + 2) % 3]
            * matrix[(line_index + 2) % 3][(place_index + 1) % 3]
            for place_index in range(3)
        ]
        for line_index in range(3)
    ]
    determinant = (
        matrix[0][0] * cofactor[0][0]
        + matrix[0][1] * cofactor[0][1]
        + matrix[0][2] * cofactor[0][2]
    )
    return [
        [cofactor[place_index][line_index] / determinant for place_index in range(3)]
        for line_index in range(3)
    ]


def root_first_column(diagonal, coupling):
    zero_entry = jnp.zeros_like(diagonal[0])
    one_entry = jnp.ones_like(diagonal[0])
    trace_scale = (diagonal[0] + diagonal[1] + diagonal[2]) / 3.0
    tridiagonal = [
        [diagonal[0], coupling[0], zero_entry],
        [coupling[0], diagonal[1], coupling[1]],
        [zero_entry, coupling[1], diagonal[2]],
    ]
    root_guess = [
        [matrix_entry / trace_scale for matrix_entry in matrix_line] for matrix_line in tridiagonal
    ]
    partner = [
        [one_entry if line_index == place_index else zero_entry for place_index in range(3)]
        for line_index in range(3)
    ]
    for repeat_index in range(ROOT_ITERS):
        inverse_partner = inverse_three(partner)
        inverse_guess = inverse_three(root_guess)
        root_guess, partner = (
            [
                [
                    0.5
                    * (
                        root_guess[line_index][place_index]
                        + inverse_partner[line_index][place_index]
                    )
                    for place_index in range(3)
                ]
                for line_index in range(3)
            ],
            [
                [
                    0.5
                    * (partner[line_index][place_index] + inverse_guess[line_index][place_index])
                    for place_index in range(3)
                ]
                for line_index in range(3)
            ],
        )
    root_scale = jnp.sqrt(trace_scale)
    return [root_scale * root_guess[line_index][0] for line_index in range(3)]


def local_dot(left, right):
    return jnp.sum(left * right, axis=(0, 1, 2, 4))


def neighbour_index(block_ids, neighbour_codes, padded_depth):
    return (
        (neighbour_codes // 9 * 3 + neighbour_codes // 3 % 3) * padded_depth
        + block_ids
        + neighbour_codes % 3
    )


def fold_rims(extended, along_dim):
    inner_size = extended.shape[along_dim] - 4
    inner_part = lax.slice_in_dim(extended, 2, 2 + inner_size, axis=along_dim)
    lower_rim = lax.slice_in_dim(extended, 0, 1, axis=along_dim)
    upper_rim = lax.slice_in_dim(extended, inner_size + 3, inner_size + 4, axis=along_dim)
    lower_pad = [(0, 0)] * extended.ndim
    upper_pad = [(0, 0)] * extended.ndim
    lower_pad[along_dim] = (0, inner_size - 1)
    upper_pad[along_dim] = (inner_size - 1, 0)
    return inner_part + jnp.pad(lower_rim, lower_pad) + jnp.pad(upper_rim, upper_pad)


def body(positions, block_fill, noise, pair_list, pair_count):
    blocks = positions.shape[2]
    bead_count = positions.shape[4]
    samples = noise.shape[3]
    row_width = 3 * bead_count
    padded_depth = blocks + 2
    padded_cells = 9 * padded_depth
    capacity = pair_list.shape[4]
    bead_slots = lax.broadcasted_iota(jnp.int32, (1, 1, blocks, bead_count), 3)
    live_mask = jnp.tile((bead_slots < block_fill[..., None]).astype(jnp.float32), (1, 1, 1, 3))[
        :, :, :, None, :
    ]
    padded_pos = padded_2(positions, (("gx", 0), ("gy", 1), ("gz", 2)), 1).reshape(
        padded_cells, 3, bead_count
    )
    block_ids = pair_list[0, 0, 0, 0]
    neighbour_codes = pair_list[0, 0, 0, 1]
    owner_flags = pair_list[0, 0, 0, 2]
    pair_total = pair_count[0, 0, 0]
    slot_ids = lax.iota(jnp.int32, capacity)
    chosen = jnp.logical_and(slot_ids < pair_total, owner_flags == 1)
    ranked_order = jnp.argsort(jnp.where(chosen, slot_ids, slot_ids + capacity), stable=True)
    block_ids = block_ids[ranked_order]
    neighbour_codes = neighbour_codes[ranked_order]
    pair_total = jnp.sum(chosen.astype(jnp.int32))
    home_index = 4 * padded_depth + 1 + block_ids
    away_index = neighbour_index(block_ids, neighbour_codes, padded_depth)
    group_turns = (pair_total + group_pairs - 1) // group_pairs

    def select_group(group_index):
        slot_index = group_index * group_pairs + lax.iota(jnp.int32, group_pairs)
        valid_mask = (slot_index < pair_total).astype(jnp.float32)
        return (jnp.minimum(slot_index, capacity - 1), valid_mask)

    start_vec = noise * live_mask
    start_norm = jnp.sqrt(lax.psum(local_dot(start_vec, start_vec), ("gx", "gy", "gz")) + epsilon)
    current = start_vec / start_norm[:, None]
    previous = jnp.zeros_like(current)
    beta_prev = jnp.zeros((samples,), jnp.float32)
    basis = []
    diagonal = []
    coupling = []
    for repeat_index in range(ITERS):
        basis.append(current)
        padded = padded_2(
            current.astype(jnp.bfloat16), (("gx", 0), ("gy", 1), ("gz", 2)), 1
        ).reshape(padded_cells, samples, row_width)

        def accumulate(group_index, running):
            slot_index, valid_mask = select_group(group_index)
            home_pick = home_index[slot_index]
            away_pick = away_index[slot_index]
            mobility = mobility_tiles(padded_pos[home_pick], padded_pos[away_pick])
            forward = jnp.einsum(
                "gsk,gmk->gsm", padded[away_pick], mobility, preferred_element_type=jnp.float32
            )
            backward = jnp.einsum(
                "gsm,gmk->gsk", padded[home_pick], mobility, preferred_element_type=jnp.float32
            )
            mirror_mask = valid_mask * (neighbour_codes[slot_index] != 13).astype(jnp.float32)
            running = running.at[home_pick].add(forward * valid_mask[:, None, None])
            return running.at[away_pick].add(backward * mirror_mask[:, None, None])

        running = lax.fori_loop(
            0, group_turns, accumulate, jnp.zeros((padded_cells, samples, row_width), jnp.float32)
        )
        partial_value = running.reshape(3, 3, padded_depth, samples, row_width)
        partial_value = fold_rims(padded_2(partial_value, (("gx", 0),), 1), 0)
        partial_value = fold_rims(padded_2(partial_value, (("gy", 1),), 1), 1)
        partial_value = fold_rims(padded_2(partial_value, (("gz", 2),), 1), 2)
        image_vec = partial_value * live_mask
        alpha_now = lax.psum(local_dot(current, image_vec), ("gx", "gy", "gz"))
        diagonal.append(alpha_now)
        if repeat_index + 1 < ITERS:
            residual = image_vec - alpha_now[:, None] * current - beta_prev[:, None] * previous
            beta_now = jnp.sqrt(
                lax.psum(local_dot(residual, residual), ("gx", "gy", "gz")) + epsilon
            )
            coupling.append(beta_now)
            previous = current
            current = residual / beta_now[:, None]
            beta_prev = beta_now
    weights = root_first_column(diagonal, coupling)
    result = (start_norm * weights[0])[:, None] * basis[0]
    for repeat_index in range(1, ITERS):
        result = result + (start_norm * weights[repeat_index])[:, None] * basis[repeat_index]
    return result


def solution(mesh):
    in_specs = (
        P("gx", "gy", "gz", None, None),
        P("gx", "gy", "gz"),
        P("gx", "gy", "gz", None, None),
        P("gx", "gy", "gz", None, None),
        P("gx", "gy", "gz"),
    )
    out_specs = P("gx", "gy", "gz", None, None)
    return jax.shard_map(body, mesh=mesh, in_specs=in_specs, out_specs=out_specs, check_vma=False)
```

profile of v0, /device:TPU:0, one launch (start us, length us, event | category | flops | bytes accessed | tf_op | source)
XLA Modules:
  0.0 794.9 jit_solution(9912883638255472303)
XLA Ops:
  1.6 42.0 %psum.42 = f32[8]{0:T(128)S(1)} all-reduce(f32[8]{0:T(128)S(1)} %multiply_reduce_fusion.4), channel_id=1, replica_groups=mesh['gx'=2,'gy'=4,'gz'=4] {'gx','gy','gz'}, use_global_device_ids=true, to_apply=%region_1.2 | all-reduce | flops 8 | bytes 64 | tf_op jit(solution)/shard_map/psum | solution.py:181
  44.4 4.2 collective-permute-start
  49.9 4.5 collective-permute-start.6
  66.2 3.8 collective-permute-start.2
  76.1 4.5 collective-permute-start.4
  82.5 4.3 collective-permute-done.5
  87.6 41.7 %while.36 = (s32[]{:T(128)}, f32[36,8,384]{2,1,0:T(8,128)}, s32[]{:T(128)}, s32[54]{0:T(128)S(1)}, s32[54]{0:T(128)S(1)}, /*index=5*/bf16[36,8,384]{2,1,0:T(8,12...) while((s32[]{:T(128)}, f32[36,8,384]{2,1,0:T(8,128)}, ...), condition=%wide.region_7.8_spmd, body=%wide.region_4.7_spmd.sunk | while | flops 47287444 | bytes 61904004 | solution.py:209
  92.8 4.6 multiply_multiply_fusion.9
  97.4 8.5 %mul.4904 = f32[8,384,384]{2,1,0:T(8,128)} reshape(f32[8,3,128,3,128]{4,3,2,1,0:T(4,128)} %multiply_multiply_fusion.9) | data formatting | bytes 9437184 | tf_op jit(solution)/shard_map/while/body/mul | solution.py:49
  105.9 4.0 mul.4905
  109.9 8.5 %mul.4906 = f32[8,384,384]{2,1,0:T(8,128)} reshape(f32[8,3,128,3,128]{4,3,2,1,0:T(4,128)} %mul.4905) | data formatting | bytes 9437184 | tf_op jit(solution)/shard_map/while/body/mul | solution.py:48
  118.7 4.4 add_convert_fusion.6
  130.4 4.6 collective-permute-start.12
  138.6 4.1 collective-permute-done.13
  145.4 5.3 collective-permute-done.15
  150.7 44.9 %collective-permute-start.16 = (f32[1,1,1,8,384]{4,3,2,1,0:T(8,128)S(1)}, f32[1,1,1,8,384]{4,3,2,1,0:T(8,128)S(1)}, u32[]{:S(2)}, u32[]{:S(2)}) collective-permute-start(f32[1,1,1,8,384]{4,3,2,1,0:T(8,128)S(1)} %get-tuple-element.598), channel_id=1, source_target_pairs={{0,1},{1,2},{2,3},{4,5},{5,6},{6,7},{8,9},{9,10},{10,11},{12,13},{... | collective-permute-start | bytes 36872 | tf_op jit(solution)/shard_map/ppermute | solution.py:23
  197.0 44.3 %collective-permute-done.17 = f32[1,1,1,8,384]{4,3,2,1,0:T(8,128)S(1)} collective-permute-done((f32[1,1,1,8,384]{4,3,2,1,0:T(8,128)S(1)}, f32[1,1,1,8,384]{4,3,2,1,0:T(8,128)S(1)}, u32[]{:S(2)}, u32[]{:S(2)}) %collective-permute-start.17) | collective-permute-done | bytes 12320 | tf_op jit(solution)/shard_map/ppermute | solution.py:24
  241.5 40.4 %psum.43 = f32[8]{0:T(128)S(1)} all-reduce(f32[8]{0:T(128)S(1)} %get-tuple-element.563), channel_id=1, replica_groups=mesh['gx'=2,'gy'=4,'gz'=4] {'gx','gy','gz'}, use_global_device_ids=true, to_apply=%region_9.10 | all-reduce | flops 8 | bytes 64 | tf_op jit(solution)/shard_map/psum | solution.py:217
  282.1 39.9 %psum.44 = f32[8]{0:T(128)S(1)} all-reduce(f32[8]{0:T(128)S(1)} %multiply_reduce_fusion.2), channel_id=1, replica_groups=mesh['gx'=2,'gy'=4,'gz'=4] {'gx','gy','gz'}, use_global_device_ids=true, to_apply=%region_11.12 | all-reduce | flops 8 | bytes 64 | tf_op jit(solution)/shard_map/psum | solution.py:222
  322.6 4.2 collective-permute-start.18
  328.2 4.2 collective-permute-done.19
  337.3 4.0 collective-permute-start.22
  343.0 4.3 collective-permute-done.23
  348.1 41.7 %while.37 = (s32[]{:T(128)}, f32[36,8,384]{2,1,0:T(8,128)}, s32[]{:T(128)}, s32[54]{0:T(128)S(1)}, s32[54]{0:T(128)S(1)}, /*index=5*/bf16[36,8,384]{2,1,0:T(8,12...) while((s32[]{:T(128)}, f32[36,8,384]{2,1,0:T(8,128)}, ...), condition=%wide.region_15.16_spmd, body=%wide.region_12.15_spmd.sunk | while | flops 47287444 | bytes 61904316 | solution.py:209
  353.3 4.6 multiply_multiply_fusion.10
  357.9 8.5 %mul.4928 = f32[8,384,384]{2,1,0:T(8,128)} reshape(f32[8,3,128,3,128]{4,3,2,1,0:T(4,128)} %multiply_multiply_fusion.10) | data formatting | bytes 9437184 | tf_op jit(solution)/shard_map/while/body/mul | solution.py:49
  366.4 4.0 mul.4929
  370.4 8.5 %mul.4930 = f32[8,384,384]{2,1,0:T(8,128)} reshape(f32[8,3,128,3,128]{4,3,2,1,0:T(4,128)} %mul.4929) | data formatting | bytes 9437184 | tf_op jit(solution)/shard_map/while/body/mul | solution.py:48
  379.2 4.4 add_convert_fusion.7
  396.5 4.7 collective-permute-done.25
  406.9 44.2 %collective-permute-start.28 = (f32[1,1,1,8,384]{4,3,2,1,0:T(8,128)S(1)}, f32[1,1,1,8,384]{4,3,2,1,0:T(8,128)S(1)}, u32[]{:S(2)}, u32[]{:S(2)}) collective-permute-start(f32[1,1,1,8,384]{4,3,2,1,0:T(8,128)S(1)} %get-tuple-element.596), channel_id=1, source_target_pairs={{0,1},{1,2},{2,3},{4,5},{5,6},{6,7},{8,9},{9,10},{10,11},{12,13},{... | collective-permute-start | bytes 36872 | tf_op jit(solution)/shard_map/ppermute | solution.py:23
  452.5 43.9 %collective-permute-done.29 = f32[1,1,1,8,384]{4,3,2,1,0:T(8,128)S(1)} collective-permute-done((f32[1,1,1,8,384]{4,3,2,1,0:T(8,128)S(1)}, f32[1,1,1,8,384]{4,3,2,1,0:T(8,128)S(1)}, u32[]{:S(2)}, u32[]{:S(2)}) %collective-permute-start.29) | collective-permute-done | bytes 12320 | tf_op jit(solution)/shard_map/ppermute | solution.py:24
  496.5 40.4 %psum.45 = f32[8]{0:T(128)S(1)} all-reduce(f32[8]{0:T(128)S(1)} %multiply_reduce_fusion.1), channel_id=1, replica_groups=mesh['gx'=2,'gy'=4,'gz'=4] {'gx','gy','gz'}, use_global_device_ids=true, to_apply=%region_17.18 | all-reduce | flops 8 | bytes 64 | tf_op jit(solution)/shard_map/psum | solution.py:217
  537.9 39.9 %psum.46 = f32[8]{0:T(128)S(1)} all-reduce(f32[8]{0:T(128)S(1)} %get-tuple-element.559), channel_id=1, replica_groups=mesh['gx'=2,'gy'=4,'gz'=4] {'gx','gy','gz'}, use_global_device_ids=true, to_apply=%region_19.20 | all-reduce | flops 8 | bytes 64 | tf_op jit(solution)/shard_map/psum | solution.py:222
  577.8 4.2 collective-permute-start.30
  583.4 4.2 collective-permute-done.31
  592.4 4.0 collective-permute-start.34
  598.2 4.3 collective-permute-done.35
  603.3 41.7 %while.38 = (s32[]{:T(128)}, f32[36,8,384]{2,1,0:T(8,128)}, s32[]{:T(128)}, s32[54]{0:T(128)S(1)}, s32[54]{0:T(128)S(1)}, /*index=5*/bf16[36,8,384]{2,1,0:T(8,12...) while((s32[]{:T(128)}, f32[36,8,384]{2,1,0:T(8,128)}, ...), condition=%wide.region_23.24_spmd, body=%wide.region_20.23_spmd.sunk | while | flops 47287444 | bytes 61904316 | solution.py:209
  608.5 4.6 multiply_multiply_fusion.11
  613.1 8.5 %mul.4952 = f32[8,384,384]{2,1,0:T(8,128)} reshape(f32[8,3,128,3,128]{4,3,2,1,0:T(4,128)} %multiply_multiply_fusion.11) | data formatting | bytes 9437184 | tf_op jit(solution)/shard_map/while/body/mul | solution.py:49
  621.6 4.0 mul.4953
  625.6 8.5 %mul.4954 = f32[8,384,384]{2,1,0:T(8,128)} reshape(f32[8,3,128,3,128]{4,3,2,1,0:T(4,128)} %mul.4953) | data formatting | bytes 9437184 | tf_op jit(solution)/shard_map/while/body/mul | solution.py:48
  634.4 4.4 add_convert_fusion.8
  651.7 4.7 collective-permute-done.37
  662.1 44.2 %collective-permute-start.40 = (f32[1,1,1,8,384]{4,3,2,1,0:T(8,128)S(1)}, f32[1,1,1,8,384]{4,3,2,1,0:T(8,128)S(1)}, u32[]{:S(2)}, u32[]{:S(2)}) collective-permute-start(f32[1,1,1,8,384]{4,3,2,1,0:T(8,128)S(1)} %get-tuple-element.594), channel_id=1, source_target_pairs={{0,1},{1,2},{2,3},{4,5},{5,6},{6,7},{8,9},{9,10},{10,11},{12,13},{... | collective-permute-start | bytes 36872 | tf_op jit(solution)/shard_map/ppermute | solution.py:23
  707.7 43.9 %collective-permute-done.41 = f32[1,1,1,8,384]{4,3,2,1,0:T(8,128)S(1)} collective-permute-done((f32[1,1,1,8,384]{4,3,2,1,0:T(8,128)S(1)}, f32[1,1,1,8,384]{4,3,2,1,0:T(8,128)S(1)}, u32[]{:S(2)}, u32[]{:S(2)}) %collective-permute-start.41) | collective-permute-done | bytes 12320 | tf_op jit(solution)/shard_map/ppermute | solution.py:24
  752.5 40.4 %psum.47 = f32[8]{0:T(128)S(1)} all-reduce(f32[8]{0:T(128)S(1)} %fusion.48), channel_id=1, replica_groups=mesh['gx'=2,'gy'=4,'gz'=4] {'gx','gy','gz'}, use_global_device_ids=true, to_apply=%region_25.26 | all-reduce | flops 8 | bytes 64 | tf_op jit(solution)/shard_map/psum | solution.py:217
  (259 shorter events, 115.8 us)
Async XLA Ops:
  43.6 279.0 %copy-start.13 = (f32[8]{0:T(128)}, f32[8]{0:T(128)S(1)}, u32[]{:S(2)}) copy-start(f32[8]{0:T(128)S(1)} %add_sqrt_fusion.2) | copy-start | bytes 100
  44.4 21.7 %collective-permute-start = (bf16[1,1,2,8,384]{4,3,2,1,0:T(8,128)(2,1)S(1)}, bf16[1,1,2,8,384]{4,3,2,1,0:T(8,128)(2,1)S(1)}, u32[]{:S(2)}, u32[]{:S(2)}) collective-permute-start(bf16[1,1,2,8,384]{4,3,2,1,0:T(8,128)(2,1)S(1)} %fusion.59), channel_id=1, source_target_pairs={{0,16},{1,17},{2,18},{3,19},{4,20},{5,21},{6,22},{7,23},{8,24},{9,... | collective-permute-start | bytes 36872 | tf_op jit(solution)/shard_map/ppermute | solution.py:23
  48.6 17.5 %collective-permute-start.1 = (bf16[1,1,2,8,384]{4,3,2,1,0:T(8,128)(2,1)S(1)}, bf16[1,1,2,8,384]{4,3,2,1,0:T(8,128)(2,1)S(1)}, u32[]{:S(2)}, u32[]{:S(2)}) collective-permute-start(bf16[1,1,2,8,384]{4,3,2,1,0:T(8,128)(2,1)S(1)} %fusion.59), channel_id=1, source_target_pairs={{16,0},{17,1},{18,2},{19,3},{20,4},{21,5},{22,6},{23,7},{24,8},{25... | collective-permute-start | bytes 36872 | tf_op jit(solution)/shard_map/ppermute | solution.py:24
  49.9 12.9 %collective-permute-start.6 = (f32[1,1,2,3,128]{4,2,3,1,0:T(2,128)}, f32[1,1,2,3,128]{4,2,3,1,0:T(2,128)S(1)}, u32[]{:S(2)}, u32[]{:S(2)}) collective-permute-start(f32[1,1,2,3,128]{4,2,3,1,0:T(2,128)} %param.11), channel_id=1, source_target_pairs={{0,16},{1,17},{2,18},{3,19},{4,20},{5,21},{6,22},{7,23},{8,24},{9,... | collective-permute-start | bytes 9224 | tf_op jit(solution)/shard_map/ppermute | solution.py:23
  54.4 9.1 %collective-permute-start.7 = (f32[1,1,2,3,128]{4,2,3,1,0:T(2,128)}, f32[1,1,2,3,128]{4,2,3,1,0:T(2,128)S(1)}, u32[]{:S(2)}, u32[]{:S(2)}) collective-permute-start(f32[1,1,2,3,128]{4,2,3,1,0:T(2,128)} %param.11), channel_id=1, source_target_pairs={{16,0},{17,1},{18,2},{19,3},{20,4},{21,5},{22,6},{23,7},{24,8},{25... | collective-permute-start | bytes 9224 | tf_op jit(solution)/shard_map/ppermute | solution.py:24
  63.5 7.7 collective-permute-start.8
  64.8 6.5 collective-permute-start.9
  66.2 9.9 %collective-permute-start.2 = (bf16[3,1,2,8,384]{4,3,2,1,0:T(8,128)(2,1)S(1)}, bf16[3,1,2,8,384]{4,3,2,1,0:T(8,128)(2,1)S(1)}, u32[]{:S(2)}, u32[]{:S(2)}) collective-permute-start(bf16[3,1,2,8,384]{4,3,2,1,0:T(8,128)(2,1)S(1)} %pad_maximum_fusion.7), channel_id=1, source_target_pairs={{0,4},{4,8},{8,12},{1,5},{5,9},{9,13},{2,6},{6,10},{10,14},{3,7},{... | collective-permute-start | bytes 110600 | tf_op jit(solution)/shard_map/ppermute | solution.py:23
  70.0 6.1 collective-permute-start.3
  71.4 10.6 %collective-permute-start.10 = (f32[3,3,1,3,128]{4,2,3,1,0:T(1,128)S(1)}, f32[3,3,1,3,128]{4,2,3,1,0:T(1,128)S(1)}, u32[]{:S(2)}, u32[]{:S(2)}) collective-permute-start(f32[3,3,1,3,128]{4,2,3,1,0:T(1,128)S(1)} %get-tuple-element.600), channel_id=1, source_target_pairs={{0,1},{1,2},{2,3},{4,5},{5,6},{6,7},{8,9},{9,10},{10,11},{12,13},{... | collective-permute-start | bytes 41480 | tf_op jit(solution)/shard_map/ppermute | solution.py:23
  74.8 7.2 collective-permute-start.11
  76.1 6.3 collective-permute-start.4
  80.7 6.1 collective-permute-start.5
  87.6 153.6 %copy-start.6 = (f32[1,1,2,8,384]{4,3,2,1,0:T(8,128)S(1)}, f32[1,1,2,8,384]{4,3,2,1,0:T(8,128)}, u32[]{:S(2)}) copy-start(f32[1,1,2,8,384]{4,3,2,1,0:T(8,128)} %param.13) | copy-start | bytes 73732
  130.4 8.2 %collective-permute-start.12 = (f32[1,3,4,8,384]{4,3,2,1,0:T(8,128)S(1)}, f32[1,3,4,8,384]{4,3,2,1,0:T(8,128)S(1)}, u32[]{:S(2)}, u32[]{:S(2)}) collective-permute-start(f32[1,3,4,8,384]{4,3,2,1,0:T(8,128)S(1)} %bitcast.395), channel_id=1, source_target_pairs={{0,16},{1,17},{2,18},{3,19},{4,20},{5,21},{6,22},{7,23},{8,24},{9,... | collective-permute-start | bytes 442376 | tf_op jit(solution)/shard_map/ppermute | solution.py:23
  135.0 7.7 collective-permute-start.13
  142.8 2.6 collective-permute-start.14
  144.1 6.6 collective-permute-start.15
  150.7 46.3 %collective-permute-start.16 = (f32[1,1,1,8,384]{4,3,2,1,0:T(8,128)S(1)}, f32[1,1,1,8,384]{4,3,2,1,0:T(8,128)S(1)}, u32[]{:S(2)}, u32[]{:S(2)}) collective-permute-start(f32[1,1,1,8,384]{4,3,2,1,0:T(8,128)S(1)} %get-tuple-element.598), channel_id=1, source_target_pairs={{0,1},{1,2},{2,3},{4,5},{5,6},{6,7},{8,9},{9,10},{10,11},{12,13},{... | collective-permute-start | bytes 36872 | tf_op jit(solution)/shard_map/ppermute | solution.py:23
  195.6 45.7 %collective-permute-start.17 = (f32[1,1,1,8,384]{4,3,2,1,0:T(8,128)S(1)}, f32[1,1,1,8,384]{4,3,2,1,0:T(8,128)S(1)}, u32[]{:S(2)}, u32[]{:S(2)}) collective-permute-start(f32[1,1,1,8,384]{4,3,2,1,0:T(8,128)S(1)} %get-tuple-element.599), channel_id=1, source_target_pairs={{1,0},{2,1},{3,2},{5,4},{6,5},{7,6},{9,8},{10,9},{11,10},{13,12},{... | collective-permute-start | bytes 36872 | tf_op jit(solution)/shard_map/ppermute | solution.py:24
  322.6 173.8 %copy-start.7 = (f32[1,1,2,8,384]{4,3,2,1,0:T(8,128)}, f32[1,1,2,8,384]{4,3,2,1,0:T(8,128)S(1)}, u32[]{:S(2)}) copy-start(f32[1,1,2,8,384]{4,3,2,1,0:T(8,128)S(1)} %get-tuple-element.562) | copy-start | bytes 73732
  322.6 5.6 collective-permute-start.18
  326.8 5.6 collective-permute-start.19
  332.4 2.6 collective-permute-start.20
  333.7 3.5 collective-permute-start.21
  337.3 5.7 collective-permute-start.22
  341.2 6.0 collective-permute-start.23
  390.9 5.6 collective-permute-start.24
  392.6 8.6 %collective-permute-start.25 = (f32[1,3,4,8,384]{4,3,2,1,0:T(8,128)S(1)}, f32[1,3,4,8,384]{4,3,2,1,0:T(8,128)S(1)}, u32[]{:S(2)}, u32[]{:S(2)}) collective-permute-start(f32[1,3,4,8,384]{4,3,2,1,0:T(8,128)S(1)} %bitcast.393), channel_id=1, source_target_pairs={{16,0},{17,1},{18,2},{19,3},{20,4},{21,5},{22,6},{23,7},{24,8},{25... | collective-permute-start | bytes 442376 | tf_op jit(solution)/shard_map/ppermute | solution.py:24
  401.2 3.3 collective-permute-start.26
  403.2 3.6 collective-permute-start.27
  406.9 45.6 %collective-permute-start.28 = (f32[1,1,1,8,384]{4,3,2,1,0:T(8,128)S(1)}, f32[1,1,1,8,384]{4,3,2,1,0:T(8,128)S(1)}, u32[]{:S(2)}, u32[]{:S(2)}) collective-permute-start(f32[1,1,1,8,384]{4,3,2,1,0:T(8,128)S(1)} %get-tuple-element.596), channel_id=1, source_target_pairs={{0,1},{1,2},{2,3},{4,5},{5,6},{6,7},{8,9},{9,10},{10,11},{12,13},{... | collective-permute-start | bytes 36872 | tf_op jit(solution)/shard_map/ppermute | solution.py:23
  451.1 45.3 %collective-permute-start.29 = (f32[1,1,1,8,384]{4,3,2,1,0:T(8,128)S(1)}, f32[1,1,1,8,384]{4,3,2,1,0:T(8,128)S(1)}, u32[]{:S(2)}, u32[]{:S(2)}) collective-permute-start(f32[1,1,1,8,384]{4,3,2,1,0:T(8,128)S(1)} %get-tuple-element.597), channel_id=1, source_target_pairs={{1,0},{2,1},{3,2},{5,4},{6,5},{7,6},{9,8},{10,9},{11,10},{13,12},{... | collective-permute-start | bytes 36872 | tf_op jit(solution)/shard_map/ppermute | solution.py:24
  577.8 5.6 collective-permute-start.30
  582.0 5.6 collective-permute-start.31
  587.6 2.6 collective-permute-start.32
  588.9 3.5 collective-permute-start.33
  592.4 5.7 collective-permute-start.34
  596.4 6.0 collective-permute-start.35
  645.0 149.1 %copy-start.8 = (f32[1,1,2,8,384]{4,3,2,1,0:T(8,128)S(1)}, f32[1,1,2,8,384]{4,3,2,1,0:T(8,128)}, u32[]{:S(2)}) copy-start(f32[1,1,2,8,384]{4,3,2,1,0:T(8,128)} %copy-done.7) | copy-start | bytes 73732
  645.0 149.2 %copy-start.14 = (f32[8]{0:T(128)S(1)}, f32[8]{0:T(128)}, u32[]{:S(2)}) copy-start(f32[8]{0:T(128)} %copy-done.13) | copy-start | bytes 100
  645.0 149.2 %copy-start.16 = (f32[8]{0:T(128)S(1)}, f32[8]{0:T(128)}, u32[]{:S(2)}) copy-start(f32[8]{0:T(128)} %copy-done.15) | copy-start | bytes 100
  646.1 5.6 collective-permute-start.36
  647.8 8.6 %collective-permute-start.37 = (f32[1,3,4,8,384]{4,3,2,1,0:T(8,128)S(1)}, f32[1,3,4,8,384]{4,3,2,1,0:T(8,128)S(1)}, u32[]{:S(2)}, u32[]{:S(2)}) collective-permute-start(f32[1,3,4,8,384]{4,3,2,1,0:T(8,128)S(1)} %bitcast.394), channel_id=1, source_target_pairs={{16,0},{17,1},{18,2},{19,3},{20,4},{21,5},{22,6},{23,7},{24,8},{25... | collective-permute-start | bytes 442376 | tf_op jit(solution)/shard_map/ppermute | solution.py:24
  656.4 3.3 collective-permute-start.38
  658.4 3.6 collective-permute-start.39
  662.1 45.6 %collective-permute-start.40 = (f32[1,1,1,8,384]{4,3,2,1,0:T(8,128)S(1)}, f32[1,1,1,8,384]{4,3,2,1,0:T(8,128)S(1)}, u32[]{:S(2)}, u32[]{:S(2)}) collective-permute-start(f32[1,1,1,8,384]{4,3,2,1,0:T(8,128)S(1)} %get-tuple-element.594), channel_id=1, source_target_pairs={{0,1},{1,2},{2,3},{4,5},{5,6},{6,7},{8,9},{9,10},{10,11},{12,13},{... | collective-permute-start | bytes 36872 | tf_op jit(solution)/shard_map/ppermute | solution.py:23
  706.3 45.3 %collective-permute-start.41 = (f32[1,1,1,8,384]{4,3,2,1,0:T(8,128)S(1)}, f32[1,1,1,8,384]{4,3,2,1,0:T(8,128)S(1)}, u32[]{:S(2)}, u32[]{:S(2)}) collective-permute-start(f32[1,1,1,8,384]{4,3,2,1,0:T(8,128)S(1)} %get-tuple-element.595), channel_id=1, source_target_pairs={{1,0},{2,1},{3,2},{5,4},{6,5},{7,6},{9,8},{10,9},{11,10},{13,12},{... | collective-permute-start | bytes 36872 | tf_op jit(solution)/shard_map/ppermute | solution.py:24
  (18 other events, 300.8 us)
where the time goes:
time: 800 us; the launch traced here: 795 us
  blocking collectives  243 us (30%)
  starting transfers between devices  214 us (27%)
  waiting for transfers between devices  190 us (24%)
  local copies, waits for them, and re-layouts  88.9 us (11%)
  other arithmetic  52.1 us (7%)
    ppermute x21, starting transfers between devices, padded_2(): before = lax.ppermute(last, axis, up)  187 us
    ppermute x21, waiting for transfers between devices, padded_2(): after = lax.ppermute(leading, axis, down)  181 us
    psum x3, blocking collectives, body(): alpha_now = lax.psum(local_dot(current, image_vec), ('gx', 'gy', 'gz'))  121 us
    psum x2, blocking collectives, body(): lax.psum(local_dot(residual, residual), ('gx', 'gy', 'gz')) + epsilon  79.7 us
    psum x1, blocking collectives, body(): lax.psum(local_dot(start_vec, start_vec), ('gx', 'gy', 'gz')) + epsilon  42 us
    mul x9, local copies, waits for them, and re-layouts, mobility_tiles(): identity_three[None, :, None, :, None] * isotropic[:, None, :, None, :]  38.1 us
    ppermute x21, starting transfers between devices, padded_2(): after = lax.ppermute(leading, axis, down)  27.1 us
    mul x3, local copies, waits for them, and re-layouts, mobility_tiles(): dyadic[:, None, :, None, :] * product  25.6 us
  transfers between devices with their start and end apart: 42, of which 27 were waited for; matrix products, arithmetic and copies ran while one was open for 1% of the time, Pallas kernels for 0%

commit v1 on v0

v1 whole, which is shorter than its diff:
```python
import functools

import jax
import jax.numpy as jnp
from jax import lax
from jax.experimental import pallas as pl
from jax.experimental.pallas import tpu as pltpu
from jax.sharding import PartitionSpec as P

ITERS = 3
ROOT_ITERS = 12
GROUP = 4
CHUNK = 32

radius = 0.08
floor_sq = 0.0001
epsilon = 1e-06

AXES = ("gx", "gy", "gz")
VMEM = pl.BlockSpec(memory_space=pltpu.VMEM)
SMEM = pl.BlockSpec(memory_space=pltpu.SMEM)
f32 = jnp.float32
bf16 = jnp.bfloat16


def matching(count, parity):
    pairs = []
    for i in range(parity, count - 1, 2):
        pairs += [(i, i + 1), (i + 1, i)]
    return pairs


def swaps(axis, first, second):
    count = lax.axis_size(axis)
    got = [lax.ppermute(first, axis, matching(count, 0))]
    if count > 2:
        got.append(lax.ppermute(second, axis, matching(count, 1)))
    return got


def spread(field):
    blocks, rows, width = field.shape
    columns = jnp.stack([field] + swaps("gx", field, field))
    odd = lax.axis_index("gz") % 2 == 1
    low, high = columns[:, 0], columns[:, blocks - 1]
    got = swaps("gz", jnp.where(odd, low, high), jnp.where(odd, high, low))
    while len(got) < 2:
        got.append(jnp.zeros_like(got[0]))
    deep = jnp.concatenate([columns] + [g[:, None] for g in got], axis=1)
    deep = deep.reshape(-1, rows, width)
    return [deep] + swaps("gy", deep, deep)


def partner(axis, step):
    if lax.axis_size(axis) == 2:
        return jnp.where(step == 0, 0, 1)
    odd = lax.axis_index(axis) % 2
    return jnp.where(step == 0, 0, jnp.where((step < 0) == (odd == 1), 1, 2))


def pair_table(pair_list, pair_count, blocks, columns, zero_slot):
    home, code = pair_list[0, 0, 0, 0], pair_list[0, 0, 0, 1]
    capacity = home.shape[0]
    step_x, step_y, step_z = code // 9 - 1, code // 3 % 3 - 1, code % 3 - 1
    z = home + step_z
    odd = lax.axis_index("gz") % 2
    below = jnp.where(odd == 1, blocks, blocks + 1)
    above = jnp.where(odd == 1, blocks + 1, blocks)
    if lax.axis_size("gz") == 2:
        below = above = blocks
    z = jnp.where(z < 0, below, jnp.where(z >= blocks, above, z))
    slot = (partner("gy", step_y) * columns + partner("gx", step_x)) * (blocks + 2) + z
    live = lax.iota(jnp.int32, capacity) < pair_count[0, 0, 0]
    pad = -capacity % GROUP
    home = jnp.pad(jnp.where(live, home, 0), (0, pad))
    slot = jnp.pad(jnp.where(live, slot, zero_slot), (0, pad), constant_values=zero_slot)
    return jnp.stack([home, slot])


def lane_mask(fill_ref, block, width, beads):
    lanes = lax.broadcasted_iota(jnp.int32, (1, width), 1)
    return (lax.rem(lanes, beads) < fill_ref[block]).astype(f32)


def pack_kernel(fill_ref, noise_ref, pos_ref, start_ref, pack_ref):
    blocks, samples, width = noise_ref.shape
    beads = pos_ref.shape[2]
    for block in range(blocks):
        start = noise_ref[block] * lane_mask(fill_ref, block, width, beads)
        start_ref[block] = start
        pos = jnp.concatenate([pos_ref[block, c : c + 1, :] for c in range(3)], axis=1)
        high = pos.astype(bf16).astype(f32)
        rest = pos - high
        mid = rest.astype(bf16).astype(f32)
        low = rest - mid
        row = lax.broadcasted_iota(jnp.int32, (8, width), 0)
        place = jnp.where(row == 0, high, jnp.where(row == 1, mid, jnp.where(row == 2, low, 0.0)))
        pack_ref[block] = jnp.concatenate([start, place], axis=0).astype(bf16)


def gather_slots(parts, slots_ref):
    count = parts[0].shape[0]
    for i, part in enumerate(parts):
        slots_ref[pl.ds(i * count, count)] = part[...]
    slots_ref[len(parts) * count] = jnp.zeros(slots_ref.shape[1:], bf16)


def position_of(slots_ref, slot, samples, beads):
    rows = slots_ref[slot].astype(f32)[samples : samples + 8]
    pos = rows[0:1] + rows[1:2] + rows[2:3]
    return [pos[:, c * beads : (c + 1) * beads] for c in range(3)]


def make_tile(table_ref, slots_ref, tiles_ref, home_slot, pair, samples, beads):
    home = position_of(slots_ref, home_slot + table_ref[0, pair], samples, beads)
    away = position_of(slots_ref, table_ref[1, pair], samples, beads)
    row = lax.broadcasted_iota(jnp.int32, (8, beads), 0)
    stacked = jnp.where(row == 0, away[0], jnp.where(row == 1, away[1], away[2]))
    turned = jnp.transpose(stacked)
    for first in range(0, beads, CHUNK):
        d = [turned[first : first + CHUNK, c : c + 1] - home[c] for c in range(3)]
        dist_sq = d[0] * d[0] + d[1] * d[1] + d[2] * d[2]
        root = lax.rsqrt(jnp.maximum(dist_sq, 1e-30))
        distance = dist_sq * root
        inv_root = jnp.minimum(root, floor_sq**-0.5)
        inverse_sq = inv_root * inv_root
        far = (0.75 * radius) * inv_root
        far_two = (2.0 * radius * radius) * (far * inverse_sq)
        apart = dist_sq >= 4.0 * radius * radius
        isotropic = jnp.where(apart, far + far_two * (1.0 / 3.0), 1.0 - (9.0 / 32.0 / radius) * distance)
        dyadic = jnp.where(apart, far - far_two, (3.0 / 32.0 / radius) * distance) * inverse_sq
        scaled = [dyadic * d[c] for c in range(3)]
        for c in range(3):
            for e in range(c, 3):
                entry = scaled[c] * d[e]
                if c == e:
                    entry = entry + isotropic
                entry = entry.astype(bf16)
                tiles_ref[pair, pl.ds(e * beads + first, CHUNK), pl.ds(c * beads, beads)] = entry
                if c != e:
                    tiles_ref[pair, pl.ds(c * beads + first, CHUNK), pl.ds(e * beads, beads)] = entry


def multiply(total, table_ref, slots_ref, tiles_ref, sum_ref, samples):
    sum_ref[...] = jnp.zeros_like(sum_ref)

    def group(turn, carry):
        products = []
        for i in range(GROUP):
            pair = turn * GROUP + i
            field = slots_ref[table_ref[1, pair]][:samples]
            tile = tiles_ref[jnp.minimum(pair, total - 1)]
            products.append(jnp.dot(field, tile, preferred_element_type=f32))
        for i in range(GROUP):
            home = table_ref[0, turn * GROUP + i]
            sum_ref[home] = sum_ref[home] + products[i]
        return carry

    lax.fori_loop(0, (total + GROUP - 1) // GROUP, group, 0)


def first_kernel(parts, home_slot, beads, count_ref, fill_ref, table_ref, start_ref, *refs):
    given, (tiles_ref, next_ref, send_ref, slots_ref, sum_ref) = refs[:parts], refs[parts:]
    blocks, samples, width = start_ref.shape
    total = count_ref[0]
    gather_slots(given, slots_ref)

    def make(pair, carry):
        make_tile(table_ref, slots_ref, tiles_ref, home_slot, pair, samples, beads)
        return carry

    lax.fori_loop(0, total, make, 0)
    multiply(total, table_ref, slots_ref, tiles_ref, sum_ref, samples)
    for block in range(blocks):
        new = sum_ref[block] * lane_mask(fill_ref, block, width, beads) - start_ref[block]
        next_ref[block] = new
        send_ref[block] = new.astype(bf16)


def next_kernel(parts, beads, count_ref, fill_ref, table_ref, tiles_ref, old_ref, *refs):
    given, (next_ref, send_ref, slots_ref, sum_ref) = refs[:parts], refs[parts:]
    blocks, samples, width = old_ref.shape
    gather_slots(given, slots_ref)
    multiply(count_ref[0], table_ref, slots_ref, tiles_ref, sum_ref, samples)
    for block in range(blocks):
        new = sum_ref[block] * lane_mask(fill_ref, block, width, beads) - old_ref[block]
        next_ref[block] = new
        send_ref[block] = new.astype(bf16)


MOMENTS = ((0, 0), (0, 1), (1, 1), (1, 2), (2, 2), (2, 3))


def last_kernel(parts, beads, count_ref, fill_ref, table_ref, tiles_ref, x0_ref, x1_ref, x2_ref, *refs):
    given, (moment_ref, slots_ref, sum_ref) = refs[:parts], refs[parts:]
    blocks, samples, width = x0_ref.shape
    gather_slots(given, slots_ref)
    multiply(count_ref[0], table_ref, slots_ref, tiles_ref, sum_ref, samples)
    lanes = moment_ref.shape[2]
    lane = lax.broadcasted_iota(jnp.int32, (samples, lanes), 1)
    row = lax.broadcasted_iota(jnp.int32, (samples, lanes), 0)
    sums = [0.0] * len(MOMENTS)
    for block in range(blocks):
        x = [x0_ref[block], x1_ref[block], x2_ref[block]]
        x.append(sum_ref[block] * lane_mask(fill_ref, block, width, beads) - x[2])
        for k, (i, j) in enumerate(MOMENTS):
            sums[k] = sums[k] + x[i] * x[j]
    grid = jnp.zeros((samples, lanes), f32)
    for k, value in enumerate(sums):
        value = jnp.sum(value, axis=1, keepdims=True)
        grid = jnp.where(lane == row + k * samples, value, grid)
    line = jnp.sum(grid, axis=0, keepdims=True)
    moment_ref[...] = jnp.broadcast_to(line[None], moment_ref.shape)


def inverse_symmetric(m):
    a, b, c, d, e, f = m
    ca, cb, cc = d * f - e * e, c * e - b * f, b * e - c * d
    scale = 1.0 / (a * ca + b * cb + c * cc)
    return (ca * scale, cb * scale, cc * scale, (a * f - c * c) * scale, (b * c - a * e) * scale, (a * d - b * b) * scale)


def final_kernel(moment_ref, x0_ref, x1_ref, x2_ref, out_ref):
    blocks, samples, width = x0_ref.shape
    lanes = moment_ref.shape[2]
    lane = lax.broadcasted_iota(jnp.int32, (samples, lanes), 1)
    row = lax.broadcasted_iota(jnp.int32, (samples, lanes), 0)
    line = jnp.broadcast_to(jnp.sum(moment_ref[...], axis=0), (samples, lanes))
    m00, m01, m11, m12, m22, m23 = [
        jnp.broadcast_to(
            jnp.sum(jnp.where(lane == row + k * samples, line, 0.0), axis=1, keepdims=True), (samples, lanes)
        )
        for k in range(len(MOMENTS))
    ]
    norm_sq = m00 + epsilon
    start_norm = jnp.sqrt(norm_sq)
    inv_sq = 1.0 / norm_sq
    alpha1 = (m00 + m01) * inv_sq
    c = 1.0 - alpha1
    res_sq = (m11 + c * (2.0 * m01 + c * m00)) * inv_sq
    beta1 = jnp.sqrt(jnp.maximum(res_sq, 0.0) + epsilon)
    k2 = 1.0 / (start_norm * beta1)
    n11 = m11 + c * (2.0 * m01 + c * m00)
    n12 = m12 + c * (2.0 * m11 + c * m01)
    alpha2 = k2 * k2 * (n11 + n12)
    f1 = 1.0 + c - alpha2
    f0 = c - alpha2 * c - beta1 * beta1
    n22 = m22 + f1 * (2.0 * m12 + f1 * m11) + f0 * (2.0 * (m11 + f1 * m01) + f0 * m00)
    beta2 = jnp.sqrt(jnp.maximum(k2 * k2 * n22, 0.0) + epsilon)
    k3 = k2 / beta2
    n23 = m23 + f1 * (2.0 * m22 + f1 * m12) + f0 * (2.0 * (m12 + f1 * m11) + f0 * m01)
    alpha3 = k3 * k3 * (jnp.maximum(n22, 0.0) + n23)

    scale = (alpha1 + alpha2 + alpha3) / 3.0
    inv_scale = 1.0 / scale
    zero, one = jnp.zeros_like(scale), jnp.ones_like(scale)
    y = (alpha1 * inv_scale, beta1 * inv_scale, zero, alpha2 * inv_scale, beta2 * inv_scale, alpha3 * inv_scale)
    z = (one, zero, zero, one, zero, one)
    for _ in range(ROOT_ITERS):
        inv_z, inv_y = inverse_symmetric(z), inverse_symmetric(y)
        y = tuple(0.5 * (p + q) for p, q in zip(y, inv_z))
        z = tuple(0.5 * (p + q) for p, q in zip(z, inv_y))
    root_scale = jnp.sqrt(scale)
    r1, r2, r3 = root_scale * y[0], root_scale * y[1], root_scale * y[2]
    w2, w3 = start_norm * r2 * k2, start_norm * r3 * k3
    p0 = r1 + w2 * c + w3 * f0
    p1 = w2 + w3 * f1
    for block in range(blocks):
        for first in range(0, width, lanes):
            at = pl.ds(first, lanes)
            out_ref[block, :, at] = p0 * x0_ref[block, :, at] + p1 * x1_ref[block, :, at] + w3 * x2_ref[block, :, at]


def call(kernel, outs, in_specs, scratch=(), limit=None, cost=None):
    return pl.pallas_call(
        kernel,
        out_shape=outs,
        in_specs=in_specs,
        out_specs=jax.tree.map(lambda _: VMEM, outs),
        scratch_shapes=list(scratch),
        compiler_params=pltpu.CompilerParams(vmem_limit_bytes=limit),
        cost_estimate=cost,
    )


def body(positions, block_fill, noise, pair_list, pair_count):
    blocks, beads = positions.shape[2], positions.shape[4]
    samples, width = noise.shape[3], noise.shape[4]
    shape = (blocks, samples, width)
    devices = lax.axis_size(AXES)
    columns = 2 if lax.axis_size("gx") == 2 else 3
    rows_y = 2 if lax.axis_size("gy") == 2 else 3
    per_part = columns * (blocks + 2)
    zero_slot = rows_y * per_part
    capacity = pair_list.shape[4]
    fill = block_fill.reshape(blocks)
    count = pair_count.reshape(1)
    limit = 24 << 20

    x0, packed = call(
        pack_kernel,
        (jax.ShapeDtypeStruct(shape, f32), jax.ShapeDtypeStruct((blocks, samples + 8, width), bf16)),
        [SMEM, VMEM, VMEM],
    )(fill, noise.reshape(shape), positions.reshape(blocks, 3, beads))
    table = pair_table(pair_list, pair_count, blocks, columns, zero_slot)
    out_field = (jax.ShapeDtypeStruct(shape, f32), jax.ShapeDtypeStruct(shape, bf16))

    def scratch(rows):
        return (pltpu.VMEM((zero_slot + 1, rows, width), bf16), pltpu.VMEM(shape, f32))

    parts = spread(packed)
    tiles, x1, send = call(
        functools.partial(first_kernel, rows_y, 0, beads),
        (jax.ShapeDtypeStruct((capacity, width, width), bf16),) + out_field,
        [SMEM] * 3 + [VMEM] * (1 + rows_y),
        scratch(samples + 8),
        limit,
    )(count, fill, table, x0, *parts)
    parts = spread(send)
    x2, send = call(
        functools.partial(next_kernel, rows_y, beads),
        out_field,
        [SMEM] * 3 + [VMEM] * (2 + rows_y),
        scratch(samples),
        limit,
    )(count, fill, table, tiles, x1, *parts)
    parts = spread(send)
    moments = call(
        functools.partial(last_kernel, rows_y, beads),
        jax.ShapeDtypeStruct((devices, 1, 128), f32),
        [SMEM] * 3 + [VMEM] * (4 + rows_y),
        scratch(samples),
        limit,
    )(count, fill, table, tiles, x0, x1, x2, *parts)
    moments = lax.all_to_all(moments, AXES, 0, 0)
    out = call(final_kernel, jax.ShapeDtypeStruct(shape, f32), [VMEM] * 4)(moments, x0, x1, x2)
    return out.reshape(noise.shape)


def solution(mesh):
    block = P("gx", "gy", "gz", None, None)
    cell = P("gx", "gy", "gz")
    return jax.shard_map(
        body, mesh=mesh, in_specs=(block, cell, block, block, cell), out_specs=block, check_vma=False
    )
```

time: 800 us -> 88.1 us (0.11)
  blocking collectives: 243 us -> 19.1 us
  waiting for transfers between devices: 190 us -> 10.1 us
  starting transfers between devices: 214 us -> 43.8 us
  local copies, waits for them, and re-layouts: 88.9 us -> 2.69 us
  other arithmetic: 52.1 us -> 2.31 us
  Pallas kernels: 0 us -> 8.65 us
    psum x6 -> x0, blocking collectives: 243 us -> none  [the longest x3 121 us: body(): alpha_now = lax.psum(local_dot(current, image_vec), ('gx', 'gy', 'gz'))]
    ppermute x42 -> x15, waiting for transfers between devices: 190 us -> 10.1 us  [the longest x9 10.1 us: swaps(): got = [lax.ppermute(first, axis, matching(count, 0))]]
    ppermute x42 -> x15, starting transfers between devices: 214 us -> 43.8 us  [the longest x9 39.9 us: swaps(): got = [lax.ppermute(first, axis, matching(count, 0))]]
    mul x12 -> x0, local copies, waits for them, and re-layouts: 63.7 us -> none  [the longest x9 38.1 us: mobility_tiles(): identity_three[None, :, None, :, None] * isotropic[:, None, :, None, :]]
    all_to_all x0 -> x1, blocking collectives: none -> 19.1 us  [body(): moments = lax.all_to_all(moments, AXES, 0, 0)]
    mul x8 -> x0, other arithmetic: 15.9 us -> none  [the longest x3 13.7 us: mobility_tiles(): dyadic[:, None, :, None, :] * product]
    convert_element_type x10 -> x0, other arithmetic: 15 us -> none  [the longest x3 13.3 us: mobility_tiles(): mobility.reshape(group_size, 3 * bead_count, 3 * bead_count)]
    gather x23 -> x0, local copies, waits for them, and re-layouts: 14.2 us -> none  [the longest x6 3.45 us: accumulate(): mobility = mobility_tiles(padded_pos[home_pick], padded_pos[away_pick])]
  transfers between devices with their start and end apart: 42 -> 15, of which waited for: 27 -> 9; matrix products, arithmetic and copies ran while one was open for 1% -> 1% of each run, Pallas kernels for 0% -> 0%
where the time goes in v1:
time: 88.1 us; the launch traced here: 87.5 us
  starting transfers between devices  43.8 us (50%)
  blocking collectives  19.1 us (22%)
  waiting for transfers between devices  10.1 us (11%)
  Pallas kernels  8.65 us (10%)
  local copies, waits for them, and re-layouts  2.69 us (3%)
  other arithmetic  2.31 us (3%)
    ppermute x9, starting transfers between devices, swaps(): got = [lax.ppermute(first, axis, matching(count, 0))]  39.9 us
    all_to_all x1, blocking collectives, body(): moments = lax.all_to_all(moments, AXES, 0, 0)  19.1 us
    ppermute x9, waiting for transfers between devices, swaps(): got = [lax.ppermute(first, axis, matching(count, 0))]  10.1 us
    ppermute x6, starting transfers between devices, swaps(): got.append(lax.ppermute(second, axis, matching(count, 1)))  3.94 us
    pallas_call x1, Pallas kernels, body(): call(functools.partial(first_kernel, rows_y, 0, beads), (jax.ShapeDtypeSt...  3.09 us
    unnamed x11, local copies, waits for them, and re-layouts  2.68 us
    pallas_call x1, Pallas kernels, body(): call(final_kernel, jax.ShapeDtypeStruct(shape, f32), [VMEM] * 4)  1.77 us
  transfers between devices with their start and end apart: 15, of which 9 were waited for; matrix products, arithmetic and copies ran while one was open for 1% of the time, Pallas kernels for 0%

profile of v1, /device:TPU:0, one launch (start us, length us, event | category | flops | bytes accessed | tf_op | source)
XLA Modules:
  0.0 87.5 jit_solution(1599971974093962155)
XLA Ops:
  0.0 1.3 %copy.19 = f32[1,1,2,3,128]{4,3,2,1,0:T(4,128)} copy(f32[1,1,2,3,128]{4,2,3,1,0:T(2,128)} %param.5) | data formatting | bytes 6144 | tf_op args[0]
  1.3 1.4 %shard_map.55 = (f32[2,8,384]{2,1,0:T(8,128)}, bf16[2,16,384]{2,1,0:T(8,128)(2,1)}) custom-call(s32[2]{0:T(128)} %bitcast.127, f32[2,8,384]{2,1,0:T(8,128)} %bitcast.141, f32[2,3,128]{2,1,0:T(4,128)} %bitcast.142), custom_call_target="tpu_custom_call" | custom-call | tf_op jit(solution)/shard_map/pallas_call | solution.py:300
  2.7 0.0 copy-start.1
  2.7 3.0 %collective-permute-start = (bf16[2,16,384]{2,1,0:T(8,128)(2,1)}, bf16[2,16,384]{2,1,0:T(8,128)(2,1)S(1)}, u32[]{:S(2)}, u32[]{:S(2)}) collective-permute-start(bf16[2,16,384]{2,1,0:T(8,128)(2,1)} %get-tuple-element.13), channel_id=1, source_target_pairs={{0,16},{16,0},{1,17},{17,1},{2,18},{18,2},{3,19},{19,3},{4,20},{20... | collective-permute-start | bytes 73736 | tf_op jit(solution)/shard_map/ppermute | solution.py:35
  6.3 0.7 compare_select_fusion.6
  7.0 0.7 collective-permute-done
  7.6 0.8 select_bitcast_fusion.1
  8.4 2.2 %collective-permute-start.1 = (bf16[2,16,384]{2,1,0:T(8,128)(2,1)S(1)}, bf16[2,16,384]{2,1,0:T(8,128)(2,1)S(1)}, u32[]{:S(2)}, u32[]{:S(2)}) collective-permute-start(bf16[2,16,384]{2,1,0:T(8,128)(2,1)S(1)} %get-tuple-element.19), channel_id=1, source_target_pairs={{0,1},{1,0},{2,3},{3,2},{4,5},{5,4},{6,7},{7,6},{8,9},{9,8},{10,11... | collective-permute-start | bytes 73736 | tf_op jit(solution)/shard_map/ppermute | solution.py:35
  10.6 0.7 collective-permute-start.2
  11.3 1.1 %collective-permute-done.1 = bf16[2,16,384]{2,1,0:T(8,128)(2,1)S(1)} collective-permute-done((bf16[2,16,384]{2,1,0:T(8,128)(2,1)S(1)}, bf16[2,16,384]{2,1,0:T(8,128)(2,1)S(1)}, u32[]{:S(2)}, u32[]{:S(2)}) %collective-permute-start.1) | collective-permute-done | bytes 24608 | tf_op jit(solution)/shard_map/ppermute | solution.py:35
  12.4 0.0 collective-permute-done.2
  12.4 0.8 pad_maximum_fusion
  13.2 0.7 collective-permute-start.4
  13.9 3.4 %collective-permute-start.3 = (bf16[8,16,384]{2,1,0:T(8,128)(2,1)S(1)}, bf16[8,16,384]{2,1,0:T(8,128)(2,1)S(1)}, u32[]{:S(2)}, u32[]{:S(2)}) collective-permute-start(bf16[8,16,384]{2,1,0:T(8,128)(2,1)S(1)} %bitcast.115), channel_id=1, source_target_pairs={{0,4},{4,0},{8,12},{12,8},{1,5},{5,1},{9,13},{13,9},{2,6},{6,2},{1... | collective-permute-start | bytes 294920 | tf_op jit(solution)/shard_map/ppermute | solution.py:35
  17.3 0.0 collective-permute-done.4.refs_2_
  17.3 0.9 %collective-permute-done.3.refs_1_ = bf16[8,16,384]{2,1,0:T(8,128)(2,1)S(1)} collective-permute-done((bf16[8,16,384]{2,1,0:T(8,128)(2,1)S(1)}, bf16[8,16,384]{2,1,0:T(8,128)(2,1)S(1)}, u32[]{:S(2)}, u32[]{:S(2)}) %collective-permute-start.3) | collective-permute-done | bytes 98336 | tf_op jit(solution)/shard_map/ppermute | solution.py:35
  18.2 0.7 copy-done
  18.9 0.7 copy-done.4
  19.6 3.1 %shard_map.56 = (bf16[54,384,384]{2,1,0:T(8,128)(2,1)S(1)}, f32[2,8,384]{2,1,0:T(8,128)S(1)}, bf16[2,8,384]{2,1,0:T(8,128)(2,1)S(1)}) custom-call(s32[1]{0:T(128)} %bitcast.110.count_ref, s32[2]{0:T(128)S(1)} %bitcast.128, s32[2,56]{1,0:T(2,128)S(1)} %pad_add_fusion.table_ref, f32[2,8,384]{2,1,0:T(8,128)S(1)} %copy-done, bf16[8,16,384]{2,1,0:T(8,128)(2,1)S(1)} %bitcast.116, ...), custom_call_target="tpu_custom_call" | custom-call | tf_op jit(solution)/shard_map/pallas_call | solution.py:312
  22.7 0.0 copy-start.2
  22.7 5.7 %collective-permute-start.5 = (bf16[2,8,384]{2,1,0:T(8,128)(2,1)S(1)}, bf16[2,8,384]{2,1,0:T(8,128)(2,1)S(1)}, u32[]{:S(2)}, u32[]{:S(2)}) collective-permute-start(bf16[2,8,384]{2,1,0:T(8,128)(2,1)S(1)} %get-tuple-element.16), channel_id=1, source_target_pairs={{0,16},{16,0},{1,17},{17,1},{2,18},{18,2},{3,19},{19,3},{4,20},{20... | collective-permute-start | bytes 36872 | tf_op jit(solution)/shard_map/ppermute | solution.py:35
  28.4 1.7 %collective-permute-done.5 = bf16[2,8,384]{2,1,0:T(8,128)(2,1)S(1)} collective-permute-done((bf16[2,8,384]{2,1,0:T(8,128)(2,1)S(1)}, bf16[2,8,384]{2,1,0:T(8,128)(2,1)S(1)}, u32[]{:S(2)}, u32[]{:S(2)}) %collective-permute-start.5) | collective-permute-done | bytes 12320 | tf_op jit(solution)/shard_map/ppermute | solution.py:35
  30.1 4.9 %collective-permute-start.6 = (bf16[2,8,384]{2,1,0:T(8,128)(2,1)S(1)}, bf16[2,8,384]{2,1,0:T(8,128)(2,1)S(1)}, u32[]{:S(2)}, u32[]{:S(2)}) collective-permute-start(bf16[2,8,384]{2,1,0:T(8,128)(2,1)S(1)} %get-tuple-element.23), channel_id=1, source_target_pairs={{0,1},{1,0},{2,3},{3,2},{4,5},{5,4},{6,7},{7,6},{8,9},{9,8},{10,11... | collective-permute-start | bytes 36872 | tf_op jit(solution)/shard_map/ppermute | solution.py:35
  35.0 0.7 collective-permute-start.7
  35.7 1.0 %collective-permute-done.6 = bf16[2,8,384]{2,1,0:T(8,128)(2,1)S(1)} collective-permute-done((bf16[2,8,384]{2,1,0:T(8,128)(2,1)S(1)}, bf16[2,8,384]{2,1,0:T(8,128)(2,1)S(1)}, u32[]{:S(2)}, u32[]{:S(2)}) %collective-permute-start.6) | collective-permute-done | bytes 12320 | tf_op jit(solution)/shard_map/ppermute | solution.py:35
  36.7 0.0 collective-permute-done.7
  36.7 0.7 collective-permute-start.9
  37.4 2.7 %collective-permute-start.8 = (bf16[8,8,384]{2,1,0:T(8,128)(2,1)S(1)}, bf16[8,8,384]{2,1,0:T(8,128)(2,1)S(1)}, u32[]{:S(2)}, u32[]{:S(2)}) collective-permute-start(bf16[8,8,384]{2,1,0:T(8,128)(2,1)S(1)} %bitcast.121), channel_id=1, source_target_pairs={{0,4},{4,0},{8,12},{12,8},{1,5},{5,1},{9,13},{13,9},{2,6},{6,2},{1... | collective-permute-start | bytes 147464 | tf_op jit(solution)/shard_map/ppermute | solution.py:35
  40.1 0.0 collective-permute-done.9.refs_2_
  40.1 0.9 %collective-permute-done.8.refs_1_ = bf16[8,8,384]{2,1,0:T(8,128)(2,1)S(1)} collective-permute-done((bf16[8,8,384]{2,1,0:T(8,128)(2,1)S(1)}, bf16[8,8,384]{2,1,0:T(8,128)(2,1)S(1)}, u32[]{:S(2)}, u32[]{:S(2)}) %collective-permute-start.8) | collective-permute-done | bytes 49184 | tf_op jit(solution)/shard_map/ppermute | solution.py:35
  40.9 1.2 %shard_map.57 = (f32[2,8,384]{2,1,0:T(8,128)S(1)}, bf16[2,8,384]{2,1,0:T(8,128)(2,1)S(1)}) custom-call(s32[1]{0:T(128)} %bitcast.111.count_ref, s32[2]{0:T(128)S(1)} %bitcast.129, s32[2,56]{1,0:T(2,128)S(1)} %pad_add_fusion.table_ref, bf16[54,384,384]{2,1,0:T(8,128)(2,1)S(1)} %get-tuple-element.14.tiles_ref, ...), custom_call_target="tpu_custom_call" | custom-call | tf_op jit(solution)/shard_map/pallas_call | solution.py:320
  42.1 0.0 copy-start.3
  42.1 1.9 %collective-permute-start.10 = (bf16[2,8,384]{2,1,0:T(8,128)(2,1)S(1)}, bf16[2,8,384]{2,1,0:T(8,128)(2,1)S(1)}, u32[]{:S(2)}, u32[]{:S(2)}) collective-permute-start(bf16[2,8,384]{2,1,0:T(8,128)(2,1)S(1)} %get-tuple-element.18), channel_id=1, source_target_pairs={{0,16},{16,0},{1,17},{17,1},{2,18},{18,2},{3,19},{19,3},{4,20},{20... | collective-permute-start | bytes 36872 | tf_op jit(solution)/shard_map/ppermute | solution.py:35
  44.0 1.9 %collective-permute-done.10 = bf16[2,8,384]{2,1,0:T(8,128)(2,1)S(1)} collective-permute-done((bf16[2,8,384]{2,1,0:T(8,128)(2,1)S(1)}, bf16[2,8,384]{2,1,0:T(8,128)(2,1)S(1)}, u32[]{:S(2)}, u32[]{:S(2)}) %collective-permute-start.10) | collective-permute-done | bytes 12320 | tf_op jit(solution)/shard_map/ppermute | solution.py:35
  45.9 12.6 %collective-permute-start.11 = (bf16[2,8,384]{2,1,0:T(8,128)(2,1)S(1)}, bf16[2,8,384]{2,1,0:T(8,128)(2,1)S(1)}, u32[]{:S(2)}, u32[]{:S(2)}) collective-permute-start(bf16[2,8,384]{2,1,0:T(8,128)(2,1)S(1)} %get-tuple-element.21), channel_id=1, source_target_pairs={{0,1},{1,0},{2,3},{3,2},{4,5},{5,4},{6,7},{7,6},{8,9},{9,8},{10,11... | collective-permute-start | bytes 36872 | tf_op jit(solution)/shard_map/ppermute | solution.py:35
  58.5 0.7 collective-permute-start.12
  59.2 1.0 %collective-permute-done.11 = bf16[2,8,384]{2,1,0:T(8,128)(2,1)S(1)} collective-permute-done((bf16[2,8,384]{2,1,0:T(8,128)(2,1)S(1)}, bf16[2,8,384]{2,1,0:T(8,128)(2,1)S(1)}, u32[]{:S(2)}, u32[]{:S(2)}) %collective-permute-start.11) | collective-permute-done | bytes 12320 | tf_op jit(solution)/shard_map/ppermute | solution.py:35
  60.2 0.0 collective-permute-done.12
  60.2 0.7 collective-permute-start.14
  60.9 3.5 %collective-permute-start.13 = (bf16[8,8,384]{2,1,0:T(8,128)(2,1)S(1)}, bf16[8,8,384]{2,1,0:T(8,128)(2,1)S(1)}, u32[]{:S(2)}, u32[]{:S(2)}) collective-permute-start(bf16[8,8,384]{2,1,0:T(8,128)(2,1)S(1)} %bitcast.118), channel_id=1, source_target_pairs={{0,4},{4,0},{8,12},{12,8},{1,5},{5,1},{9,13},{13,9},{2,6},{6,2},{1... | collective-permute-start | bytes 147464 | tf_op jit(solution)/shard_map/ppermute | solution.py:35
  64.4 0.0 collective-permute-done.14.refs_2_
  64.4 0.9 %collective-permute-done.13.refs_1_ = bf16[8,8,384]{2,1,0:T(8,128)(2,1)S(1)} collective-permute-done((bf16[8,8,384]{2,1,0:T(8,128)(2,1)S(1)}, bf16[8,8,384]{2,1,0:T(8,128)(2,1)S(1)}, u32[]{:S(2)}, u32[]{:S(2)}) %collective-permute-start.13) | collective-permute-done | bytes 49184 | tf_op jit(solution)/shard_map/ppermute | solution.py:35
  65.3 0.0 copy-done.1
  65.3 1.3 %shard_map.58 = f32[32,1,128]{2,1,0:T(1,128)S(1)} custom-call(s32[1]{0:T(128)} %bitcast.112.count_ref, s32[2]{0:T(128)S(1)} %bitcast.130, s32[2,56]{1,0:T(2,128)S(1)} %pad_add_fusion.table_ref, bf16[54,384,384]{2,1,0:T(8,128)(2,1)S(1)} %get-tuple-element.14.tiles_ref, f32[2,8,384]{2,1,0:T(8,128)S(1)} %copy-done.1, ...), custom_call_target="tpu_custom_call" | custom-call | tf_op jit(solution)/shard_map/pallas_call | solution.py:328
  66.6 0.0 copy-done.2
  66.6 19.1 %all_to_all.5.moment_ref = f32[32,1,128]{2,1,0:T(1,128)} all-to-all(f32[32,1,128]{2,1,0:T(1,128)S(1)} %shard_map.58), channel_id=1, replica_groups=mesh['gx'=2,'gy'=4,'gz'=4] {'gx','gy','gz'}, dimensions={0} | all-to-all | bytes 32768 | tf_op jit(solution)/shard_map/all_to_all | solution.py:335
  85.7 0.0 copy-done.3
  85.7 1.8 %shard_map.59 = f32[2,8,384]{2,1,0:T(8,128)} custom-call(f32[32,1,128]{2,1,0:T(1,128)} %all_to_all.5.moment_ref, f32[2,8,384]{2,1,0:T(8,128)} %get-tuple-element.12.start_ref.x0_ref, f32[2,8,384]{2,1,0:T(8,128)} %copy-done.2, f32[2,8,384]{2,1,0:T(8,128)} %copy-done.3), custom_call_target="tpu_custom_call" | custom-call | tf_op jit(solution)/shard_map/pallas_call | solution.py:336
  (9 shorter events, 0.1 us)
Async XLA Ops:
  2.7 62.7 %copy-start.1 = (f32[2,8,384]{2,1,0:T(8,128)S(1)}, f32[2,8,384]{2,1,0:T(8,128)}, u32[]{:S(2)}) copy-start(f32[2,8,384]{2,1,0:T(8,128)} %get-tuple-element.12.start_ref.x0_ref) | copy-start | bytes 73732
  2.7 5.0 %collective-permute-start = (bf16[2,16,384]{2,1,0:T(8,128)(2,1)}, bf16[2,16,384]{2,1,0:T(8,128)(2,1)S(1)}, u32[]{:S(2)}, u32[]{:S(2)}) collective-permute-start(bf16[2,16,384]{2,1,0:T(8,128)(2,1)} %get-tuple-element.13), channel_id=1, source_target_pairs={{0,16},{16,0},{1,17},{17,1},{2,18},{18,2},{3,19},{19,3},{4,20},{20... | collective-permute-start | bytes 73736 | tf_op jit(solution)/shard_map/ppermute | solution.py:35
  8.4 4.0 %collective-permute-start.1 = (bf16[2,16,384]{2,1,0:T(8,128)(2,1)S(1)}, bf16[2,16,384]{2,1,0:T(8,128)(2,1)S(1)}, u32[]{:S(2)}, u32[]{:S(2)}) collective-permute-start(bf16[2,16,384]{2,1,0:T(8,128)(2,1)S(1)} %get-tuple-element.19), channel_id=1, source_target_pairs={{0,1},{1,0},{2,3},{3,2},{4,5},{5,4},{6,7},{7,6},{8,9},{9,8},{10,11... | collective-permute-start | bytes 73736 | tf_op jit(solution)/shard_map/ppermute | solution.py:35
  10.6 1.8 %collective-permute-start.2 = (bf16[2,16,384]{2,1,0:T(8,128)(2,1)S(1)}, bf16[2,16,384]{2,1,0:T(8,128)(2,1)S(1)}, u32[]{:S(2)}, u32[]{:S(2)}) collective-permute-start(bf16[2,16,384]{2,1,0:T(8,128)(2,1)S(1)} %get-tuple-element.20), channel_id=1, source_target_pairs={{1,2},{2,1},{5,6},{6,5},{9,10},{10,9},{13,14},{14,13},{17,18},{18,... | collective-permute-start | bytes 73736 | tf_op jit(solution)/shard_map/ppermute | solution.py:37
  13.2 4.1 %collective-permute-start.4 = (bf16[8,16,384]{2,1,0:T(8,128)(2,1)S(1)}, bf16[8,16,384]{2,1,0:T(8,128)(2,1)S(1)}, u32[]{:S(2)}, u32[]{:S(2)}) collective-permute-start(bf16[8,16,384]{2,1,0:T(8,128)(2,1)S(1)} %bitcast.114), channel_id=1, source_target_pairs={{4,8},{8,4},{5,9},{9,5},{6,10},{10,6},{7,11},{11,7},{20,24},{24,20... | collective-permute-start | bytes 294920 | tf_op jit(solution)/shard_map/ppermute | solution.py:37
  13.9 4.3 %collective-permute-start.3 = (bf16[8,16,384]{2,1,0:T(8,128)(2,1)S(1)}, bf16[8,16,384]{2,1,0:T(8,128)(2,1)S(1)}, u32[]{:S(2)}, u32[]{:S(2)}) collective-permute-start(bf16[8,16,384]{2,1,0:T(8,128)(2,1)S(1)} %bitcast.115), channel_id=1, source_target_pairs={{0,4},{4,0},{8,12},{12,8},{1,5},{5,1},{9,13},{13,9},{2,6},{6,2},{1... | collective-permute-start | bytes 294920 | tf_op jit(solution)/shard_map/ppermute | solution.py:35
  18.2 0.7 copy-start
  18.9 0.7 copy-start.4
  22.7 43.9 %copy-start.2 = (f32[2,8,384]{2,1,0:T(8,128)}, f32[2,8,384]{2,1,0:T(8,128)S(1)}, u32[]{:S(2)}) copy-start(f32[2,8,384]{2,1,0:T(8,128)S(1)} %get-tuple-element.15.old_ref.x1_ref) | copy-start | bytes 73732
  22.7 7.4 %collective-permute-start.5 = (bf16[2,8,384]{2,1,0:T(8,128)(2,1)S(1)}, bf16[2,8,384]{2,1,0:T(8,128)(2,1)S(1)}, u32[]{:S(2)}, u32[]{:S(2)}) collective-permute-start(bf16[2,8,384]{2,1,0:T(8,128)(2,1)S(1)} %get-tuple-element.16), channel_id=1, source_target_pairs={{0,16},{16,0},{1,17},{17,1},{2,18},{18,2},{3,19},{19,3},{4,20},{20... | collective-permute-start | bytes 36872 | tf_op jit(solution)/shard_map/ppermute | solution.py:35
  30.1 6.6 %collective-permute-start.6 = (bf16[2,8,384]{2,1,0:T(8,128)(2,1)S(1)}, bf16[2,8,384]{2,1,0:T(8,128)(2,1)S(1)}, u32[]{:S(2)}, u32[]{:S(2)}) collective-permute-start(bf16[2,8,384]{2,1,0:T(8,128)(2,1)S(1)} %get-tuple-element.23), channel_id=1, source_target_pairs={{0,1},{1,0},{2,3},{3,2},{4,5},{5,4},{6,7},{7,6},{8,9},{9,8},{10,11... | collective-permute-start | bytes 36872 | tf_op jit(solution)/shard_map/ppermute | solution.py:35
  35.0 1.7 %collective-permute-start.7 = (bf16[2,8,384]{2,1,0:T(8,128)(2,1)S(1)}, bf16[2,8,384]{2,1,0:T(8,128)(2,1)S(1)}, u32[]{:S(2)}, u32[]{:S(2)}) collective-permute-start(bf16[2,8,384]{2,1,0:T(8,128)(2,1)S(1)} %get-tuple-element.24), channel_id=1, source_target_pairs={{1,2},{2,1},{5,6},{6,5},{9,10},{10,9},{13,14},{14,13},{17,18},{18,... | collective-permute-start | bytes 36872 | tf_op jit(solution)/shard_map/ppermute | solution.py:37
  36.7 3.3 %collective-permute-start.9 = (bf16[8,8,384]{2,1,0:T(8,128)(2,1)S(1)}, bf16[8,8,384]{2,1,0:T(8,128)(2,1)S(1)}, u32[]{:S(2)}, u32[]{:S(2)}) collective-permute-start(bf16[8,8,384]{2,1,0:T(8,128)(2,1)S(1)} %bitcast.120), channel_id=1, source_target_pairs={{4,8},{8,4},{5,9},{9,5},{6,10},{10,6},{7,11},{11,7},{20,24},{24,20... | collective-permute-start | bytes 147464 | tf_op jit(solution)/shard_map/ppermute | solution.py:37
  37.4 3.5 %collective-permute-start.8 = (bf16[8,8,384]{2,1,0:T(8,128)(2,1)S(1)}, bf16[8,8,384]{2,1,0:T(8,128)(2,1)S(1)}, u32[]{:S(2)}, u32[]{:S(2)}) collective-permute-start(bf16[8,8,384]{2,1,0:T(8,128)(2,1)S(1)} %bitcast.121), channel_id=1, source_target_pairs={{0,4},{4,0},{8,12},{12,8},{1,5},{5,1},{9,13},{13,9},{2,6},{6,2},{1... | collective-permute-start | bytes 147464 | tf_op jit(solution)/shard_map/ppermute | solution.py:35
  42.1 43.6 %copy-start.3 = (f32[2,8,384]{2,1,0:T(8,128)}, f32[2,8,384]{2,1,0:T(8,128)S(1)}, u32[]{:S(2)}) copy-start(f32[2,8,384]{2,1,0:T(8,128)S(1)} %get-tuple-element.17.x2_ref) | copy-start | bytes 73732
  42.1 3.8 %collective-permute-start.10 = (bf16[2,8,384]{2,1,0:T(8,128)(2,1)S(1)}, bf16[2,8,384]{2,1,0:T(8,128)(2,1)S(1)}, u32[]{:S(2)}, u32[]{:S(2)}) collective-permute-start(bf16[2,8,384]{2,1,0:T(8,128)(2,1)S(1)} %get-tuple-element.18), channel_id=1, source_target_pairs={{0,16},{16,0},{1,17},{17,1},{2,18},{18,2},{3,19},{19,3},{4,20},{20... | collective-permute-start | bytes 36872 | tf_op jit(solution)/shard_map/ppermute | solution.py:35
  45.9 14.3 %collective-permute-start.11 = (bf16[2,8,384]{2,1,0:T(8,128)(2,1)S(1)}, bf16[2,8,384]{2,1,0:T(8,128)(2,1)S(1)}, u32[]{:S(2)}, u32[]{:S(2)}) collective-permute-start(bf16[2,8,384]{2,1,0:T(8,128)(2,1)S(1)} %get-tuple-element.21), channel_id=1, source_target_pairs={{0,1},{1,0},{2,3},{3,2},{4,5},{5,4},{6,7},{7,6},{8,9},{9,8},{10,11... | collective-permute-start | bytes 36872 | tf_op jit(solution)/shard_map/ppermute | solution.py:35
  58.5 1.7 %collective-permute-start.12 = (bf16[2,8,384]{2,1,0:T(8,128)(2,1)S(1)}, bf16[2,8,384]{2,1,0:T(8,128)(2,1)S(1)}, u32[]{:S(2)}, u32[]{:S(2)}) collective-permute-start(bf16[2,8,384]{2,1,0:T(8,128)(2,1)S(1)} %get-tuple-element.22), channel_id=1, source_target_pairs={{1,2},{2,1},{5,6},{6,5},{9,10},{10,9},{13,14},{14,13},{17,18},{18,... | collective-permute-start | bytes 36872 | tf_op jit(solution)/shard_map/ppermute | solution.py:37
  60.2 4.2 %collective-permute-start.14 = (bf16[8,8,384]{2,1,0:T(8,128)(2,1)S(1)}, bf16[8,8,384]{2,1,0:T(8,128)(2,1)S(1)}, u32[]{:S(2)}, u32[]{:S(2)}) collective-permute-start(bf16[8,8,384]{2,1,0:T(8,128)(2,1)S(1)} %bitcast.117), channel_id=1, source_target_pairs={{4,8},{8,4},{5,9},{9,5},{6,10},{10,6},{7,11},{11,7},{20,24},{24,20... | collective-permute-start | bytes 147464 | tf_op jit(solution)/shard_map/ppermute | solution.py:37
  60.9 4.4 %collective-permute-start.13 = (bf16[8,8,384]{2,1,0:T(8,128)(2,1)S(1)}, bf16[8,8,384]{2,1,0:T(8,128)(2,1)S(1)}, u32[]{:S(2)}, u32[]{:S(2)}) collective-permute-start(bf16[8,8,384]{2,1,0:T(8,128)(2,1)S(1)} %bitcast.118), channel_id=1, source_target_pairs={{0,4},{4,0},{8,12},{12,8},{1,5},{5,1},{9,13},{13,9},{2,6},{6,2},{1... | collective-permute-start | bytes 147464 | tf_op jit(solution)/shard_map/ppermute | solution.py:35

commit v2 on v1

v2 whole, which is shorter than its diff:
```python
import functools

import jax
import jax.numpy as jnp
from jax import lax
from jax.experimental import pallas as pl
from jax.experimental.pallas import tpu as pltpu
from jax.sharding import PartitionSpec as P

ITERS = 3
ROOT_ITERS = 12
GROUP = 4
CHUNK = 32

radius = 0.08
floor_sq = 0.0001
epsilon = 1e-06

AXES = ("gx", "gy", "gz")
VMEM = pl.BlockSpec(memory_space=pltpu.VMEM)
HBM = pl.BlockSpec(memory_space=pltpu.HBM)
SMEM = pl.BlockSpec(memory_space=pltpu.SMEM)
f32 = jnp.float32
bf16 = jnp.bfloat16
PLACES = ((0, 0), (0, 1), (0, 2), (1, 1), (1, 2), (2, 2))


def matching(count, parity):
    pairs = []
    for i in range(parity, count - 1, 2):
        pairs += [(i, i + 1), (i + 1, i)]
    return pairs


def swaps(axis, first, second):
    count = lax.axis_size(axis)
    got = [lax.ppermute(first, axis, matching(count, 0))]
    if count > 2:
        got.append(lax.ppermute(second, axis, matching(count, 1)))
    return got


def spread(field):
    blocks, rows, width = field.shape
    columns = jnp.stack([field] + swaps("gx", field, field))
    odd = lax.axis_index("gz") % 2 == 1
    low, high = columns[:, 0], columns[:, blocks - 1]
    got = swaps("gz", jnp.where(odd, low, high), jnp.where(odd, high, low))
    while len(got) < 2:
        got.append(jnp.zeros_like(got[0]))
    deep = jnp.concatenate([columns] + [g[:, None] for g in got], axis=1)
    deep = deep.reshape(-1, rows, width)
    return [deep] + swaps("gy", deep, deep)


def partner(axis, step):
    if lax.axis_size(axis) == 2:
        return jnp.where(step == 0, 0, 1)
    odd = lax.axis_index(axis) % 2
    return jnp.where(step == 0, 0, jnp.where((step < 0) == (odd == 1), 1, 2))


def pair_table(pair_list, pair_count, blocks, columns, zero_slot):
    home, code = pair_list[0, 0, 0, 0], pair_list[0, 0, 0, 1]
    capacity = home.shape[0]
    size = -(-(capacity + blocks * (GROUP - 1)) // GROUP + 1) * GROUP
    step_x, step_y, step_z = code // 9 - 1, code // 3 % 3 - 1, code % 3 - 1
    z = home + step_z
    odd = lax.axis_index("gz") % 2
    below = jnp.where(odd == 1, blocks, blocks + 1)
    above = jnp.where(odd == 1, blocks + 1, blocks)
    if lax.axis_size("gz") == 2:
        below = above = blocks
    z = jnp.where(z < 0, below, jnp.where(z >= blocks, above, z))
    slot = (partner("gy", step_y) * columns + partner("gx", step_x)) * (blocks + 2) + z
    order = lax.iota(jnp.int32, capacity)
    live = order < pair_count[0, 0, 0]
    earlier = order[None, :] < order[:, None]
    place = jnp.zeros_like(order)
    starts = []
    start = jnp.zeros((), jnp.int32)
    index = lax.iota(jnp.int32, size)
    for block in range(blocks):
        mine = live & (home == block)
        rank = jnp.sum(jnp.where(earlier & mine[None, :], 1, 0), axis=1)
        starts.append(start)
        place = jnp.where(mine, start + rank, place)
        start = start + (jnp.sum(jnp.where(mine, 1, 0)) + GROUP - 1) // GROUP * GROUP
    there = live[:, None] & (place[:, None] == index[None, :])
    slots = jnp.sum(jnp.where(there, slot[:, None] - zero_slot, 0), axis=0) + zero_slot
    homes = sum(jnp.where(index * GROUP >= first, 1, 0) for first in starts) - 1
    groups = jnp.full((size,), start // GROUP, jnp.int32)
    return jnp.stack([slots, homes, groups])


def pack_kernel(fill_hbm, noise_hbm, pos_hbm, start_ref, mask_ref, pack_ref, fill_ref, noise_ref, pos_ref, sems):
    pairs = ((fill_hbm, fill_ref), (noise_hbm, noise_ref), (pos_hbm, pos_ref))
    copies = [pltpu.make_async_copy(a, b, sems.at[i]) for i, (a, b) in enumerate(pairs)]
    for copy in copies:
        copy.start()
    for copy in copies:
        copy.wait()
    blocks, samples, width = noise_ref.shape[2:]
    beads = width // 3
    row = lax.broadcasted_iota(jnp.int32, (16, beads), 0)
    for block in range(blocks):
        mask = (lax.broadcasted_iota(jnp.int32, (8, beads), 1) < fill_ref[0, 0, block]).astype(f32)
        mask_ref[block] = mask
        noise = [noise_ref[0, 0, block, :, pl.ds(c * beads, beads)] for c in range(3)]
        start = jnp.concatenate([part * mask[:1] for part in noise], axis=0)
        start_ref[block] = start
        place = jnp.zeros((16, beads), f32)
        for c in range(3):
            pos = pos_ref[0, 0, c, pl.ds(block, 1)]
            high = pos.astype(bf16).astype(f32)
            rest = pos - high
            mid = rest.astype(bf16).astype(f32)
            for i, piece in enumerate((high, mid, rest - mid)):
                place = jnp.where(row == 3 * i + c, piece, place)
        pack_ref[block] = jnp.concatenate([start, place], axis=0).astype(bf16)


def gather_slots(parts, slots_ref):
    count = parts[0].shape[0]
    for i, part in enumerate(parts):
        slots_ref[pl.ds(i * count, count)] = part[...]
    slots_ref[len(parts) * count] = jnp.zeros(slots_ref.shape[1:], bf16)


def position_of(slots_ref, slot, field_rows):
    rows = slots_ref[slot].astype(f32)[field_rows:]
    return [rows[c : c + 1] + rows[3 + c : 4 + c] + rows[6 + c : 7 + c] for c in range(3)]


def turn_position(slots_ref, slot, field_rows):
    away = position_of(slots_ref, slot, field_rows)
    row = lax.broadcasted_iota(jnp.int32, (8, away[0].shape[1]), 0)
    return jnp.transpose(jnp.where(row == 0, away[0], jnp.where(row == 1, away[1], away[2])))


def make_tile(home, turned_ref, tiles_ref, pair, base):
    beads = home[0].shape[1]
    for first in range(0, beads, CHUNK):
        turned = turned_ref[pl.ds(first, CHUNK)]
        d = [turned[:, c : c + 1] - home[c] for c in range(3)]
        dist_sq = d[0] * d[0] + d[1] * d[1] + d[2] * d[2]
        root = lax.rsqrt(jnp.maximum(dist_sq, 1e-30))
        distance = dist_sq * root
        inv_root = jnp.minimum(root, floor_sq**-0.5)
        inverse_sq = inv_root * inv_root
        far = (0.75 * radius) * inv_root
        far_two = (2.0 * radius * radius) * (far * inverse_sq)
        apart = dist_sq >= 4.0 * radius * radius
        isotropic = jnp.where(apart, far + far_two * (1.0 / 3.0), 1.0 - (9.0 / 32.0 / radius) * distance)
        dyadic = jnp.where(apart, far - far_two, (3.0 / 32.0 / radius) * distance) * inverse_sq
        scaled = [dyadic * d[c] for c in range(3)]
        for k, (c, e) in enumerate(PLACES):
            entry = scaled[c] * d[e]
            if c == e:
                entry = entry + isotropic
            tiles_ref[pair, pl.ds(base + first, CHUNK), pl.ds(k * beads, beads)] = entry.astype(bf16)


def add_product(sum_ref, home, product):
    rows, beads = sum_ref.shape[1:]
    samples = rows // 3
    out = [0.0] * 3
    for k, (c, e) in enumerate(PLACES):
        column = product[:, k * beads : (k + 1) * beads]
        out[c] = out[c] + column[e * samples : (e + 1) * samples]
        if c != e:
            out[e] = out[e] + column[c * samples : (c + 1) * samples]
    sum_ref[home] = sum_ref[home] + jnp.concatenate(out, axis=0)


def field_of(table_ref, slots_ref, first, rows):
    return jnp.concatenate([slots_ref[table_ref[0, first + i]][:rows] for i in range(2)], axis=1)


def multiply(table_ref, slots_ref, even_ref, odd_ref, sum_ref, zero_slot):
    rows = sum_ref.shape[1]
    sum_ref[...] = jnp.zeros_like(sum_ref)

    def group(turn, carry):
        first = turn * GROUP
        field = [field_of(table_ref, slots_ref, first + i, rows) for i in (0, 2)]
        odd = jnp.where(table_ref[0, first + 2] == zero_slot, 0, turn)
        tile = jnp.concatenate([even_ref[turn], odd_ref[odd]], axis=0)
        product = jnp.dot(jnp.concatenate(field, axis=1), tile, preferred_element_type=f32)
        add_product(sum_ref, table_ref[1, turn], product)
        return carry

    lax.fori_loop(0, table_ref[2, 0], group, 0)


def new_field(block, mask_ref, sum_ref, old_ref):
    return sum_ref[block] * mask_ref[block, :1] - old_ref[block]


def first_kernel(parts, zero_slot, table_ref, mask_ref, start_ref, *refs):
    given, refs = refs[:parts], refs[parts:]
    even_ref, odd_ref, next_ref, send_ref, slots_ref, sum_ref, turn_even, turn_odd = refs
    blocks, rows, beads = start_ref.shape
    gather_slots(given, slots_ref)
    sum_ref[...] = jnp.zeros_like(sum_ref)
    odd_ref[0] = jnp.zeros(odd_ref.shape[1:], bf16)

    def prepare(first, turned_ref):
        for i in range(2):
            turned_ref[i, :, :8] = turn_position(slots_ref, table_ref[0, first + i], rows)

    def consume(first, tile, index):
        product = jnp.dot(
            field_of(table_ref, slots_ref, first, rows), tile[index], preferred_element_type=f32
        )
        add_product(sum_ref, table_ref[1, first // GROUP], product)

    def make(home, turned_ref, tile, index):
        for i in range(2):
            make_tile(home, turned_ref.at[i], tile, index, i * beads)

    def group(turn, carry):
        pending, spare = carry
        first = turn * GROUP
        home = position_of(slots_ref, table_ref[1, turn], rows)
        full = table_ref[0, first + 2] != zero_slot
        prepare(first + 2, turn_odd)
        consume(pending, odd_ref, spare)
        make(home, turn_even, even_ref, turn)

        @pl.when(full)
        def _():
            prepare(first + GROUP, turn_even)
            consume(first, even_ref, turn)
            make(home, turn_odd, odd_ref, turn)

        @pl.when(jnp.logical_not(full))
        def _():
            prepare(first + GROUP, turn_even)
            consume(first, even_ref, turn)

        return first + 2, jnp.where(full, turn, spare)

    prepare(0, turn_even)
    none = table_ref.shape[1] - 2
    pending, spare = lax.fori_loop(0, table_ref[2, 0], group, (none, 0))
    consume(pending, odd_ref, spare)
    for block in range(blocks):
        new = new_field(block, mask_ref, sum_ref, start_ref)
        next_ref[block] = new
        send_ref[block] = new.astype(bf16)


def next_kernel(parts, zero_slot, table_ref, mask_ref, even_ref, odd_ref, old_ref, *refs):
    given, (next_ref, send_ref, slots_ref, sum_ref) = refs[:parts], refs[parts:]
    gather_slots(given, slots_ref)
    multiply(table_ref, slots_ref, even_ref, odd_ref, sum_ref, zero_slot)
    for block in range(old_ref.shape[0]):
        new = new_field(block, mask_ref, sum_ref, old_ref)
        next_ref[block] = new
        send_ref[block] = new.astype(bf16)


MOMENTS = ((0, 0), (0, 1), (1, 1), (1, 2), (2, 2), (2, 3))


def last_kernel(parts, zero_slot, table_ref, mask_ref, even_ref, odd_ref, x0_ref, x1_ref, x2_ref, *refs):
    given, (moment_ref, slots_ref, sum_ref) = refs[:parts], refs[parts:]
    blocks, rows, beads = x0_ref.shape
    samples = rows // 3
    gather_slots(given, slots_ref)
    multiply(table_ref, slots_ref, even_ref, odd_ref, sum_ref, zero_slot)
    lanes = moment_ref.shape[2]
    lane = lax.broadcasted_iota(jnp.int32, (samples, lanes), 1)
    row = lax.broadcasted_iota(jnp.int32, (samples, lanes), 0)
    sums = [0.0] * len(MOMENTS)
    for block in range(blocks):
        x = [x0_ref[block], x1_ref[block], x2_ref[block]]
        x.append(new_field(block, mask_ref, sum_ref, x2_ref))
        for k, (i, j) in enumerate(MOMENTS):
            both = x[i] * x[j]
            sums[k] = sums[k] + both[:samples] + both[samples : 2 * samples] + both[2 * samples :]
    grid = jnp.zeros((samples, lanes), f32)
    for k, value in enumerate(sums):
        value = jnp.sum(value, axis=1, keepdims=True)
        grid = jnp.where(lane == row + k * samples, value, grid)
    line = jnp.sum(grid, axis=0, keepdims=True)
    moment_ref[...] = jnp.broadcast_to(line[None], moment_ref.shape)


def inverse_symmetric(m):
    a, b, c, d, e, f = m
    ca, cb, cc = d * f - e * e, c * e - b * f, b * e - c * d
    scale = 1.0 / (a * ca + b * cb + c * cc)
    return (ca * scale, cb * scale, cc * scale, (a * f - c * c) * scale, (b * c - a * e) * scale, (a * d - b * b) * scale)


def final_kernel(moment_ref, x0_ref, x1_ref, x2_ref, out_ref):
    blocks, rows, beads = x0_ref.shape
    samples = rows // 3
    lanes = moment_ref.shape[2]
    lane = lax.broadcasted_iota(jnp.int32, (samples, lanes), 1)
    row = lax.broadcasted_iota(jnp.int32, (samples, lanes), 0)
    line = jnp.broadcast_to(jnp.sum(moment_ref[...], axis=0), (samples, lanes))
    m00, m01, m11, m12, m22, m23 = [
        jnp.broadcast_to(
            jnp.sum(jnp.where(lane == row + k * samples, line, 0.0), axis=1, keepdims=True), (samples, lanes)
        )
        for k in range(len(MOMENTS))
    ]
    norm_sq = m00 + epsilon
    start_norm = jnp.sqrt(norm_sq)
    inv_sq = 1.0 / norm_sq
    alpha1 = (m00 + m01) * inv_sq
    c = 1.0 - alpha1
    res_sq = (m11 + c * (2.0 * m01 + c * m00)) * inv_sq
    beta1 = jnp.sqrt(jnp.maximum(res_sq, 0.0) + epsilon)
    k2 = 1.0 / (start_norm * beta1)
    n11 = m11 + c * (2.0 * m01 + c * m00)
    n12 = m12 + c * (2.0 * m11 + c * m01)
    alpha2 = k2 * k2 * (n11 + n12)
    f1 = 1.0 + c - alpha2
    f0 = c - alpha2 * c - beta1 * beta1
    n22 = m22 + f1 * (2.0 * m12 + f1 * m11) + f0 * (2.0 * (m11 + f1 * m01) + f0 * m00)
    beta2 = jnp.sqrt(jnp.maximum(k2 * k2 * n22, 0.0) + epsilon)
    k3 = k2 / beta2
    n23 = m23 + f1 * (2.0 * m22 + f1 * m12) + f0 * (2.0 * (m12 + f1 * m11) + f0 * m01)
    alpha3 = k3 * k3 * (jnp.maximum(n22, 0.0) + n23)

    scale = (alpha1 + alpha2 + alpha3) / 3.0
    inv_scale = 1.0 / scale
    zero, one = jnp.zeros_like(scale), jnp.ones_like(scale)
    y = (alpha1 * inv_scale, beta1 * inv_scale, zero, alpha2 * inv_scale, beta2 * inv_scale, alpha3 * inv_scale)
    z = (one, zero, zero, one, zero, one)
    for _ in range(ROOT_ITERS):
        inv_z, inv_y = inverse_symmetric(z), inverse_symmetric(y)
        y = tuple(0.5 * (p + q) for p, q in zip(y, inv_z))
        z = tuple(0.5 * (p + q) for p, q in zip(z, inv_y))
    root_scale = jnp.sqrt(scale)
    r1, r2, r3 = root_scale * y[0], root_scale * y[1], root_scale * y[2]
    w2, w3 = start_norm * r2 * k2, start_norm * r3 * k3
    p0 = r1 + w2 * c + w3 * f0
    p1 = w2 + w3 * f1
    for block in range(blocks):
        for c in range(3):
            at = pl.ds(c * samples, samples)
            out = p0 * x0_ref[block, at] + p1 * x1_ref[block, at] + w3 * x2_ref[block, at]
            out_ref[0, 0, block, :, pl.ds(c * beads, beads)] = out


def call(kernel, outs, in_specs, scratch=(), limit=None, cost=None):
    return pl.pallas_call(
        kernel,
        out_shape=outs,
        in_specs=in_specs,
        out_specs=jax.tree.map(lambda _: VMEM, outs),
        scratch_shapes=list(scratch),
        compiler_params=pltpu.CompilerParams(vmem_limit_bytes=limit),
        cost_estimate=cost,
    )


def body(positions, block_fill, noise, pair_list, pair_count):
    blocks, beads = positions.shape[2], positions.shape[4]
    samples = noise.shape[3]
    rows = 3 * samples
    shape = (blocks, rows, beads)
    devices = lax.axis_size(AXES)
    columns = 2 if lax.axis_size("gx") == 2 else 3
    parts_y = 2 if lax.axis_size("gy") == 2 else 3
    zero_slot = parts_y * columns * (blocks + 2)
    limit = 24 << 20

    x0, mask, packed = call(
        pack_kernel,
        (
            jax.ShapeDtypeStruct(shape, f32),
            jax.ShapeDtypeStruct((blocks, 8, beads), f32),
            jax.ShapeDtypeStruct((blocks, rows + 16, beads), bf16),
        ),
        [HBM] * 3,
        (
            pltpu.SMEM(block_fill.shape, jnp.int32),
            pltpu.VMEM(noise.shape, f32),
            pltpu.VMEM((1, 1, 3, blocks, beads), f32),
            pltpu.SemaphoreType.DMA((3,)),
        ),
        4 << 20,
    )(block_fill, noise, jnp.swapaxes(positions, 2, 3))
    table = pair_table(pair_list, pair_count, blocks, columns, zero_slot)
    out_field = (jax.ShapeDtypeStruct(shape, f32), jax.ShapeDtypeStruct(shape, bf16))
    tile = jax.ShapeDtypeStruct((table.shape[1] // GROUP, 2 * beads, len(PLACES) * beads), bf16)

    def scratch(rows):
        return (pltpu.VMEM((zero_slot + 1, rows, beads), bf16), pltpu.VMEM(shape, f32))

    parts = spread(packed)
    even, odd, x1, send = call(
        functools.partial(first_kernel, parts_y, zero_slot),
        (tile, tile) + out_field,
        [SMEM] + [VMEM] * (2 + parts_y),
        scratch(rows + 16) + (pltpu.VMEM((2, beads, 128), f32),) * 2,
        limit,
    )(table, mask, x0, *parts)
    parts = spread(send)
    x2, send = call(
        functools.partial(next_kernel, parts_y, zero_slot),
        out_field,
        [SMEM] + [VMEM] * (4 + parts_y),
        scratch(rows),
        limit,
    )(table, mask, even, odd, x1, *parts)
    parts = spread(send)
    moments = call(
        functools.partial(last_kernel, parts_y, zero_slot),
        jax.ShapeDtypeStruct((devices, 1, 128), f32),
        [SMEM] + [VMEM] * (6 + parts_y),
        scratch(rows),
        limit,
    )(table, mask, even, odd, x0, x1, x2, *parts)
    moments = lax.all_to_all(moments, AXES, 0, 0)
    return call(final_kernel, jax.ShapeDtypeStruct(noise.shape, f32), [VMEM] * 4, (), 4 << 20)(moments, x0, x1, x2)


def solution(mesh):
    block = P("gx", "gy", "gz", None, None)
    cell = P("gx", "gy", "gz")
    return jax.shard_map(
        body, mesh=mesh, in_specs=(block, cell, block, block, cell), out_specs=block, check_vma=False
    )
```

time: 88.1 us -> 77.7 us (0.88)
  starting transfers between devices: 43.8 us -> 37.4 us
  Pallas kernels: 8.65 us -> 5.97 us
  between operations: 0.8 us -> 2.15 us
    ppermute x9, starting transfers between devices: 39.9 us -> 33.5 us  [swaps(): got = [lax.ppermute(first, axis, matching(count, 0))]]
    pallas_call x4, Pallas kernels: 7.27 us -> 5.38 us  [the longest x1 2.17 us: body(): call(functools.partial(first_kernel, parts_y, zero_slot), (tile, tile) +...]
    reduce_sum x0 -> x3, other arithmetic: none -> 1.62 us  [the longest x1 1.4 us: pair_table(): jnp.sum(jnp.where(mine, 1, 0)) + GROUP - 1]
    unnamed x11 -> x6, local copies, waits for them, and re-layouts: 2.68 us -> 2.08 us
  transfers between devices with their start and end apart: 15 -> 15, of which waited for: 9 -> 8; matrix products, arithmetic and copies ran while one was open for 1% -> 2% of each run, Pallas kernels for 0% -> 0%
where the time goes in v2:
time: 77.7 us; the launch traced here: 77.3 us
  starting transfers between devices  37.4 us (48%)
  blocking collectives  18.5 us (24%)
  waiting for transfers between devices  9.34 us (12%)
  Pallas kernels  5.97 us (8%)
  local copies, waits for them, and re-layouts  2.16 us (3%)
  between operations  2.15 us (3%)
  other arithmetic  1.78 us (2%)
    ppermute x9, starting transfers between devices, swaps(): got = [lax.ppermute(first, axis, matching(count, 0))]  33.5 us
    all_to_all x1, blocking collectives, body(): moments = lax.all_to_all(moments, AXES, 0, 0)  18.5 us
    ppermute x9, waiting for transfers between devices, swaps(): got = [lax.ppermute(first, axis, matching(count, 0))]  9.33 us
    ppermute x6, starting transfers between devices, swaps(): got.append(lax.ppermute(second, axis, matching(count, 1)))  3.94 us
    pallas_call x1, Pallas kernels, body(): call(functools.partial(first_kernel, parts_y, zero_slot), (tile, tile) +...  2.17 us
    unnamed x6, local copies, waits for them, and re-layouts  2.08 us
  transfers between devices with their start and end apart: 15, of which 8 were waited for; matrix products, arithmetic and copies ran while one was open for 2% of the time, Pallas kernels for 0%

profile of v2, /device:TPU:0, one launch (start us, length us, event | category | flops | bytes accessed | tf_op | source)
XLA Modules:
  0.0 77.3 jit_solution(10950455433201570362)
XLA Ops:
  0.0 0.0 copy-start
  0.0 0.7 copy-done
  0.7 0.0 copy-start.1
  0.7 0.7 copy-done.1
  1.4 0.0 copy-start.2
  1.4 0.7 copy-done.2
  2.1 0.6 shard_map.55
  2.7 3.0 %collective-permute-start = (bf16[2,40,128]{2,1,0:T(8,128)(2,1)S(1)}, bf16[2,40,128]{2,1,0:T(8,128)(2,1)S(1)}, u32[]{:S(2)}, u32[]{:S(2)}) collective-permute-start(bf16[2,40,128]{2,1,0:T(8,128)(2,1)S(1)} %get-tuple-element.16), channel_id=1, source_target_pairs={{0,16},{16,0},{1,17},{17,1},{2,18},{18,2},{3,19},{19,3},{4,20},{20... | collective-permute-start | bytes 61448 | tf_op jit(solution)/shard_map/ppermute | solution.py:37
  6.4 1.4 %select_reduce_fusion.3 = (s32[]{:T(128)}, pred[54]{0:T(512)(128)(4,1)S(1)}, s32[]{:T(128)}, pred[54]{0:T(512)(128)(4,1)S(1)}, s32[54]{0:T(128)S(1)}) fusion(s32[1,1,1,3,54]{4,2,3,1,0:T(1,128)} %param.8, s32[]{:T(128)} %bitcast.107, s32[]{:T(128)S(6)} %select_n.224, s32[]{:T(128)S(6)} %select_n.223, pred[]{:T(512)S(6)} %eq.84), kind=kLoop, calls=%fused_computation.56 | loop fusion | flops 2860 | bytes 777 | tf_op jit(solution)/shard_map/reduce_sum | solution.py:88
  8.4 0.1 select_reduce_fusion.1
  8.6 0.1 select_reduce_fusion
  8.7 0.0 collective-permute-done
  8.7 1.6 %collective-permute-start.1 = (bf16[2,40,128]{2,1,0:T(8,128)(2,1)S(1)}, bf16[2,40,128]{2,1,0:T(8,128)(2,1)S(1)}, u32[]{:S(2)}, u32[]{:S(2)}) collective-permute-start(bf16[2,40,128]{2,1,0:T(8,128)(2,1)S(1)} %get-tuple-element.27), channel_id=1, source_target_pairs={{0,1},{1,0},{2,3},{3,2},{4,5},{5,4},{6,7},{7,6},{8,9},{9,8},{10,11... | collective-permute-start | bytes 61448 | tf_op jit(solution)/shard_map/ppermute | solution.py:37
  10.4 0.7 collective-permute-start.2
  11.7 0.1 pad.20.clone
  11.8 0.8 %collective-permute-done.1 = bf16[2,40,128]{2,1,0:T(8,128)(2,1)S(1)} collective-permute-done((bf16[2,40,128]{2,1,0:T(8,128)(2,1)S(1)}, bf16[2,40,128]{2,1,0:T(8,128)(2,1)S(1)}, u32[]{:S(2)}, u32[]{:S(2)}) %collective-permute-start.1) | collective-permute-done | bytes 20512 | tf_op jit(solution)/shard_map/ppermute | solution.py:37
  12.6 0.0 collective-permute-done.2
  12.6 0.7 collective-permute-start.4
  13.3 2.9 %collective-permute-start.3 = (bf16[8,40,128]{2,1,0:T(8,128)(2,1)S(1)}, bf16[8,40,128]{2,1,0:T(8,128)(2,1)S(1)}, u32[]{:S(2)}, u32[]{:S(2)}) collective-permute-start(bf16[8,40,128]{2,1,0:T(8,128)(2,1)S(1)} %bitcast.109), channel_id=1, source_target_pairs={{0,4},{4,0},{8,12},{12,8},{1,5},{5,1},{9,13},{13,9},{2,6},{6,2},{1... | collective-permute-start | bytes 245768 | tf_op jit(solution)/shard_map/ppermute | solution.py:37
  16.2 0.1 add_add_fusion.table_ref
  16.3 0.0 collective-permute-done.4.refs_2_
  16.3 0.8 %collective-permute-done.3.refs_1_ = bf16[8,40,128]{2,1,0:T(8,128)(2,1)S(1)} collective-permute-done((bf16[8,40,128]{2,1,0:T(8,128)(2,1)S(1)}, bf16[8,40,128]{2,1,0:T(8,128)(2,1)S(1)}, u32[]{:S(2)}, u32[]{:S(2)}) %collective-permute-start.3) | collective-permute-done | bytes 81952 | tf_op jit(solution)/shard_map/ppermute | solution.py:37
  17.1 2.2 %shard_map.56 = (bf16[14,256,768]{2,1,0:T(8,128)(2,1)S(1)}, bf16[14,256,768]{2,1,0:T(8,128)(2,1)S(1)}, f32[2,24,128]{2,1,0:T(8,128)S(1)}, bf16[2,24,128]{2,1,0:T(8,128)(2,1)S(1)}) custom-call(s32[3,56]{1,0:T(4,128)S(1)} %add_add_fusion.table_ref, f32[2,8,128]{2,1,0:T(8,128)S(1)} %get-tuple-element.14.mask_ref, ...), custom_call_target="tpu_custom_call" | custom-call | tf_op jit(solution)/shard_map/pallas_call | solution.py:398
  19.3 1.5 %collective-permute-start.5 = (bf16[2,24,128]{2,1,0:T(8,128)(2,1)S(1)}, bf16[2,24,128]{2,1,0:T(8,128)(2,1)S(1)}, u32[]{:S(2)}, u32[]{:S(2)}) collective-permute-start(bf16[2,24,128]{2,1,0:T(8,128)(2,1)S(1)} %get-tuple-element.20), channel_id=1, source_target_pairs={{0,16},{16,0},{1,17},{17,1},{2,18},{18,2},{3,19},{19,3},{4,20},{20... | collective-permute-start | bytes 36872 | tf_op jit(solution)/shard_map/ppermute | solution.py:37
  20.8 2.2 %collective-permute-done.5 = bf16[2,24,128]{2,1,0:T(8,128)(2,1)S(1)} collective-permute-done((bf16[2,24,128]{2,1,0:T(8,128)(2,1)S(1)}, bf16[2,24,128]{2,1,0:T(8,128)(2,1)S(1)}, u32[]{:S(2)}, u32[]{:S(2)}) %collective-permute-start.5) | collective-permute-done | bytes 12320 | tf_op jit(solution)/shard_map/ppermute | solution.py:37
  23.1 7.4 %collective-permute-start.6 = (bf16[2,24,128]{2,1,0:T(8,128)(2,1)S(1)}, bf16[2,24,128]{2,1,0:T(8,128)(2,1)S(1)}, u32[]{:S(2)}, u32[]{:S(2)}) collective-permute-start(bf16[2,24,128]{2,1,0:T(8,128)(2,1)S(1)} %get-tuple-element.31), channel_id=1, source_target_pairs={{0,1},{1,0},{2,3},{3,2},{4,5},{5,4},{6,7},{7,6},{8,9},{9,8},{10,11... | collective-permute-start | bytes 36872 | tf_op jit(solution)/shard_map/ppermute | solution.py:37
  30.5 0.7 collective-permute-start.7
  31.1 1.0 %collective-permute-done.6 = bf16[2,24,128]{2,1,0:T(8,128)(2,1)S(1)} collective-permute-done((bf16[2,24,128]{2,1,0:T(8,128)(2,1)S(1)}, bf16[2,24,128]{2,1,0:T(8,128)(2,1)S(1)}, u32[]{:S(2)}, u32[]{:S(2)}) %collective-permute-start.6) | collective-permute-done | bytes 12320 | tf_op jit(solution)/shard_map/ppermute | solution.py:37
  32.2 0.0 collective-permute-done.7
  32.2 0.7 collective-permute-start.9
  32.9 4.3 %collective-permute-start.8 = (bf16[8,24,128]{2,1,0:T(8,128)(2,1)S(1)}, bf16[8,24,128]{2,1,0:T(8,128)(2,1)S(1)}, u32[]{:S(2)}, u32[]{:S(2)}) collective-permute-start(bf16[8,24,128]{2,1,0:T(8,128)(2,1)S(1)} %bitcast.115), channel_id=1, source_target_pairs={{0,4},{4,0},{8,12},{12,8},{1,5},{5,1},{9,13},{13,9},{2,6},{6,2},{1... | collective-permute-start | bytes 147464 | tf_op jit(solution)/shard_map/ppermute | solution.py:37
  37.2 0.0 collective-permute-done.9.refs_2_
  37.2 0.9 %collective-permute-done.8.refs_1_ = bf16[8,24,128]{2,1,0:T(8,128)(2,1)S(1)} collective-permute-done((bf16[8,24,128]{2,1,0:T(8,128)(2,1)S(1)}, bf16[8,24,128]{2,1,0:T(8,128)(2,1)S(1)}, u32[]{:S(2)}, u32[]{:S(2)}) %collective-permute-start.8) | collective-permute-done | bytes 49184 | tf_op jit(solution)/shard_map/ppermute | solution.py:37
  38.1 1.1 %shard_map.57 = (f32[2,24,128]{2,1,0:T(8,128)S(1)}, bf16[2,24,128]{2,1,0:T(8,128)(2,1)S(1)}) custom-call(s32[3,56]{1,0:T(4,128)S(1)} %add_add_fusion.table_ref, f32[2,8,128]{2,1,0:T(8,128)S(1)} %get-tuple-element.14.mask_ref, bf16[14,256,768]{2,1,0:T(8,128)(2,1)S(1)} %get-tuple-element.17.even_ref, bf16[14,256,768]{2,1,0:T(8,128)(2,1)S(1)} %get-tuple-element.18.odd_ref, ...), custom_call_target="tpu_custom_call" | custom-call | tf_op jit(solution)/shard_map/pallas_call | solution.py:406
  39.1 2.3 %collective-permute-start.10 = (bf16[2,24,128]{2,1,0:T(8,128)(2,1)S(1)}, bf16[2,24,128]{2,1,0:T(8,128)(2,1)S(1)}, u32[]{:S(2)}, u32[]{:S(2)}) collective-permute-start(bf16[2,24,128]{2,1,0:T(8,128)(2,1)S(1)} %get-tuple-element.22), channel_id=1, source_target_pairs={{0,16},{16,0},{1,17},{17,1},{2,18},{18,2},{3,19},{19,3},{4,20},{20... | collective-permute-start | bytes 36872 | tf_op jit(solution)/shard_map/ppermute | solution.py:37
  41.5 1.7 %collective-permute-done.10 = bf16[2,24,128]{2,1,0:T(8,128)(2,1)S(1)} collective-permute-done((bf16[2,24,128]{2,1,0:T(8,128)(2,1)S(1)}, bf16[2,24,128]{2,1,0:T(8,128)(2,1)S(1)}, u32[]{:S(2)}, u32[]{:S(2)}) %collective-permute-start.10) | collective-permute-done | bytes 12320 | tf_op jit(solution)/shard_map/ppermute | solution.py:37
  43.1 5.9 %collective-permute-start.11 = (bf16[2,24,128]{2,1,0:T(8,128)(2,1)S(1)}, bf16[2,24,128]{2,1,0:T(8,128)(2,1)S(1)}, u32[]{:S(2)}, u32[]{:S(2)}) collective-permute-start(bf16[2,24,128]{2,1,0:T(8,128)(2,1)S(1)} %get-tuple-element.29), channel_id=1, source_target_pairs={{0,1},{1,0},{2,3},{3,2},{4,5},{5,4},{6,7},{7,6},{8,9},{9,8},{10,11... | collective-permute-start | bytes 36872 | tf_op jit(solution)/shard_map/ppermute | solution.py:37
  49.1 0.7 collective-permute-start.12
  49.7 1.0 %collective-permute-done.11 = bf16[2,24,128]{2,1,0:T(8,128)(2,1)S(1)} collective-permute-done((bf16[2,24,128]{2,1,0:T(8,128)(2,1)S(1)}, bf16[2,24,128]{2,1,0:T(8,128)(2,1)S(1)}, u32[]{:S(2)}, u32[]{:S(2)}) %collective-permute-start.11) | collective-permute-done | bytes 12320 | tf_op jit(solution)/shard_map/ppermute | solution.py:37
  50.8 0.0 collective-permute-done.12
  50.8 0.7 collective-permute-start.14
  51.4 4.3 %collective-permute-start.13 = (bf16[8,24,128]{2,1,0:T(8,128)(2,1)S(1)}, bf16[8,24,128]{2,1,0:T(8,128)(2,1)S(1)}, u32[]{:S(2)}, u32[]{:S(2)}) collective-permute-start(bf16[8,24,128]{2,1,0:T(8,128)(2,1)S(1)} %bitcast.112), channel_id=1, source_target_pairs={{0,4},{4,0},{8,12},{12,8},{1,5},{5,1},{9,13},{13,9},{2,6},{6,2},{1... | collective-permute-start | bytes 147464 | tf_op jit(solution)/shard_map/ppermute | solution.py:37
  55.8 0.0 collective-permute-done.14.refs_2_
  55.8 0.9 %collective-permute-done.13.refs_1_ = bf16[8,24,128]{2,1,0:T(8,128)(2,1)S(1)} collective-permute-done((bf16[8,24,128]{2,1,0:T(8,128)(2,1)S(1)}, bf16[8,24,128]{2,1,0:T(8,128)(2,1)S(1)}, u32[]{:S(2)}, u32[]{:S(2)}) %collective-permute-start.13) | collective-permute-done | bytes 49184 | tf_op jit(solution)/shard_map/ppermute | solution.py:37
  56.7 1.2 %shard_map.58 = f32[32,1,128]{2,1,0:T(1,128)S(1)} custom-call(s32[3,56]{1,0:T(4,128)S(1)} %add_add_fusion.table_ref, f32[2,8,128]{2,1,0:T(8,128)S(1)} %get-tuple-element.14.mask_ref, bf16[14,256,768]{2,1,0:T(8,128)(2,1)S(1)} %get-tuple-element.17.even_ref, bf16[14,256,768]{2,1,0:T(8,128)(2,1)S(1)} %get-tuple-element.18.odd_ref, ...), custom_call_target="tpu_custom_call" | custom-call | tf_op jit(solution)/shard_map/pallas_call | solution.py:414
  57.8 18.5 %all_to_all.5.moment_ref = f32[32,1,128]{2,1,0:T(1,128)S(1)} all-to-all(f32[32,1,128]{2,1,0:T(1,128)S(1)} %shard_map.58), channel_id=1, replica_groups=mesh['gx'=2,'gy'=4,'gz'=4] {'gx','gy','gz'}, dimensions={0} | all-to-all | bytes 32768 | tf_op jit(solution)/shard_map/all_to_all | solution.py:421
  76.3 1.0 %shard_map.59 = f32[1,1,2,8,384]{4,3,2,1,0:T(8,128)} custom-call(f32[32,1,128]{2,1,0:T(1,128)S(1)} %all_to_all.5.moment_ref, f32[2,24,128]{2,1,0:T(8,128)S(1)} %get-tuple-element.15.start_ref.x0_ref, f32[2,24,128]{2,1,0:T(8,128)S(1)} %get-tuple-element.19.old_ref.x1_ref, f32[2,24,128]{2,1,0:T(8,128)S(1)} %get-tuple-element.21.x2_ref), custom_call_target="tpu_custom_call" | custom-call | tf_op jit(solution)/shard_map/pallas_call | solution.py:422
  (11 shorter events, 0.1 us)
Async XLA Ops:
  0.0 0.7 copy-start
  0.7 0.7 copy-start.1
  1.4 0.7 copy-start.2
  2.7 6.0 %collective-permute-start = (bf16[2,40,128]{2,1,0:T(8,128)(2,1)S(1)}, bf16[2,40,128]{2,1,0:T(8,128)(2,1)S(1)}, u32[]{:S(2)}, u32[]{:S(2)}) collective-permute-start(bf16[2,40,128]{2,1,0:T(8,128)(2,1)S(1)} %get-tuple-element.16), channel_id=1, source_target_pairs={{0,16},{16,0},{1,17},{17,1},{2,18},{18,2},{3,19},{19,3},{4,20},{20... | collective-permute-start | bytes 61448 | tf_op jit(solution)/shard_map/ppermute | solution.py:37
  8.7 3.8 %collective-permute-start.1 = (bf16[2,40,128]{2,1,0:T(8,128)(2,1)S(1)}, bf16[2,40,128]{2,1,0:T(8,128)(2,1)S(1)}, u32[]{:S(2)}, u32[]{:S(2)}) collective-permute-start(bf16[2,40,128]{2,1,0:T(8,128)(2,1)S(1)} %get-tuple-element.27), channel_id=1, source_target_pairs={{0,1},{1,0},{2,3},{3,2},{4,5},{5,4},{6,7},{7,6},{8,9},{9,8},{10,11... | collective-permute-start | bytes 61448 | tf_op jit(solution)/shard_map/ppermute | solution.py:37
  10.4 2.2 %collective-permute-start.2 = (bf16[2,40,128]{2,1,0:T(8,128)(2,1)S(1)}, bf16[2,40,128]{2,1,0:T(8,128)(2,1)S(1)}, u32[]{:S(2)}, u32[]{:S(2)}) collective-permute-start(bf16[2,40,128]{2,1,0:T(8,128)(2,1)S(1)} %get-tuple-element.28), channel_id=1, source_target_pairs={{1,2},{2,1},{5,6},{6,5},{9,10},{10,9},{13,14},{14,13},{17,18},{18,... | collective-permute-start | bytes 61448 | tf_op jit(solution)/shard_map/ppermute | solution.py:39
  12.6 3.7 %collective-permute-start.4 = (bf16[8,40,128]{2,1,0:T(8,128)(2,1)S(1)}, bf16[8,40,128]{2,1,0:T(8,128)(2,1)S(1)}, u32[]{:S(2)}, u32[]{:S(2)}) collective-permute-start(bf16[8,40,128]{2,1,0:T(8,128)(2,1)S(1)} %bitcast.108), channel_id=1, source_target_pairs={{4,8},{8,4},{5,9},{9,5},{6,10},{10,6},{7,11},{11,7},{20,24},{24,20... | collective-permute-start | bytes 245768 | tf_op jit(solution)/shard_map/ppermute | solution.py:39
  13.3 3.9 %collective-permute-start.3 = (bf16[8,40,128]{2,1,0:T(8,128)(2,1)S(1)}, bf16[8,40,128]{2,1,0:T(8,128)(2,1)S(1)}, u32[]{:S(2)}, u32[]{:S(2)}) collective-permute-start(bf16[8,40,128]{2,1,0:T(8,128)(2,1)S(1)} %bitcast.109), channel_id=1, source_target_pairs={{0,4},{4,0},{8,12},{12,8},{1,5},{5,1},{9,13},{13,9},{2,6},{6,2},{1... | collective-permute-start | bytes 245768 | tf_op jit(solution)/shard_map/ppermute | solution.py:37
  19.3 3.8 %collective-permute-start.5 = (bf16[2,24,128]{2,1,0:T(8,128)(2,1)S(1)}, bf16[2,24,128]{2,1,0:T(8,128)(2,1)S(1)}, u32[]{:S(2)}, u32[]{:S(2)}) collective-permute-start(bf16[2,24,128]{2,1,0:T(8,128)(2,1)S(1)} %get-tuple-element.20), channel_id=1, source_target_pairs={{0,16},{16,0},{1,17},{17,1},{2,18},{18,2},{3,19},{19,3},{4,20},{20... | collective-permute-start | bytes 36872 | tf_op jit(solution)/shard_map/ppermute | solution.py:37
  23.1 9.1 %collective-permute-start.6 = (bf16[2,24,128]{2,1,0:T(8,128)(2,1)S(1)}, bf16[2,24,128]{2,1,0:T(8,128)(2,1)S(1)}, u32[]{:S(2)}, u32[]{:S(2)}) collective-permute-start(bf16[2,24,128]{2,1,0:T(8,128)(2,1)S(1)} %get-tuple-element.31), channel_id=1, source_target_pairs={{0,1},{1,0},{2,3},{3,2},{4,5},{5,4},{6,7},{7,6},{8,9},{9,8},{10,11... | collective-permute-start | bytes 36872 | tf_op jit(solution)/shard_map/ppermute | solution.py:37
  30.5 1.7 %collective-permute-start.7 = (bf16[2,24,128]{2,1,0:T(8,128)(2,1)S(1)}, bf16[2,24,128]{2,1,0:T(8,128)(2,1)S(1)}, u32[]{:S(2)}, u32[]{:S(2)}) collective-permute-start(bf16[2,24,128]{2,1,0:T(8,128)(2,1)S(1)} %get-tuple-element.32), channel_id=1, source_target_pairs={{1,2},{2,1},{5,6},{6,5},{9,10},{10,9},{13,14},{14,13},{17,18},{18,... | collective-permute-start | bytes 36872 | tf_op jit(solution)/shard_map/ppermute | solution.py:39
  32.2 5.0 %collective-permute-start.9 = (bf16[8,24,128]{2,1,0:T(8,128)(2,1)S(1)}, bf16[8,24,128]{2,1,0:T(8,128)(2,1)S(1)}, u32[]{:S(2)}, u32[]{:S(2)}) collective-permute-start(bf16[8,24,128]{2,1,0:T(8,128)(2,1)S(1)} %bitcast.114), channel_id=1, source_target_pairs={{4,8},{8,4},{5,9},{9,5},{6,10},{10,6},{7,11},{11,7},{20,24},{24,20... | collective-permute-start | bytes 147464 | tf_op jit(solution)/shard_map/ppermute | solution.py:39
  32.9 5.2 %collective-permute-start.8 = (bf16[8,24,128]{2,1,0:T(8,128)(2,1)S(1)}, bf16[8,24,128]{2,1,0:T(8,128)(2,1)S(1)}, u32[]{:S(2)}, u32[]{:S(2)}) collective-permute-start(bf16[8,24,128]{2,1,0:T(8,128)(2,1)S(1)} %bitcast.115), channel_id=1, source_target_pairs={{0,4},{4,0},{8,12},{12,8},{1,5},{5,1},{9,13},{13,9},{2,6},{6,2},{1... | collective-permute-start | bytes 147464 | tf_op jit(solution)/shard_map/ppermute | solution.py:37
  39.1 4.0 %collective-permute-start.10 = (bf16[2,24,128]{2,1,0:T(8,128)(2,1)S(1)}, bf16[2,24,128]{2,1,0:T(8,128)(2,1)S(1)}, u32[]{:S(2)}, u32[]{:S(2)}) collective-permute-start(bf16[2,24,128]{2,1,0:T(8,128)(2,1)S(1)} %get-tuple-element.22), channel_id=1, source_target_pairs={{0,16},{16,0},{1,17},{17,1},{2,18},{18,2},{3,19},{19,3},{4,20},{20... | collective-permute-start | bytes 36872 | tf_op jit(solution)/shard_map/ppermute | solution.py:37
  43.1 7.6 %collective-permute-start.11 = (bf16[2,24,128]{2,1,0:T(8,128)(2,1)S(1)}, bf16[2,24,128]{2,1,0:T(8,128)(2,1)S(1)}, u32[]{:S(2)}, u32[]{:S(2)}) collective-permute-start(bf16[2,24,128]{2,1,0:T(8,128)(2,1)S(1)} %get-tuple-element.29), channel_id=1, source_target_pairs={{0,1},{1,0},{2,3},{3,2},{4,5},{5,4},{6,7},{7,6},{8,9},{9,8},{10,11... | collective-permute-start | bytes 36872 | tf_op jit(solution)/shard_map/ppermute | solution.py:37
  49.1 1.7 %collective-permute-start.12 = (bf16[2,24,128]{2,1,0:T(8,128)(2,1)S(1)}, bf16[2,24,128]{2,1,0:T(8,128)(2,1)S(1)}, u32[]{:S(2)}, u32[]{:S(2)}) collective-permute-start(bf16[2,24,128]{2,1,0:T(8,128)(2,1)S(1)} %get-tuple-element.30), channel_id=1, source_target_pairs={{1,2},{2,1},{5,6},{6,5},{9,10},{10,9},{13,14},{14,13},{17,18},{18,... | collective-permute-start | bytes 36872 | tf_op jit(solution)/shard_map/ppermute | solution.py:39
  50.8 5.0 %collective-permute-start.14 = (bf16[8,24,128]{2,1,0:T(8,128)(2,1)S(1)}, bf16[8,24,128]{2,1,0:T(8,128)(2,1)S(1)}, u32[]{:S(2)}, u32[]{:S(2)}) collective-permute-start(bf16[8,24,128]{2,1,0:T(8,128)(2,1)S(1)} %bitcast.111), channel_id=1, source_target_pairs={{4,8},{8,4},{5,9},{9,5},{6,10},{10,6},{7,11},{11,7},{20,24},{24,20... | collective-permute-start | bytes 147464 | tf_op jit(solution)/shard_map/ppermute | solution.py:39
  51.4 5.2 %collective-permute-start.13 = (bf16[8,24,128]{2,1,0:T(8,128)(2,1)S(1)}, bf16[8,24,128]{2,1,0:T(8,128)(2,1)S(1)}, u32[]{:S(2)}, u32[]{:S(2)}) collective-permute-start(bf16[8,24,128]{2,1,0:T(8,128)(2,1)S(1)} %bitcast.112), channel_id=1, source_target_pairs={{0,4},{4,0},{8,12},{12,8},{1,5},{5,1},{9,13},{13,9},{2,6},{6,2},{1... | collective-permute-start | bytes 147464 | tf_op jit(solution)/shard_map/ppermute | solution.py:37

commit v3 on v2

--- a/solution.py
+++ b/solution.py
@@ -40,57 +40,98 @@
     return got
 
 
-def spread(field):
-    blocks, rows, width = field.shape
+def spread(field, *before):
     columns = jnp.stack([field] + swaps("gx", field, field))
+    columns, *before = lax.optimization_barrier((columns, *before))
+    columns = jnp.concatenate([columns] + swaps("gy", columns, columns))
     odd = lax.axis_index("gz") % 2 == 1
-    low, high = columns[:, 0], columns[:, blocks - 1]
-    got = swaps("gz", jnp.where(odd, low, high), jnp.where(odd, high, low))
-    while len(got) < 2:
-        got.append(jnp.zeros_like(got[0]))
-    deep = jnp.concatenate([columns] + [g[:, None] for g in got], axis=1)
-    deep = deep.reshape(-1, rows, width)
-    return [deep] + swaps("gy", deep, deep)
-
-
-def partner(axis, step):
-    if lax.axis_size(axis) == 2:
-        return jnp.where(step == 0, 0, 1)
-    odd = lax.axis_index(axis) % 2
-    return jnp.where(step == 0, 0, jnp.where((step < 0) == (odd == 1), 1, 2))
-
-
-def pair_table(pair_list, pair_count, blocks, columns, zero_slot):
-    home, code = pair_list[0, 0, 0, 0], pair_list[0, 0, 0, 1]
-    capacity = home.shape[0]
-    size = -(-(capacity + blocks * (GROUP - 1)) // GROUP + 1) * GROUP
-    step_x, step_y, step_z = code // 9 - 1, code // 3 % 3 - 1, code % 3 - 1
-    z = home + step_z
-    odd = lax.axis_index("gz") % 2
-    below = jnp.where(odd == 1, blocks, blocks + 1)
-    above = jnp.where(odd == 1, blocks + 1, blocks)
-    if lax.axis_size("gz") == 2:
-        below = above = blocks
-    z = jnp.where(z < 0, below, jnp.where(z >= blocks, above, z))
-    slot = (partner("gy", step_y) * columns + partner("gx", step_x)) * (blocks + 2) + z
-    order = lax.iota(jnp.int32, capacity)
-    live = order < pair_count[0, 0, 0]
-    earlier = order[None, :] < order[:, None]
-    place = jnp.zeros_like(order)
-    starts = []
-    start = jnp.zeros((), jnp.int32)
-    index = lax.iota(jnp.int32, size)
-    for block in range(blocks):
-        mine = live & (home == block)
-        rank = jnp.sum(jnp.where(earlier & mine[None, :], 1, 0), axis=1)
-        starts.append(start)
-        place = jnp.where(mine, start + rank, place)
-        start = start + (jnp.sum(jnp.where(mine, 1, 0)) + GROUP - 1) // GROUP * GROUP
-    there = live[:, None] & (place[:, None] == index[None, :])
-    slots = jnp.sum(jnp.where(there, slot[:, None] - zero_slot, 0), axis=0) + zero_slot
-    homes = sum(jnp.where(index * GROUP >= first, 1, 0) for first in starts) - 1
-    groups = jnp.full((size,), start // GROUP, jnp.int32)
-    return jnp.stack([slots, homes, groups])
+    low, high = columns[:, 0], columns[:, field.shape[0] - 1]
+    far = swaps("gz", jnp.where(odd, low, high), jnp.where(odd, high, low))
+    return columns.reshape((-1,) + field.shape[1:]), far, *before
+
+
+def table_kernel(sizes, slots, blocks, odd_ref, count_ref, list_hbm, near_ref, far_ref, list_ref, sem):
+    copy = pltpu.make_async_copy(list_hbm, list_ref, sem)
+    copy.start()
+    outs = (near_ref, far_ref)
+    for out, empty in zip(outs, slots):
+        for block in range(blocks):
+            out[1, block] = 0
+        for i in range(2):
+            out[0, out.shape[1] - 1 - i] = empty
+    odd = [odd_ref[axis] == 1 for axis in range(3)]
+
+    def partner(axis, step):
+        if sizes[axis] == 2:
+            return jnp.where(step == 0, 0, 1)
+        return jnp.where(step == 0, 0, jnp.where((step < 0) == odd[axis], 1, 2))
+
+    segment = near_ref.shape[1] // blocks
+
+    def enter(t, carry):
+        home, code = list_ref[0, 0, 0, 0, t], list_ref[0, 0, 1, 0, t]
+        plane, third = (code * 57) >> 9, (code * 43) >> 7
+        column = partner(1, third - 3 * plane - 1) * (2 if sizes[0] == 2 else 3) + partner(0, plane - 1)
+        z = home + code - 3 * third - 1
+        far = (z < 0) | (z >= blocks)
+
+        @pl.when(jnp.logical_not(far))
+        def _():
+            place = near_ref[1, home]
+            near_ref[1, home] = place + 1
+            near_ref[0, home * segment + place] = column * blocks + z
+
+        @pl.when(far)
+        def _():
+            place = far_ref[1, home]
+            far_ref[1, home] = place + 1
+            side = partner(2, jnp.where(z < 0, -1, 1)) - 1
+            far_ref[0, home * segment + place] = side * (slots[0] // blocks) + column
+
+        return carry
+
+    copy.wait()
+    lax.fori_loop(0, count_ref[0, 0, 0], enter, 0)
+    for out, empty in zip(outs, slots):
+        for block in range(blocks):
+            end = block * segment + out[1, block]
+            for i in range(GROUP + 1):
+                out[0, end + i] = empty
+
+
+def pair_tables(pair_list, pair_count, blocks, near_slots, far_slots):
+    segment = -(-pair_list.shape[4] // GROUP + 2) * GROUP
+    table = jax.ShapeDtypeStruct((2, blocks * segment), jnp.int32)
+    sizes = [lax.axis_size(axis) for axis in AXES]
+    odd = jnp.stack([lax.axis_index(axis) % 2 for axis in AXES])
+    pair_list = pltpu.with_memory_space_constraint(jnp.swapaxes(pair_list, 2, 3), pltpu.HBM)
+    return pl.pallas_call(
+        functools.partial(table_kernel, sizes, (near_slots, far_slots), blocks),
+        out_shape=(table, table),
+        in_specs=[SMEM, SMEM, HBM],
+        out_specs=(SMEM, SMEM),
+        scratch_shapes=[
+            pltpu.SMEM(pair_list.shape, jnp.int32),
+            pltpu.SemaphoreType.DMA,
+        ],
+        compiler_params=pltpu.CompilerParams(vmem_limit_bytes=1 << 20),
+        cost_estimate=pl.CostEstimate(flops=10**6, bytes_accessed=10**6, transcendentals=0),
+    )(odd, pair_count, pair_list)
+
+
+def groups_of(table_ref, blocks):
+    segment = table_ref.shape[1] // blocks
+    counts = [(table_ref[1, block] + (GROUP - 1)) // GROUP for block in range(blocks)]
+    ends = [sum(counts[: block + 1]) for block in range(blocks)]
+
+    def home_of(turn):
+        return sum([jnp.where(turn >= end, 1, 0) for end in ends[:-1]], 0)
+
+    def first_of(turn):
+        skip = [jnp.where(turn >= ends[i], segment - counts[i] * GROUP, 0) for i in range(blocks - 1)]
+        return turn * GROUP + sum(skip)
+
+    return ends[-1], home_of, first_of
 
 
 def pack_kernel(fill_hbm, noise_hbm, pos_hbm, start_ref, mask_ref, pack_ref, fill_ref, noise_ref, pos_ref, sems):
@@ -115,8 +156,8 @@
             high = pos.astype(bf16).astype(f32)
             rest = pos - high
             mid = rest.astype(bf16).astype(f32)
-            for i, piece in enumerate((high, mid, rest - mid)):
-                place = jnp.where(row == 3 * i + c, piece, place)
+            for i, piece in ((0, high), (8, mid), (3, rest - mid)):
+                place = jnp.where(row == i + c, piece, place)
         pack_ref[block] = jnp.concatenate([start, place], axis=0).astype(bf16)
 
 
@@ -129,20 +170,22 @@
 
 def position_of(slots_ref, slot, field_rows):
     rows = slots_ref[slot].astype(f32)[field_rows:]
-    return [rows[c : c + 1] + rows[3 + c : 4 + c] + rows[6 + c : 7 + c] for c in range(3)]
-
-
-def turn_position(slots_ref, slot, field_rows):
-    away = position_of(slots_ref, slot, field_rows)
-    row = lax.broadcasted_iota(jnp.int32, (8, away[0].shape[1]), 0)
-    return jnp.transpose(jnp.where(row == 0, away[0], jnp.where(row == 1, away[1], away[2])))
-
-
-def make_tile(home, turned_ref, tiles_ref, pair, base):
-    beads = home[0].shape[1]
+    return rows[:8] + rows[8:] + pltpu.roll(rows[:8], 5, 0)
+
+
+def turn_positions(slots_ref, first, second, field_rows):
+    first = position_of(slots_ref, first, field_rows)
+    second = pltpu.roll(position_of(slots_ref, second, field_rows), 3, 0)
+    row = lax.broadcasted_iota(jnp.int32, first.shape, 0)
+    return jnp.transpose(jnp.where(row < 3, first, second))
+
+
+def make_tile(home, turned_ref, tiles_ref, pair, half):
+    beads = home.shape[1]
+    base = half * beads
     for first in range(0, beads, CHUNK):
         turned = turned_ref[pl.ds(first, CHUNK)]
-        d = [turned[:, c : c + 1] - home[c] for c in range(3)]
+        d = [turned[:, 3 * half + c : 3 * half + c + 1] - home[c : c + 1] for c in range(3)]
         dist_sq = d[0] * d[0] + d[1] * d[1] + d[2] * d[2]
         root = lax.rsqrt(jnp.maximum(dist_sq, 1e-30))
         distance = dist_sq * root
@@ -177,84 +220,103 @@
     return jnp.concatenate([slots_ref[table_ref[0, first + i]][:rows] for i in range(2)], axis=1)
 
 
-def multiply(table_ref, slots_ref, even_ref, odd_ref, sum_ref, zero_slot):
-    rows = sum_ref.shape[1]
-    sum_ref[...] = jnp.zeros_like(sum_ref)
+def multiply(table_ref, slots_ref, even_ref, odd_ref, sum_ref):
+    blocks, rows = sum_ref.shape[:2]
+    zero_slot = slots_ref.shape[0] - 1
+    count, home_of, first_of = groups_of(table_ref, blocks)
 
     def group(turn, carry):
-        first = turn * GROUP
+        first = first_of(turn)
         field = [field_of(table_ref, slots_ref, first + i, rows) for i in (0, 2)]
         odd = jnp.where(table_ref[0, first + 2] == zero_slot, 0, turn)
         tile = jnp.concatenate([even_ref[turn], odd_ref[odd]], axis=0)
         product = jnp.dot(jnp.concatenate(field, axis=1), tile, preferred_element_type=f32)
-        add_product(sum_ref, table_ref[1, turn], product)
+        add_product(sum_ref, home_of(turn), product)
         return carry
 
-    lax.fori_loop(0, table_ref[2, 0], group, 0)
+    lax.fori_loop(0, count, group, 0)
 
 
 def new_field(block, mask_ref, sum_ref, old_ref):
     return sum_ref[block] * mask_ref[block, :1] - old_ref[block]
 
 
-def first_kernel(parts, zero_slot, table_ref, mask_ref, start_ref, *refs):
-    given, refs = refs[:parts], refs[parts:]
-    even_ref, odd_ref, next_ref, send_ref, slots_ref, sum_ref, turn_even, turn_odd = refs
-    blocks, rows, beads = start_ref.shape
-    gather_slots(given, slots_ref)
-    sum_ref[...] = jnp.zeros_like(sum_ref)
+def build(table_ref, own_ref, slots_ref, even_ref, odd_ref, sum_ref, turn_even, turn_odd):
+    blocks, rows, beads = sum_ref.shape
+    zero_slot = slots_ref.shape[0] - 1
+    count, home_of, first_of = groups_of(table_ref, blocks)
     odd_ref[0] = jnp.zeros(odd_ref.shape[1:], bf16)
 
     def prepare(first, turned_ref):
-        for i in range(2):
-            turned_ref[i, :, :8] = turn_position(slots_ref, table_ref[0, first + i], rows)
-
-    def consume(first, tile, index):
+        turned_ref[:, :8] = turn_positions(slots_ref, table_ref[0, first], table_ref[0, first + 1], rows)
+
+    def consume(home, first, tile, index):
         product = jnp.dot(
             field_of(table_ref, slots_ref, first, rows), tile[index], preferred_element_type=f32
         )
-        add_product(sum_ref, table_ref[1, first // GROUP], product)
+        add_product(sum_ref, home, product)
 
     def make(home, turned_ref, tile, index):
         for i in range(2):
-            make_tile(home, turned_ref.at[i], tile, index, i * beads)
+            make_tile(home, turned_ref, tile, index, i)
 
     def group(turn, carry):
-        pending, spare = carry
-        first = turn * GROUP
-        home = position_of(slots_ref, table_ref[1, turn], rows)
+        pending, pending_home, spare = carry
+        first, home = first_of(turn), home_of(turn)
+        place = position_of(own_ref, home, rows)
         full = table_ref[0, first + 2] != zero_slot
+        make(place, turn_even, even_ref, turn)
         prepare(first + 2, turn_odd)
-        consume(pending, odd_ref, spare)
-        make(home, turn_even, even_ref, turn)
+        consume(pending_home, pending, odd_ref, spare)
 
         @pl.when(full)
         def _():
-            prepare(first + GROUP, turn_even)
-            consume(first, even_ref, turn)
-            make(home, turn_odd, odd_ref, turn)
+            make(place, turn_odd, odd_ref, turn)
+            prepare(first_of(turn + 1), turn_even)
+            consume(home, first, even_ref, turn)
 
         @pl.when(jnp.logical_not(full))
         def _():
-            prepare(first + GROUP, turn_even)
-            consume(first, even_ref, turn)
-
-        return first + 2, jnp.where(full, turn, spare)
-
-    prepare(0, turn_even)
+            prepare(first_of(turn + 1), turn_even)
+            consume(home, first, even_ref, turn)
+
+        return first + 2, home, jnp.where(full, turn, spare)
+
+    prepare(first_of(0), turn_even)
     none = table_ref.shape[1] - 2
-    pending, spare = lax.fori_loop(0, table_ref[2, 0], group, (none, 0))
-    consume(pending, odd_ref, spare)
-    for block in range(blocks):
-        new = new_field(block, mask_ref, sum_ref, start_ref)
-        next_ref[block] = new
-        send_ref[block] = new.astype(bf16)
-
-
-def next_kernel(parts, zero_slot, table_ref, mask_ref, even_ref, odd_ref, old_ref, *refs):
-    given, (next_ref, send_ref, slots_ref, sum_ref) = refs[:parts], refs[parts:]
+    pending, pending_home, spare = lax.fori_loop(0, count, group, (none, 0, 0))
+    consume(pending_home, pending, odd_ref, spare)
+
+
+def build_near(table_ref, own_ref, part_ref, even_ref, odd_ref, sum_ref, slots_ref, *turned):
+    gather_slots([part_ref], slots_ref)
+    sum_ref[...] = jnp.zeros_like(sum_ref)
+    build(table_ref, own_ref, slots_ref, even_ref, odd_ref, sum_ref, *turned)
+
+
+def build_far(sides, table_ref, own_ref, mask_ref, old_ref, near_ref, *refs):
+    given, (even_ref, odd_ref, next_ref, send_ref, slots_ref, sum_ref, *turned) = refs[:sides], refs[sides:]
     gather_slots(given, slots_ref)
-    multiply(table_ref, slots_ref, even_ref, odd_ref, sum_ref, zero_slot)
+    sum_ref[...] = near_ref[...]
+    build(table_ref, own_ref, slots_ref, even_ref, odd_ref, sum_ref, *turned)
+    finish(mask_ref, sum_ref, old_ref, next_ref, send_ref)
+
+
+def apply_near(table_ref, even_ref, odd_ref, part_ref, sum_ref, slots_ref):
+    gather_slots([part_ref], slots_ref)
+    sum_ref[...] = jnp.zeros_like(sum_ref)
+    multiply(table_ref, slots_ref, even_ref, odd_ref, sum_ref)
+
+
+def apply_far(sides, table_ref, even_ref, odd_ref, mask_ref, old_ref, near_ref, *refs):
+    given, (next_ref, send_ref, slots_ref, sum_ref) = refs[:sides], refs[sides:]
+    gather_slots(given, slots_ref)
+    sum_ref[...] = near_ref[...]
+    multiply(table_ref, slots_ref, even_ref, odd_ref, sum_ref)
+    finish(mask_ref, sum_ref, old_ref, next_ref, send_ref)
+
+
+def finish(mask_ref, sum_ref, old_ref, next_ref, send_ref):
     for block in range(old_ref.shape[0]):
         new = new_field(block, mask_ref, sum_ref, old_ref)
         next_ref[block] = new
@@ -264,12 +326,13 @@
 MOMENTS = ((0, 0), (0, 1), (1, 1), (1, 2), (2, 2), (2, 3))
 
 
-def last_kernel(parts, zero_slot, table_ref, mask_ref, even_ref, odd_ref, x0_ref, x1_ref, x2_ref, *refs):
-    given, (moment_ref, slots_ref, sum_ref) = refs[:parts], refs[parts:]
+def last_far(sides, table_ref, even_ref, odd_ref, mask_ref, x0_ref, x1_ref, x2_ref, near_ref, *refs):
+    given, (moment_ref, slots_ref, sum_ref) = refs[:sides], refs[sides:]
     blocks, rows, beads = x0_ref.shape
     samples = rows // 3
     gather_slots(given, slots_ref)
-    multiply(table_ref, slots_ref, even_ref, odd_ref, sum_ref, zero_slot)
+    sum_ref[...] = near_ref[...]
+    multiply(table_ref, slots_ref, even_ref, odd_ref, sum_ref)
     lanes = moment_ref.shape[2]
     lane = lax.broadcasted_iota(jnp.int32, (samples, lanes), 1)
     row = lax.broadcasted_iota(jnp.int32, (samples, lanes), 0)
@@ -366,10 +429,11 @@
     rows = 3 * samples
     shape = (blocks, rows, beads)
     devices = lax.axis_size(AXES)
-    columns = 2 if lax.axis_size("gx") == 2 else 3
-    parts_y = 2 if lax.axis_size("gy") == 2 else 3
-    zero_slot = parts_y * columns * (blocks + 2)
-    limit = 24 << 20
+    columns_x = 2 if lax.axis_size("gx") == 2 else 3
+    columns = columns_x * (2 if lax.axis_size("gy") == 2 else 3)
+    sides = 1 if lax.axis_size("gz") == 2 else 2
+    near_slots, far_slots = columns * blocks, columns * sides
+    limit = 8 << 20
 
     x0, mask, packed = call(
         pack_kernel,
@@ -386,38 +450,57 @@
             pltpu.SemaphoreType.DMA((3,)),
         ),
         4 << 20,
-    )(block_fill, noise, jnp.swapaxes(positions, 2, 3))
-    table = pair_table(pair_list, pair_count, blocks, columns, zero_slot)
-    out_field = (jax.ShapeDtypeStruct(shape, f32), jax.ShapeDtypeStruct(shape, bf16))
-    tile = jax.ShapeDtypeStruct((table.shape[1] // GROUP, 2 * beads, len(PLACES) * beads), bf16)
-
-    def scratch(rows):
-        return (pltpu.VMEM((zero_slot + 1, rows, beads), bf16), pltpu.VMEM(shape, f32))
-
-    parts = spread(packed)
-    even, odd, x1, send = call(
-        functools.partial(first_kernel, parts_y, zero_slot),
-        (tile, tile) + out_field,
-        [SMEM] + [VMEM] * (2 + parts_y),
-        scratch(rows + 16) + (pltpu.VMEM((2, beads, 128), f32),) * 2,
+    )(*[pltpu.with_memory_space_constraint(a, pltpu.HBM) for a in (block_fill, noise, jnp.swapaxes(positions, 2, 3))])
+    near_table, far_table = pair_tables(pair_list, pair_count, blocks, near_slots, far_slots)
+    field, sent = jax.ShapeDtypeStruct(shape, f32), jax.ShapeDtypeStruct(shape, bf16)
+    tile = jax.ShapeDtypeStruct((pair_list.shape[4] // GROUP + blocks, 2 * beads, len(PLACES) * beads), bf16)
+    total = pltpu.VMEM(shape, f32)
+    turned = (pltpu.VMEM((beads, 128), f32),) * 2
+    cost = pl.CostEstimate(flops=10**8, bytes_accessed=10**7, transcendentals=0)
+
+    def slots(count, rows):
+        return pltpu.VMEM((count + 1, rows, beads), bf16)
+
+    part, far, near_table, far_table = spread(packed, near_table, far_table)
+    even_n, odd_n, near = call(
+        build_near,
+        (tile, tile, field),
+        [SMEM] + [VMEM] * 2,
+        (slots(near_slots, rows + 16),) + turned,
         limit,
-    )(table, mask, x0, *parts)
-    parts = spread(send)
+        cost,
+    )(near_table, packed, part)
+    even_f, odd_f, x1, send = call(
+        functools.partial(build_far, sides),
+        (tile, tile, field, sent),
+        [SMEM] + [VMEM] * (4 + sides),
+        (slots(far_slots, rows + 16), total) + turned,
+        limit,
+    )(far_table, packed, mask, x0, near, *far)
+
+    def near_product(part):
+        return call(
+            apply_near, field, [SMEM] + [VMEM] * 3, (slots(near_slots, rows),), limit, cost
+        )(near_table, even_n, odd_n, part)
+
+    part, far = spread(send)
+    near = near_product(part)
     x2, send = call(
-        functools.partial(next_kernel, parts_y, zero_slot),
-        out_field,
-        [SMEM] + [VMEM] * (4 + parts_y),
-        scratch(rows),
+        functools.partial(apply_far, sides),
+        (field, sent),
+        [SMEM] + [VMEM] * (5 + sides),
+        (slots(far_slots, rows), total),
         limit,
-    )(table, mask, even, odd, x1, *parts)
-    parts = spread(send)
+    )(far_table, even_f, odd_f, mask, x1, near, *far)
+    part, far = spread(send)
+    near = near_product(part)
     moments = call(
-        functools.partial(last_kernel, parts_y, zero_slot),
+        functools.partial(last_far, sides),
         jax.ShapeDtypeStruct((devices, 1, 128), f32),
-        [SMEM] + [VMEM] * (6 + parts_y),
-        scratch(rows),
+        [SMEM] + [VMEM] * (7 + sides),
+        (slots(far_slots, rows), total),
         limit,
-    )(table, mask, even, odd, x0, x1, x2, *parts)
+    )(far_table, even_f, odd_f, mask, x0, x1, x2, near, *far)
     moments = lax.all_to_all(moments, AXES, 0, 0)
     return call(final_kernel, jax.ShapeDtypeStruct(noise.shape, f32), [VMEM] * 4, (), 4 << 20)(moments, x0, x1, x2)
 

time: 77.7 us -> 68.8 us (0.89)
  Pallas kernels: 5.97 us -> 13.2 us
  starting transfers between devices: 37.4 us -> 32.2 us
  blocking collectives: 18.5 us -> 14.3 us
  local copies, waits for them, and re-layouts: 2.16 us -> 0.06 us
  waiting for transfers between devices: 9.34 us -> 7.57 us
  other arithmetic: 1.78 us -> 0.15 us
  between operations: 2.15 us -> 0.9 us
    pallas_call x3 -> x7, Pallas kernels: 4.4 us -> 11.4 us  [the longest x2 3.06 us: near_product(): call(apply_near, field, [SMEM] + [VMEM] * 3, (slots(near_slots, rows),),...]
    ppermute x9, starting transfers between devices: 33.5 us -> 28.3 us  [swaps(): got = [lax.ppermute(first, axis, matching(count, 0))]]
    all_to_all x1, blocking collectives: 18.5 us -> 14.3 us  [body(): moments = lax.all_to_all(moments, AXES, 0, 0)]
    unnamed x6 -> x2, local copies, waits for them, and re-layouts: 2.08 us -> 0.02 us
    ppermute x9, waiting for transfers between devices: 9.33 us -> 7.53 us  [swaps(): got = [lax.ppermute(first, axis, matching(count, 0))]]
    reduce_sum x3 -> x0, other arithmetic: 1.62 us -> none  [the longest x1 1.4 us: pair_table(): jnp.sum(jnp.where(mine, 1, 0)) + GROUP - 1]
  transfers between devices with their start and end apart: 15 -> 15, of which waited for: 8 -> 5; matrix products, arithmetic and copies ran while one was open for 2% -> 0% of each run, Pallas kernels for 0% -> 12%
where the time goes in v3:
time: 68.8 us; the launch traced here: 68.4 us
  starting transfers between devices  32.2 us (47%)
  blocking collectives  14.3 us (21%)
  Pallas kernels  13.2 us (19%)
  waiting for transfers between devices  7.57 us (11%)
  between operations  0.9 us (1%)
    ppermute x9, starting transfers between devices, swaps(): got = [lax.ppermute(first, axis, matching(count, 0))]  28.3 us
    all_to_all x1, blocking collectives, body(): moments = lax.all_to_all(moments, AXES, 0, 0)  14.3 us
    ppermute x9, waiting for transfers between devices, swaps(): got = [lax.ppermute(first, axis, matching(count, 0))]  7.53 us
    ppermute x6, starting transfers between devices, swaps(): got.append(lax.ppermute(second, axis, matching(count, 1)))  3.92 us
    pallas_call x2, Pallas kernels, near_product(): call(apply_near, field, [SMEM] + [VMEM] * 3, (slots(near_slots, rows),),...  3.06 us
    pallas_call x1, Pallas kernels, body(): call(build_near, (tile, tile, field), [SMEM] + [VMEM] * 2, (slots(near_sl...  3.04 us
    pallas_call x1, Pallas kernels, pair_tables(): pl.pallas_call(functools.partial(table_kernel, sizes, (near_slots, far_sl...  2.22 us
    pallas_call x1, Pallas kernels, body(): call(functools.partial(build_far, sides), (tile, tile, field, sent), [SME...  1.39 us
  transfers between devices with their start and end apart: 15, of which 5 were waited for; matrix products, arithmetic and copies ran while one was open for 0% of the time, Pallas kernels for 12%

profile of v3, /device:TPU:0, one launch (start us, length us, event | category | flops | bytes accessed | tf_op | source)
XLA Modules:
  0.0 68.4 jit_solution(1047151469832391234)
XLA Ops:
  0.0 0.8 %shard_map.55 = (f32[2,24,128]{2,1,0:T(8,128)S(1)}, f32[2,8,128]{2,1,0:T(8,128)S(1)}, bf16[2,40,128]{2,1,0:T(8,128)(2,1)S(1)}) custom-call(s32[1,1,2]{2,1,0:T(1,128)} %fill_hbm.1, f32[1,1,2,8,384]{4,3,2,1,0:T(8,128)} %noise_hbm.1, f32[1,1,3,2,128]{4,3,2,1,0:T(2,128)} %bitcast.35), custom_call_target="tpu_custom_call" | custom-call | tf_op jit(solution)/shard_map/pallas_call | solution.py:438
  0.8 3.0 %collective-permute-start = (bf16[2,40,128]{2,1,0:T(8,128)(2,1)S(1)}, bf16[2,40,128]{2,1,0:T(8,128)(2,1)S(1)}, u32[]{:S(2)}, u32[]{:S(2)}) collective-permute-start(bf16[2,40,128]{2,1,0:T(8,128)(2,1)S(1)} %get-tuple-element.22.own_ref), channel_id=1, source_target_pairs={{0,16},{16,0},{1,17},{17,1},{2,18},{18,2},{3,19},{19,3},{4,20},{20... | collective-permute-start | bytes 61448 | tf_op jit(solution)/shard_map/ppermute | solution.py:37
  3.8 0.1 pad_add_fusion.odd_ref
  4.6 2.2 %shard_map.56 = (s32[2,96]{1,0:T(2,128)S(1)}, s32[2,96]{1,0:T(2,128)S(1)}) custom-call(s32[3]{0:T(128)S(1)} %pad_add_fusion.odd_ref, s32[1,1,1]{2,1,0:T(1,128)S(6)} %copy.11.count_ref, s32[1,1,3,1,54]{4,3,2,1,0:T(1,128)} %bitcast.36), custom_call_target="tpu_custom_call" | custom-call | flops 1000000 | bytes 1000000 | tf_op jit(solution)/shard_map/pallas_call | solution.py:108
  6.8 0.0 collective-permute-done
  6.8 0.1 collective-permute-start.1
  6.9 0.7 collective-permute-start.2
  7.6 0.5 collective-permute-done.1
  8.1 0.0 collective-permute-done.2
  8.1 1.6 %collective-permute-start.3 = (bf16[6,40,128]{2,1,0:T(8,128)(2,1)S(1)}, bf16[6,40,128]{2,1,0:T(8,128)(2,1)S(1)}, u32[]{:S(2)}, u32[]{:S(2)}) collective-permute-start(bf16[6,40,128]{2,1,0:T(8,128)(2,1)S(1)} %get-tuple-element.40), channel_id=1, source_target_pairs={{0,1},{1,0},{2,3},{3,2},{4,5},{5,4},{6,7},{7,6},{8,9},{9,8},{10,11... | collective-permute-start | bytes 184328 | tf_op jit(solution)/shard_map/ppermute | solution.py:37
  9.7 0.7 collective-permute-start.4
  10.4 3.0 %shard_map.57 = (bf16[15,256,768]{2,1,0:T(8,128)(2,1)S(1)}, bf16[15,256,768]{2,1,0:T(8,128)(2,1)S(1)}, f32[2,24,128]{2,1,0:T(8,128)S(1)}) custom-call(s32[2,96]{1,0:T(2,128)S(1)} %get-tuple-element.28.table_ref, bf16[2,40,128]{2,1,0:T(8,128)(2,1)S(1)} %get-tuple-element.22.own_ref, bf16[12,40,128]{2,1,0:T(8,128)(2,1)S(1)} %bitcast.28), custom_call_target="tpu_custom_call" | custom-call | flops 100000000 | bytes 10000000 | tf_op jit(solution)/shard_map/pallas_call | solution.py:465
  13.5 0.0 collective-permute-done.3.refs_0_
  13.5 0.0 collective-permute-done.4.refs_1_
  13.5 1.4 %shard_map.58 = (bf16[15,256,768]{2,1,0:T(8,128)(2,1)S(1)}, bf16[15,256,768]{2,1,0:T(8,128)(2,1)S(1)}, f32[2,24,128]{2,1,0:T(8,128)S(1)}, bf16[2,24,128]{2,1,0:T(8,128)(2,1)S(1)}) custom-call(s32[2,96]{1,0:T(2,128)S(1)} %get-tuple-element.25.table_ref, bf16[2,40,128]{2,1,0:T(8,128)(2,1)S(1)} %get-tuple-element.22.own_ref, ...), custom_call_target="tpu_custom_call" | custom-call | tf_op jit(solution)/shard_map/pallas_call | solution.py:473
  14.9 1.2 %collective-permute-start.5 = (bf16[2,24,128]{2,1,0:T(8,128)(2,1)S(1)}, bf16[2,24,128]{2,1,0:T(8,128)(2,1)S(1)}, u32[]{:S(2)}, u32[]{:S(2)}) collective-permute-start(bf16[2,24,128]{2,1,0:T(8,128)(2,1)S(1)} %get-tuple-element.36), channel_id=1, source_target_pairs={{0,16},{16,0},{1,17},{17,1},{2,18},{18,2},{3,19},{19,3},{4,20},{20... | collective-permute-start | bytes 36872 | tf_op jit(solution)/shard_map/ppermute | solution.py:37
  16.1 2.6 %collective-permute-done.5 = bf16[2,24,128]{2,1,0:T(8,128)(2,1)S(1)} collective-permute-done((bf16[2,24,128]{2,1,0:T(8,128)(2,1)S(1)}, bf16[2,24,128]{2,1,0:T(8,128)(2,1)S(1)}, u32[]{:S(2)}, u32[]{:S(2)}) %collective-permute-start.5) | collective-permute-done | bytes 12320 | tf_op jit(solution)/shard_map/ppermute | solution.py:37
  18.7 0.7 collective-permute-start.7
  19.3 8.8 %collective-permute-start.6 = (bf16[2,2,24,128]{3,2,0,1:T(8,128)(2,1)S(1)}, bf16[2,2,24,128]{3,2,0,1:T(8,128)(2,1)S(1)}, u32[]{:S(2)}, u32[]{:S(2)}) collective-permute-start(bf16[2,2,24,128]{3,2,0,1:T(8,128)(2,1)S(1)} %pad_maximum_fusion.3), channel_id=1, source_target_pairs={{0,4},{4,0},{8,12},{12,8},{1,5},{5,1},{9,13},{13,9},{2,6},{6,2},{1... | collective-permute-start | bytes 73736 | tf_op jit(solution)/shard_map/ppermute | solution.py:37
  28.1 0.0 collective-permute-done.7
  28.1 0.8 %collective-permute-done.6 = bf16[2,2,24,128]{3,2,0,1:T(8,128)(2,1)S(1)} collective-permute-done((bf16[2,2,24,128]{3,2,0,1:T(8,128)(2,1)S(1)}, bf16[2,2,24,128]{3,2,0,1:T(8,128)(2,1)S(1)}, u32[]{:S(2)}, u32[]{:S(2)}) %collective-permute-start.6) | collective-permute-done | bytes 24608 | tf_op jit(solution)/shard_map/ppermute | solution.py:37
  29.0 4.6 %collective-permute-start.8 = (bf16[6,24,128]{2,1,0:T(8,128)(2,1)S(1)}, bf16[6,24,128]{2,1,0:T(8,128)(2,1)S(1)}, u32[]{:S(2)}, u32[]{:S(2)}) collective-permute-start(bf16[6,24,128]{2,1,0:T(8,128)(2,1)S(1)} %get-tuple-element.44), channel_id=1, source_target_pairs={{0,1},{1,0},{2,3},{3,2},{4,5},{5,4},{6,7},{7,6},{8,9},{9,8},{10,11... | collective-permute-start | bytes 110600 | tf_op jit(solution)/shard_map/ppermute | solution.py:37
  33.5 0.7 collective-permute-start.9
  34.2 1.5 %shard_map.59.near_ref = f32[2,24,128]{2,1,0:T(8,128)S(1)} custom-call(s32[2,96]{1,0:T(2,128)S(1)} %get-tuple-element.28.table_ref, bf16[15,256,768]{2,1,0:T(8,128)(2,1)S(1)} %get-tuple-element.34.even_ref, bf16[15,256,768]{2,1,0:T(8,128)(2,1)S(1)} %get-tuple-element.35.odd_ref, bf16[12,24,128]{2,1,0:T(8,128)(2,1)S(1)} %bitcast.27), custom_call_target="tpu_custom_call" | custom-call | flops 100000000 | bytes 10000000 | tf_op jit(solution)/shard_map/pallas_call | solution.py:482
  35.8 0.0 collective-permute-done.8.refs_0_
  35.8 0.0 collective-permute-done.9.refs_1_
  35.8 0.8 %shard_map.60 = (f32[2,24,128]{2,1,0:T(8,128)S(1)}, bf16[2,24,128]{2,1,0:T(8,128)(2,1)S(1)}) custom-call(s32[2,96]{1,0:T(2,128)S(1)} %get-tuple-element.25.table_ref, bf16[15,256,768]{2,1,0:T(8,128)(2,1)S(1)} %get-tuple-element.31.even_ref, bf16[15,256,768]{2,1,0:T(8,128)(2,1)S(1)} %get-tuple-element.32.odd_ref, ...), custom_call_target="tpu_custom_call" | custom-call | tf_op jit(solution)/shard_map/pallas_call | solution.py:488
  36.6 1.1 %collective-permute-start.10 = (bf16[2,24,128]{2,1,0:T(8,128)(2,1)S(1)}, bf16[2,24,128]{2,1,0:T(8,128)(2,1)S(1)}, u32[]{:S(2)}, u32[]{:S(2)}) collective-permute-start(bf16[2,24,128]{2,1,0:T(8,128)(2,1)S(1)} %get-tuple-element.38), channel_id=1, source_target_pairs={{0,16},{16,0},{1,17},{17,1},{2,18},{18,2},{3,19},{19,3},{4,20},{20... | collective-permute-start | bytes 36872 | tf_op jit(solution)/shard_map/ppermute | solution.py:37
  37.7 2.7 %collective-permute-done.10 = bf16[2,24,128]{2,1,0:T(8,128)(2,1)S(1)} collective-permute-done((bf16[2,24,128]{2,1,0:T(8,128)(2,1)S(1)}, bf16[2,24,128]{2,1,0:T(8,128)(2,1)S(1)}, u32[]{:S(2)}, u32[]{:S(2)}) %collective-permute-start.10) | collective-permute-done | bytes 12320 | tf_op jit(solution)/shard_map/ppermute | solution.py:37
  40.4 0.7 collective-permute-start.12
  41.0 4.1 %collective-permute-start.11 = (bf16[2,2,24,128]{3,2,0,1:T(8,128)(2,1)S(1)}, bf16[2,2,24,128]{3,2,0,1:T(8,128)(2,1)S(1)}, u32[]{:S(2)}, u32[]{:S(2)}) collective-permute-start(bf16[2,2,24,128]{3,2,0,1:T(8,128)(2,1)S(1)} %pad_maximum_fusion.4), channel_id=1, source_target_pairs={{0,4},{4,0},{8,12},{12,8},{1,5},{5,1},{9,13},{13,9},{2,6},{6,2},{1... | collective-permute-start | bytes 73736 | tf_op jit(solution)/shard_map/ppermute | solution.py:37
  45.1 0.0 collective-permute-done.12
  45.2 0.8 %collective-permute-done.11 = bf16[2,2,24,128]{3,2,0,1:T(8,128)(2,1)S(1)} collective-permute-done((bf16[2,2,24,128]{3,2,0,1:T(8,128)(2,1)S(1)}, bf16[2,2,24,128]{3,2,0,1:T(8,128)(2,1)S(1)}, u32[]{:S(2)}, u32[]{:S(2)}) %collective-permute-start.11) | collective-permute-done | bytes 24608 | tf_op jit(solution)/shard_map/ppermute | solution.py:37
  46.0 3.9 %collective-permute-start.13 = (bf16[6,24,128]{2,1,0:T(8,128)(2,1)S(1)}, bf16[6,24,128]{2,1,0:T(8,128)(2,1)S(1)}, u32[]{:S(2)}, u32[]{:S(2)}) collective-permute-start(bf16[6,24,128]{2,1,0:T(8,128)(2,1)S(1)} %get-tuple-element.42), channel_id=1, source_target_pairs={{0,1},{1,0},{2,3},{3,2},{4,5},{5,4},{6,7},{7,6},{8,9},{9,8},{10,11... | collective-permute-start | bytes 110600 | tf_op jit(solution)/shard_map/ppermute | solution.py:37
  50.0 0.7 collective-permute-start.14
  50.6 1.5 %shard_map.61.near_ref = f32[2,24,128]{2,1,0:T(8,128)S(1)} custom-call(s32[2,96]{1,0:T(2,128)S(1)} %get-tuple-element.28.table_ref, bf16[15,256,768]{2,1,0:T(8,128)(2,1)S(1)} %get-tuple-element.34.even_ref, bf16[15,256,768]{2,1,0:T(8,128)(2,1)S(1)} %get-tuple-element.35.odd_ref, bf16[12,24,128]{2,1,0:T(8,128)(2,1)S(1)} %bitcast.26), custom_call_target="tpu_custom_call" | custom-call | flops 100000000 | bytes 10000000 | tf_op jit(solution)/shard_map/pallas_call | solution.py:482
  52.2 0.0 collective-permute-done.13.refs_0_
  52.2 0.0 collective-permute-done.14.refs_1_
  52.2 0.9 %shard_map.62 = f32[32,1,128]{2,1,0:T(1,128)S(1)} custom-call(s32[2,96]{1,0:T(2,128)S(1)} %get-tuple-element.25.table_ref, bf16[15,256,768]{2,1,0:T(8,128)(2,1)S(1)} %get-tuple-element.31.even_ref, bf16[15,256,768]{2,1,0:T(8,128)(2,1)S(1)} %get-tuple-element.32.odd_ref, f32[2,8,128]{2,1,0:T(8,128)S(1)} %get-tuple-element.26.mask_ref, ...), custom_call_target="tpu_custom_call" | custom-call | tf_op jit(solution)/shard_map/pallas_call | solution.py:497
  53.1 14.3 %all_to_all.5.moment_ref = f32[32,1,128]{2,1,0:T(1,128)S(1)} all-to-all(f32[32,1,128]{2,1,0:T(1,128)S(1)} %shard_map.62), channel_id=1, replica_groups=mesh['gx'=2,'gy'=4,'gz'=4] {'gx','gy','gz'}, dimensions={0} | all-to-all | bytes 32768 | tf_op jit(solution)/shard_map/all_to_all | solution.py:504
  67.5 1.0 %shard_map.63 = f32[1,1,2,8,384]{4,3,2,1,0:T(8,128)} custom-call(f32[32,1,128]{2,1,0:T(1,128)S(1)} %all_to_all.5.moment_ref, f32[2,24,128]{2,1,0:T(8,128)S(1)} %get-tuple-element.27.old_ref.x0_ref, f32[2,24,128]{2,1,0:T(8,128)S(1)} %get-tuple-element.33.old_ref.x1_ref, f32[2,24,128]{2,1,0:T(8,128)S(1)} %get-tuple-element.37.x2_ref), custom_call_target="tpu_custom_call" | custom-call | tf_op jit(solution)/shard_map/pallas_call | solution.py:505
  (14 shorter events, 0.1 us)
Async XLA Ops:
  0.8 6.0 %collective-permute-start = (bf16[2,40,128]{2,1,0:T(8,128)(2,1)S(1)}, bf16[2,40,128]{2,1,0:T(8,128)(2,1)S(1)}, u32[]{:S(2)}, u32[]{:S(2)}) collective-permute-start(bf16[2,40,128]{2,1,0:T(8,128)(2,1)S(1)} %get-tuple-element.22.own_ref), channel_id=1, source_target_pairs={{0,16},{16,0},{1,17},{17,1},{2,18},{18,2},{3,19},{19,3},{4,20},{20... | collective-permute-start | bytes 61448 | tf_op jit(solution)/shard_map/ppermute | solution.py:37
  6.8 1.3 %collective-permute-start.1 = (bf16[2,2,40,128]{3,2,0,1:T(8,128)(2,1)S(1)}, bf16[2,2,40,128]{3,2,0,1:T(8,128)(2,1)S(1)}, u32[]{:S(2)}, u32[]{:S(2)}) collective-permute-start(bf16[2,2,40,128]{3,2,0,1:T(8,128)(2,1)S(1)} %pad_maximum_fusion.2), channel_id=1, source_target_pairs={{0,4},{4,0},{8,12},{12,8},{1,5},{5,1},{9,13},{13,9},{2,6},{6,2},{1... | collective-permute-start | bytes 122888 | tf_op jit(solution)/shard_map/ppermute | solution.py:37
  6.9 1.2 %collective-permute-start.2 = (bf16[2,2,40,128]{3,2,0,1:T(8,128)(2,1)S(1)}, bf16[2,2,40,128]{3,2,0,1:T(8,128)(2,1)S(1)}, u32[]{:S(2)}, u32[]{:S(2)}) collective-permute-start(bf16[2,2,40,128]{3,2,0,1:T(8,128)(2,1)S(1)} %pad_maximum_fusion.2), channel_id=1, source_target_pairs={{4,8},{8,4},{5,9},{9,5},{6,10},{10,6},{7,11},{11,7},{20,24},{24,20... | collective-permute-start | bytes 122888 | tf_op jit(solution)/shard_map/ppermute | solution.py:39
  8.1 5.3 %collective-permute-start.3 = (bf16[6,40,128]{2,1,0:T(8,128)(2,1)S(1)}, bf16[6,40,128]{2,1,0:T(8,128)(2,1)S(1)}, u32[]{:S(2)}, u32[]{:S(2)}) collective-permute-start(bf16[6,40,128]{2,1,0:T(8,128)(2,1)S(1)} %get-tuple-element.40), channel_id=1, source_target_pairs={{0,1},{1,0},{2,3},{3,2},{4,5},{5,4},{6,7},{7,6},{8,9},{9,8},{10,11... | collective-permute-start | bytes 184328 | tf_op jit(solution)/shard_map/ppermute | solution.py:37
  9.7 3.8 %collective-permute-start.4 = (bf16[6,40,128]{2,1,0:T(8,128)(2,1)S(1)}, bf16[6,40,128]{2,1,0:T(8,128)(2,1)S(1)}, u32[]{:S(2)}, u32[]{:S(2)}) collective-permute-start(bf16[6,40,128]{2,1,0:T(8,128)(2,1)S(1)} %get-tuple-element.39), channel_id=1, source_target_pairs={{1,2},{2,1},{5,6},{6,5},{9,10},{10,9},{13,14},{14,13},{17,18},{18,... | collective-permute-start | bytes 184328 | tf_op jit(solution)/shard_map/ppermute | solution.py:39
  14.9 3.8 %collective-permute-start.5 = (bf16[2,24,128]{2,1,0:T(8,128)(2,1)S(1)}, bf16[2,24,128]{2,1,0:T(8,128)(2,1)S(1)}, u32[]{:S(2)}, u32[]{:S(2)}) collective-permute-start(bf16[2,24,128]{2,1,0:T(8,128)(2,1)S(1)} %get-tuple-element.36), channel_id=1, source_target_pairs={{0,16},{16,0},{1,17},{17,1},{2,18},{18,2},{3,19},{19,3},{4,20},{20... | collective-permute-start | bytes 36872 | tf_op jit(solution)/shard_map/ppermute | solution.py:37
  18.7 9.4 %collective-permute-start.7 = (bf16[2,2,24,128]{3,2,0,1:T(8,128)(2,1)S(1)}, bf16[2,2,24,128]{3,2,0,1:T(8,128)(2,1)S(1)}, u32[]{:S(2)}, u32[]{:S(2)}) collective-permute-start(bf16[2,2,24,128]{3,2,0,1:T(8,128)(2,1)S(1)} %pad_maximum_fusion.3), channel_id=1, source_target_pairs={{4,8},{8,4},{5,9},{9,5},{6,10},{10,6},{7,11},{11,7},{20,24},{24,20... | collective-permute-start | bytes 73736 | tf_op jit(solution)/shard_map/ppermute | solution.py:39
  19.3 9.6 %collective-permute-start.6 = (bf16[2,2,24,128]{3,2,0,1:T(8,128)(2,1)S(1)}, bf16[2,2,24,128]{3,2,0,1:T(8,128)(2,1)S(1)}, u32[]{:S(2)}, u32[]{:S(2)}) collective-permute-start(bf16[2,2,24,128]{3,2,0,1:T(8,128)(2,1)S(1)} %pad_maximum_fusion.3), channel_id=1, source_target_pairs={{0,4},{4,0},{8,12},{12,8},{1,5},{5,1},{9,13},{13,9},{2,6},{6,2},{1... | collective-permute-start | bytes 73736 | tf_op jit(solution)/shard_map/ppermute | solution.py:37
  29.0 6.8 %collective-permute-start.8 = (bf16[6,24,128]{2,1,0:T(8,128)(2,1)S(1)}, bf16[6,24,128]{2,1,0:T(8,128)(2,1)S(1)}, u32[]{:S(2)}, u32[]{:S(2)}) collective-permute-start(bf16[6,24,128]{2,1,0:T(8,128)(2,1)S(1)} %get-tuple-element.44), channel_id=1, source_target_pairs={{0,1},{1,0},{2,3},{3,2},{4,5},{5,4},{6,7},{7,6},{8,9},{9,8},{10,11... | collective-permute-start | bytes 110600 | tf_op jit(solution)/shard_map/ppermute | solution.py:37
  33.5 2.2 %collective-permute-start.9 = (bf16[6,24,128]{2,1,0:T(8,128)(2,1)S(1)}, bf16[6,24,128]{2,1,0:T(8,128)(2,1)S(1)}, u32[]{:S(2)}, u32[]{:S(2)}) collective-permute-start(bf16[6,24,128]{2,1,0:T(8,128)(2,1)S(1)} %get-tuple-element.43), channel_id=1, source_target_pairs={{1,2},{2,1},{5,6},{6,5},{9,10},{10,9},{13,14},{14,13},{17,18},{18,... | collective-permute-start | bytes 110600 | tf_op jit(solution)/shard_map/ppermute | solution.py:39
  36.6 3.8 %collective-permute-start.10 = (bf16[2,24,128]{2,1,0:T(8,128)(2,1)S(1)}, bf16[2,24,128]{2,1,0:T(8,128)(2,1)S(1)}, u32[]{:S(2)}, u32[]{:S(2)}) collective-permute-start(bf16[2,24,128]{2,1,0:T(8,128)(2,1)S(1)} %get-tuple-element.38), channel_id=1, source_target_pairs={{0,16},{16,0},{1,17},{17,1},{2,18},{18,2},{3,19},{19,3},{4,20},{20... | collective-permute-start | bytes 36872 | tf_op jit(solution)/shard_map/ppermute | solution.py:37
  40.4 4.8 %collective-permute-start.12 = (bf16[2,2,24,128]{3,2,0,1:T(8,128)(2,1)S(1)}, bf16[2,2,24,128]{3,2,0,1:T(8,128)(2,1)S(1)}, u32[]{:S(2)}, u32[]{:S(2)}) collective-permute-start(bf16[2,2,24,128]{3,2,0,1:T(8,128)(2,1)S(1)} %pad_maximum_fusion.4), channel_id=1, source_target_pairs={{4,8},{8,4},{5,9},{9,5},{6,10},{10,6},{7,11},{11,7},{20,24},{24,20... | collective-permute-start | bytes 73736 | tf_op jit(solution)/shard_map/ppermute | solution.py:39
  41.0 5.0 %collective-permute-start.11 = (bf16[2,2,24,128]{3,2,0,1:T(8,128)(2,1)S(1)}, bf16[2,2,24,128]{3,2,0,1:T(8,128)(2,1)S(1)}, u32[]{:S(2)}, u32[]{:S(2)}) collective-permute-start(bf16[2,2,24,128]{3,2,0,1:T(8,128)(2,1)S(1)} %pad_maximum_fusion.4), channel_id=1, source_target_pairs={{0,4},{4,0},{8,12},{12,8},{1,5},{5,1},{9,13},{13,9},{2,6},{6,2},{1... | collective-permute-start | bytes 73736 | tf_op jit(solution)/shard_map/ppermute | solution.py:37
  46.0 6.2 %collective-permute-start.13 = (bf16[6,24,128]{2,1,0:T(8,128)(2,1)S(1)}, bf16[6,24,128]{2,1,0:T(8,128)(2,1)S(1)}, u32[]{:S(2)}, u32[]{:S(2)}) collective-permute-start(bf16[6,24,128]{2,1,0:T(8,128)(2,1)S(1)} %get-tuple-element.42), channel_id=1, source_target_pairs={{0,1},{1,0},{2,3},{3,2},{4,5},{5,4},{6,7},{7,6},{8,9},{9,8},{10,11... | collective-permute-start | bytes 110600 | tf_op jit(solution)/shard_map/ppermute | solution.py:37
  50.0 2.2 %collective-permute-start.14 = (bf16[6,24,128]{2,1,0:T(8,128)(2,1)S(1)}, bf16[6,24,128]{2,1,0:T(8,128)(2,1)S(1)}, u32[]{:S(2)}, u32[]{:S(2)}) collective-permute-start(bf16[6,24,128]{2,1,0:T(8,128)(2,1)S(1)} %get-tuple-element.41), channel_id=1, source_target_pairs={{1,2},{2,1},{5,6},{6,5},{9,10},{10,9},{13,14},{14,13},{17,18},{18,... | collective-permute-start | bytes 110600 | tf_op jit(solution)/shard_map/ppermute | solution.py:39

commit v4 on v3

v4 whole, which is shorter than its diff:
```python
import functools

import jax
import jax.numpy as jnp
from jax import lax
from jax.experimental import pallas as pl
from jax.experimental.pallas import tpu as pltpu
from jax.sharding import PartitionSpec as P

ITERS = 3
ROOT_ITERS = 12
CHUNK = 16

radius = 0.08
floor_sq = 0.0001
epsilon = 1e-06

AXES = ("gx", "gy", "gz")
VMEM = pl.BlockSpec(memory_space=pltpu.VMEM)
HBM = pl.BlockSpec(memory_space=pltpu.HBM)
SMEM = pl.BlockSpec(memory_space=pltpu.SMEM)
f32 = jnp.float32
bf16 = jnp.bfloat16
PLACES = ((0, 0), (0, 1), (0, 2), (1, 1), (1, 2), (2, 2))


def matching(count, parity):
    pairs = []
    for i in range(parity, count - 1, 2):
        pairs += [(i, i + 1), (i + 1, i)]
    return pairs


def swaps(axis, first, second):
    count = lax.axis_size(axis)
    got = [lax.ppermute(first, axis, matching(count, 0))]
    if count > 2:
        got.append(lax.ppermute(second, axis, matching(count, 1)))
    return got


def spread(field, table, stage):
    shape = (-1,) + field.shape[1:]
    columns = jnp.stack([field] + swaps("gx", field, field))
    columns, table = lax.optimization_barrier((columns, table))
    others = swaps("gy", columns, columns)
    result = stage(table, 0, [columns.reshape(shape)], None)
    odd = lax.axis_index("gz") % 2 == 1
    low = jnp.concatenate([part[:, 0] for part in [columns] + others])
    high = jnp.concatenate([part[:, field.shape[0] - 1] for part in [columns] + others])
    low, high, result = lax.optimization_barrier((jnp.where(odd, low, high), jnp.where(odd, high, low), result))
    far = swaps("gz", low, high)
    result = stage(table, 1, [part.reshape(shape) for part in others], result)
    return stage(table, 2, far, result)


def table_kernel(sizes, slots, blocks, count_ref, list_hbm, table_ref, list_ref, sem):
    copy = pltpu.make_async_copy(list_hbm, list_ref, sem)
    copy.start()
    sets = len(slots) * blocks
    segment = table_ref.shape[1] // sets
    for i in range(sets):
        table_ref[1, i] = 0
    odd = [lax.rem(lax.axis_index(axis), 2) == 1 for axis in AXES]

    def partner(axis, step):
        if sizes[axis] == 2:
            return jnp.where(step == 0, 0, 1)
        return jnp.where(step == 0, 0, jnp.where((step < 0) == odd[axis], 1, 2))

    def enter(t, carry):
        home, code = list_ref[0, 0, 0, 0, t], list_ref[0, 0, 1, 0, t]
        plane, third = (code * 57) >> 9, (code * 43) >> 7
        x, y = partner(0, plane - 1), partner(1, third - 3 * plane - 1)
        z = home + code - 3 * third - 1
        far = (z < 0) | (z >= blocks)
        width = slots[0] // blocks
        side = partner(2, jnp.where(z < 0, -1, 1)) - 1
        slot = (jnp.maximum(y - 1, 0) * width + x) * blocks + z
        slot = jnp.where(far, side * (slots[2] // (1 if sizes[2] == 2 else 2)) + y * width + x, slot)
        at = jnp.where(far, 2, jnp.minimum(y, 1)) * blocks + home
        place = table_ref[1, at]
        table_ref[1, at] = place + 1
        table_ref[0, at * segment + place] = slot
        return carry

    copy.wait()
    lax.fori_loop(0, count_ref[0, 0, 0], enter, 0)
    for stage, empty in enumerate(slots):
        for block in range(blocks):
            at = stage * blocks + block
            end = at * segment + table_ref[1, at]
            for i in range(3):
                table_ref[0, end + i] = empty


def pair_table(pair_list, pair_count, blocks, slots):
    segment = -(-(pair_list.shape[4] + 3) // 2) * 2
    sizes = [lax.axis_size(axis) for axis in AXES]
    pair_list = pltpu.with_memory_space_constraint(jnp.swapaxes(pair_list, 2, 3), pltpu.HBM)
    return pl.pallas_call(
        functools.partial(table_kernel, sizes, slots, blocks),
        out_shape=jax.ShapeDtypeStruct((2, len(slots) * blocks * segment), jnp.int32),
        in_specs=[SMEM, HBM],
        out_specs=SMEM,
        scratch_shapes=[pltpu.SMEM(pair_list.shape, jnp.int32), pltpu.SemaphoreType.DMA],
        compiler_params=pltpu.CompilerParams(vmem_limit_bytes=1 << 20),
        cost_estimate=pl.CostEstimate(flops=10**6, bytes_accessed=10**6, transcendentals=0),
    )(pair_count, pair_list)


def duos_of(table_ref, stage, blocks):
    segment = table_ref.shape[1] // (3 * blocks)
    counts = [(table_ref[1, stage * blocks + block] + 1) >> 1 for block in range(blocks)]
    ends = [sum(counts[: block + 1]) for block in range(blocks)]

    def home_of(duo):
        return sum([jnp.where(duo >= end, 1, 0) for end in ends[:-1]], 0)

    def first_of(duo):
        skip = [jnp.where(duo >= ends[i], segment - 2 * counts[i], 0) for i in range(blocks - 1)]
        return stage * blocks * segment + 2 * duo + sum(skip)

    return ends[-1], home_of, first_of


def pack_kernel(fill_hbm, noise_hbm, pos_hbm, start_ref, mask_ref, pack_ref, fill_ref, noise_ref, pos_ref, sems):
    pairs = ((fill_hbm, fill_ref), (noise_hbm, noise_ref), (pos_hbm, pos_ref))
    copies = [pltpu.make_async_copy(a, b, sems.at[i]) for i, (a, b) in enumerate(pairs)]
    for copy in copies:
        copy.start()
    for copy in copies:
        copy.wait()
    blocks, samples, width = noise_ref.shape[2:]
    beads = width // 3
    row = lax.broadcasted_iota(jnp.int32, (16, beads), 0)
    for block in range(blocks):
        mask = (lax.broadcasted_iota(jnp.int32, (8, beads), 1) < fill_ref[0, 0, block]).astype(f32)
        mask_ref[block] = mask
        noise = [noise_ref[0, 0, block, :, pl.ds(c * beads, beads)] for c in range(3)]
        start = jnp.concatenate([part * mask[:1] for part in noise], axis=0)
        start_ref[block] = start
        place = jnp.zeros((16, beads), f32)
        for c in range(3):
            pos = pos_ref[0, 0, c, pl.ds(block, 1)]
            high = pos.astype(bf16).astype(f32)
            rest = pos - high
            mid = rest.astype(bf16).astype(f32)
            for i, piece in ((0, high), (8, mid), (3, rest - mid)):
                place = jnp.where(row == i + c, piece, place)
        pack_ref[block] = jnp.concatenate([start, place], axis=0).astype(bf16)


def gather_slots(parts, slots_ref):
    count = parts[0].shape[0]
    for i, part in enumerate(parts):
        slots_ref[pl.ds(i * count, count)] = part[...]
    slots_ref[len(parts) * count] = jnp.zeros(slots_ref.shape[1:], bf16)


def position_of(slots_ref, slot, field_rows):
    rows = slots_ref[slot].astype(f32)[field_rows:]
    return rows[:8] + rows[8:] + pltpu.roll(rows[:8], 5, 0)


def turn_positions(slots_ref, first, second, field_rows):
    first = position_of(slots_ref, first, field_rows)
    second = pltpu.roll(position_of(slots_ref, second, field_rows), 3, 0)
    row = lax.broadcasted_iota(jnp.int32, first.shape, 0)
    return jnp.transpose(jnp.where(row < 3, first, second))


def make_tile(home, turned_ref, tiles_ref, pair, half):
    beads = home.shape[1]
    base = half * beads
    for first in range(0, beads, CHUNK):
        turned = turned_ref[pl.ds(first, CHUNK)]
        d = [turned[:, 3 * half + c : 3 * half + c + 1] - home[c : c + 1] for c in range(3)]
        dist_sq = d[0] * d[0] + d[1] * d[1] + d[2] * d[2]
        root = lax.rsqrt(jnp.maximum(dist_sq, 1e-30))
        distance = dist_sq * root
        inv_root = jnp.minimum(root, floor_sq**-0.5)
        inverse_sq = inv_root * inv_root
        far = (0.75 * radius) * inv_root
        far_two = (2.0 * radius * radius) * (far * inverse_sq)
        apart = dist_sq >= 4.0 * radius * radius
        isotropic = jnp.where(apart, far + far_two * (1.0 / 3.0), 1.0 - (9.0 / 32.0 / radius) * distance)
        dyadic = jnp.where(apart, far - far_two, (3.0 / 32.0 / radius) * distance) * inverse_sq
        scaled = [dyadic * d[c] for c in range(3)]
        entries = []
        for c, e in PLACES:
            entry = scaled[c] * d[e]
            entries.append(entry + isotropic if c == e else entry)
        tiles_ref[pair, pl.ds(base + first, CHUNK)] = jnp.concatenate(entries, axis=1).astype(bf16)


def add_product(sum_ref, home, product):
    rows, beads = sum_ref.shape[1:]
    samples = rows // 3
    out = [0.0] * 3
    for k, (c, e) in enumerate(PLACES):
        column = product[:, k * beads : (k + 1) * beads]
        out[c] = out[c] + column[e * samples : (e + 1) * samples]
        if c != e:
            out[e] = out[e] + column[c * samples : (c + 1) * samples]
    sum_ref[home] = sum_ref[home] + jnp.concatenate(out, axis=0)


def field_of(table_ref, slots_ref, first, rows):
    return jnp.concatenate([slots_ref[table_ref[0, first + i]][:rows] for i in range(2)], axis=1)


def product(field, tile):
    return jnp.dot(field, tile, preferred_element_type=f32)


def multiply(table_ref, stage, slots_ref, even_ref, odd_ref, sum_ref):
    blocks, rows = sum_ref.shape[:2]
    count, home_of, first_of = duos_of(table_ref, stage, blocks)

    def both(turn, carry):
        duo = 2 * turn
        odd = jnp.where(duo + 1 < count, turn, 0)
        first = product(field_of(table_ref, slots_ref, first_of(duo), rows), even_ref[turn])
        second = product(field_of(table_ref, slots_ref, first_of(duo + 1), rows), odd_ref[odd])
        add_product(sum_ref, home_of(duo), first)
        add_product(sum_ref, jnp.minimum(home_of(duo + 1), blocks - 1), second)
        return carry

    lax.fori_loop(0, (count + 1) >> 1, both, 0)


def build(table_ref, stage, own_ref, slots_ref, even_ref, odd_ref, sum_ref, turn_even, turn_odd):
    blocks, rows = sum_ref.shape[:2]
    count, home_of, first_of = duos_of(table_ref, stage, blocks)
    odd_ref[0] = jnp.zeros(odd_ref.shape[1:], bf16)

    def prepare(duo, columns_ref):
        first = first_of(duo)
        columns_ref[:, :8] = turn_positions(slots_ref, table_ref[0, first], table_ref[0, first + 1], rows)

    def consume(duo, tile, index):
        field = field_of(table_ref, slots_ref, first_of(duo), rows)
        add_product(sum_ref, jnp.minimum(home_of(duo), blocks - 1), product(field, tile[index]))

    def make(duo, columns_ref, tile, index):
        place = position_of(own_ref, home_of(duo), rows)
        for i in range(2):
            make_tile(place, columns_ref, tile, index, i)

    def both(turn, spare):
        duo = 2 * turn
        full = duo + 1 < count
        make(duo, turn_even, even_ref, turn)
        prepare(duo + 1, turn_odd)
        consume(jnp.where(turn == 0, count, duo - 1), odd_ref, spare)

        @pl.when(full)
        def _():
            make(duo + 1, turn_odd, odd_ref, turn)
            prepare(duo + 2, turn_even)
            consume(duo, even_ref, turn)

        @pl.when(jnp.logical_not(full))
        def _():
            consume(duo, even_ref, turn)

        return jnp.where(full, turn, spare)

    prepare(0, turn_even)
    spare = lax.fori_loop(0, (count + 1) >> 1, both, 0)
    consume(jnp.where(count % 2 == 0, jnp.maximum(count - 1, 0), count), odd_ref, spare)


def new_field(block, mask_ref, sum_ref, old_ref):
    return sum_ref[block] * mask_ref[block, :1] - old_ref[block]


def stage_kernel(stage, building, moments, *refs):
    refs = list(refs)
    table_ref, own_ref = refs.pop(0), refs.pop(0) if building else None
    tiles = None if building else (refs.pop(0), refs.pop(0))
    before_ref = refs.pop(0) if stage else None
    last = stage == 2
    mask_ref = refs.pop(0) if last else None
    old = [refs.pop(0) for _ in range(3 if moments else 1)] if last else []
    columns = [refs.pop(), refs.pop()] if building else []
    sum_ref = refs.pop() if last else None
    slots_ref = refs.pop()
    outs = [refs.pop() for _ in range(1 if moments or not last else 2)][::-1]
    if building:
        tiles = [refs.pop(), refs.pop()][::-1]
    gather_slots(refs, slots_ref)
    if not last:
        sum_ref = outs[0]
    sum_ref[...] = before_ref[...] if stage else jnp.zeros_like(sum_ref)
    if building:
        build(table_ref, stage, own_ref, slots_ref, *tiles, sum_ref, *columns)
    else:
        multiply(table_ref, stage, slots_ref, *tiles, sum_ref)
    if moments:
        take_moments(mask_ref, sum_ref, *old, outs[0])
    elif last:
        for block in range(sum_ref.shape[0]):
            new = new_field(block, mask_ref, sum_ref, old[0])
            outs[0][block] = new
            outs[1][block] = new.astype(bf16)


MOMENTS = ((0, 0), (0, 1), (1, 1), (1, 2), (2, 2), (2, 3))


def take_moments(mask_ref, sum_ref, x0_ref, x1_ref, x2_ref, moment_ref):
    blocks, rows, beads = x0_ref.shape
    samples = rows // 3
    lanes = moment_ref.shape[2]
    lane = lax.broadcasted_iota(jnp.int32, (samples, lanes), 1)
    row = lax.broadcasted_iota(jnp.int32, (samples, lanes), 0)
    sums = [0.0] * len(MOMENTS)
    for block in range(blocks):
        x = [x0_ref[block], x1_ref[block], x2_ref[block]]
        x.append(new_field(block, mask_ref, sum_ref, x2_ref))
        for k, (i, j) in enumerate(MOMENTS):
            both = x[i] * x[j]
            sums[k] = sums[k] + both[:samples] + both[samples : 2 * samples] + both[2 * samples :]
    grid = jnp.zeros((samples, lanes), f32)
    for k, value in enumerate(sums):
        value = jnp.sum(value, axis=1, keepdims=True)
        grid = jnp.where(lane == row + k * samples, value, grid)
    line = jnp.sum(grid, axis=0, keepdims=True)
    moment_ref[...] = jnp.broadcast_to(line[None], moment_ref.shape)


def inverse_symmetric(m):
    a, b, c, d, e, f = m
    ca, cb, cc = d * f - e * e, c * e - b * f, b * e - c * d
    scale = 1.0 / (a * ca + b * cb + c * cc)
    return (ca * scale, cb * scale, cc * scale, (a * f - c * c) * scale, (b * c - a * e) * scale, (a * d - b * b) * scale)


def final_kernel(moment_ref, x0_ref, x1_ref, x2_ref, out_ref):
    blocks, rows, beads = x0_ref.shape
    samples = rows // 3
    lanes = moment_ref.shape[2]
    lane = lax.broadcasted_iota(jnp.int32, (samples, lanes), 1)
    row = lax.broadcasted_iota(jnp.int32, (samples, lanes), 0)
    line = jnp.broadcast_to(jnp.sum(moment_ref[...], axis=0), (samples, lanes))
    m00, m01, m11, m12, m22, m23 = [
        jnp.broadcast_to(
            jnp.sum(jnp.where(lane == row + k * samples, line, 0.0), axis=1, keepdims=True), (samples, lanes)
        )
        for k in range(len(MOMENTS))
    ]
    norm_sq = m00 + epsilon
    start_norm = jnp.sqrt(norm_sq)
    inv_sq = 1.0 / norm_sq
    alpha1 = (m00 + m01) * inv_sq
    c = 1.0 - alpha1
    res_sq = (m11 + c * (2.0 * m01 + c * m00)) * inv_sq
    beta1 = jnp.sqrt(jnp.maximum(res_sq, 0.0) + epsilon)
    k2 = 1.0 / (start_norm * beta1)
    n11 = m11 + c * (2.0 * m01 + c * m00)
    n12 = m12 + c * (2.0 * m11 + c * m01)
    alpha2 = k2 * k2 * (n11 + n12)
    f1 = 1.0 + c - alpha2
    f0 = c - alpha2 * c - beta1 * beta1
    n22 = m22 + f1 * (2.0 * m12 + f1 * m11) + f0 * (2.0 * (m11 + f1 * m01) + f0 * m00)
    beta2 = jnp.sqrt(jnp.maximum(k2 * k2 * n22, 0.0) + epsilon)
    k3 = k2 / beta2
    n23 = m23 + f1 * (2.0 * m22 + f1 * m12) + f0 * (2.0 * (m12 + f1 * m11) + f0 * m01)
    alpha3 = k3 * k3 * (jnp.maximum(n22, 0.0) + n23)

    scale = (alpha1 + alpha2 + alpha3) / 3.0
    inv_scale = 1.0 / scale
    zero, one = jnp.zeros_like(scale), jnp.ones_like(scale)
    y = (alpha1 * inv_scale, beta1 * inv_scale, zero, alpha2 * inv_scale, beta2 * inv_scale, alpha3 * inv_scale)
    z = (one, zero, zero, one, zero, one)
    for _ in range(ROOT_ITERS):
        inv_z, inv_y = inverse_symmetric(z), inverse_symmetric(y)
        y = tuple(0.5 * (p + q) for p, q in zip(y, inv_z))
        z = tuple(0.5 * (p + q) for p, q in zip(z, inv_y))
    root_scale = jnp.sqrt(scale)
    r1, r2, r3 = root_scale * y[0], root_scale * y[1], root_scale * y[2]
    w2, w3 = start_norm * r2 * k2, start_norm * r3 * k3
    p0 = r1 + w2 * c + w3 * f0
    p1 = w2 + w3 * f1
    for block in range(blocks):
        for c in range(3):
            at = pl.ds(c * samples, samples)
            out = p0 * x0_ref[block, at] + p1 * x1_ref[block, at] + w3 * x2_ref[block, at]
            out_ref[0, 0, block, :, pl.ds(c * beads, beads)] = out


def call(kernel, outs, in_specs, scratch=(), limit=None, cost=None):
    return pl.pallas_call(
        kernel,
        out_shape=outs,
        in_specs=in_specs,
        out_specs=jax.tree.map(lambda _: VMEM, outs),
        scratch_shapes=list(scratch),
        compiler_params=pltpu.CompilerParams(vmem_limit_bytes=limit),
        cost_estimate=cost,
    )


def body(positions, block_fill, noise, pair_list, pair_count):
    blocks, beads = positions.shape[2], positions.shape[4]
    samples = noise.shape[3]
    rows = 3 * samples
    shape = (blocks, rows, beads)
    devices = lax.axis_size(AXES)
    columns = 2 if lax.axis_size("gx") == 2 else 3
    others = 1 if lax.axis_size("gy") == 2 else 2
    sides = 1 if lax.axis_size("gz") == 2 else 2
    slots = (columns * blocks, others * columns * blocks, sides * (1 + others) * columns)
    limit = 8 << 20

    x0, mask, packed = call(
        pack_kernel,
        (
            jax.ShapeDtypeStruct(shape, f32),
            jax.ShapeDtypeStruct((blocks, 8, beads), f32),
            jax.ShapeDtypeStruct((blocks, rows + 16, beads), bf16),
        ),
        [HBM] * 3,
        (
            pltpu.SMEM(block_fill.shape, jnp.int32),
            pltpu.VMEM(noise.shape, f32),
            pltpu.VMEM((1, 1, 3, blocks, beads), f32),
            pltpu.SemaphoreType.DMA((3,)),
        ),
        4 << 20,
    )(*[pltpu.with_memory_space_constraint(a, pltpu.HBM) for a in (block_fill, noise, jnp.swapaxes(positions, 2, 3))])
    table = pair_table(pair_list, pair_count, blocks, slots)
    field, sent = jax.ShapeDtypeStruct(shape, f32), jax.ShapeDtypeStruct(shape, bf16)
    capacity = (pair_list.shape[4] + blocks) // 4 + 1
    tile = jax.ShapeDtypeStruct((capacity, 2 * beads, len(PLACES) * beads), bf16)
    total = pltpu.VMEM(shape, f32)
    moment = jax.ShapeDtypeStruct((devices, 1, 128), f32)
    cost = pl.CostEstimate(flops=10**8, bytes_accessed=10**7, transcendentals=0)

    def apply(vector, tiles, olds):
        building, moments = not tiles, len(olds) == 3

        def stage(table, index, given, result):
            last = index == 2
            outs = (moment,) if last and moments else (field, sent) if last else (field,)
            scratch = [pltpu.VMEM((slots[index] + 1,) + given[0].shape[1:], bf16)]
            scratch += [total] * last + [pltpu.VMEM((beads, 128), f32)] * (2 * building)
            args = [packed] if building else list(tiles[index])
            args += ([result] if index else []) + ([mask] + olds if last else []) + given
            result = call(
                functools.partial(stage_kernel, index, building, last and moments),
                (tile, tile) * building + outs,
                [SMEM] + [VMEM] * len(args),
                scratch,
                limit,
                None if last else cost,
            )(table, *args)
            if building:
                tiles.append(result[:2])
                result = result[2:]
            return result if last and not moments else result[0]

        return spread(vector, table, stage)

    tiles = []
    x1, send = apply(packed, tiles, [x0])
    x2, send = apply(send, tiles, [x1])
    moments = apply(send, tiles, [x0, x1, x2])
    moments = lax.all_to_all(moments, AXES, 0, 0)
    return call(final_kernel, jax.ShapeDtypeStruct(noise.shape, f32), [VMEM] * 4, (), 4 << 20)(moments, x0, x1, x2)


def solution(mesh):
    block = P("gx", "gy", "gz", None, None)
    cell = P("gx", "gy", "gz")
    return jax.shard_map(
        body, mesh=mesh, in_specs=(block, cell, block, block, cell), out_specs=block, check_vma=False
    )
```

time: 68.8 us -> 67.5 us (0.981)
    pallas_call x7 -> x10, Pallas kernels: 11.4 us -> 10.9 us  [the longest x9 9.25 us: stage(): call(functools.partial(stage_kernel, index, building, last and moments),...]
  transfers between devices with their start and end apart: 15 -> 15, of which waited for: 5 -> 5; matrix products, arithmetic and copies ran while one was open for 0% -> 0% of each run, Pallas kernels for 12% -> 11%
where the time goes in v4:
time: 67.5 us; the launch traced here: 67.2 us
  starting transfers between devices  32.2 us (48%)
  blocking collectives  14 us (21%)
  Pallas kernels  12.6 us (19%)
  waiting for transfers between devices  7.07 us (10%)
  between operations  1.03 us (2%)
    ppermute x9, starting transfers between devices, swaps(): got = [lax.ppermute(first, axis, matching(count, 0))]  28.3 us
    all_to_all x1, blocking collectives, body(): moments = lax.all_to_all(moments, AXES, 0, 0)  14 us
    pallas_call x9, Pallas kernels, stage(): call(functools.partial(stage_kernel, index, building, last and moments),...  9.25 us
    ppermute x9, waiting for transfers between devices, swaps(): got = [lax.ppermute(first, axis, matching(count, 0))]  7 us
    ppermute x6, starting transfers between devices, swaps(): got.append(lax.ppermute(second, axis, matching(count, 1)))  3.92 us
    pallas_call x1, Pallas kernels, pair_table(): pl.pallas_call(functools.partial(table_kernel, sizes, slots, blocks), out...  1.63 us
  transfers between devices with their start and end apart: 15, of which 5 were waited for; matrix products, arithmetic and copies ran while one was open for 0% of the time, Pallas kernels for 11%

profile of v4, /device:TPU:0, one launch (start us, length us, event | category | flops | bytes accessed | tf_op | source)
XLA Modules:
  0.0 67.2 jit_solution(9487216039579856833)
XLA Ops:
  0.0 0.8 %shard_map.55 = (f32[2,24,128]{2,1,0:T(8,128)S(1)}, f32[2,8,128]{2,1,0:T(8,128)S(1)}, bf16[2,40,128]{2,1,0:T(8,128)(2,1)S(1)}) custom-call(s32[1,1,2]{2,1,0:T(1,128)} %fill_hbm.1, f32[1,1,2,8,384]{4,3,2,1,0:T(8,128)} %noise_hbm.1, f32[1,1,3,2,128]{4,3,2,1,0:T(2,128)} %bitcast.68), custom_call_target="tpu_custom_call" | custom-call | tf_op jit(solution)/shard_map/pallas_call | solution.py:418
  0.8 3.0 %collective-permute-start = (bf16[2,40,128]{2,1,0:T(8,128)(2,1)S(1)}, bf16[2,40,128]{2,1,0:T(8,128)(2,1)S(1)}, u32[]{:S(2)}, u32[]{:S(2)}) collective-permute-start(bf16[2,40,128]{2,1,0:T(8,128)(2,1)S(1)} %get-tuple-element.35.refs_1_), channel_id=1, source_target_pairs={{0,16},{16,0},{1,17},{17,1},{2,18},{18,2},{3,19},{19,3},{4,20},{20... | collective-permute-start | bytes 61448 | tf_op jit(solution)/shard_map/ppermute | solution.py:36
  4.5 1.6 %shard_map.56.refs_0_ = s32[2,348]{1,0:T(2,128)S(1)} custom-call(s32[1,1,1]{2,1,0:T(1,128)S(6)} %copy.15.count_ref, s32[1,1,3,1,54]{4,3,2,1,0:T(1,128)} %bitcast.69), custom_call_target="tpu_custom_call" | custom-call | flops 1000000 | bytes 1000000 | tf_op jit(solution)/shard_map/pallas_call | solution.py:101
  6.1 0.0 collective-permute-done
  6.1 0.7 collective-permute-start.2
  6.8 3.2 %collective-permute-start.1 = (bf16[2,2,40,128]{3,2,0,1:T(8,128)(2,1)S(1)}, bf16[2,2,40,128]{3,2,0,1:T(8,128)(2,1)S(1)}, u32[]{:S(2)}, u32[]{:S(2)}) collective-permute-start(bf16[2,2,40,128]{3,2,0,1:T(8,128)(2,1)S(1)} %pad_maximum_fusion.2), channel_id=1, source_target_pairs={{0,4},{4,0},{8,12},{12,8},{1,5},{5,1},{9,13},{13,9},{2,6},{6,2},{1... | collective-permute-start | bytes 122888 | tf_op jit(solution)/shard_map/ppermute | solution.py:36
  10.0 1.4 %shard_map.57 = (bf16[15,256,768]{2,1,0:T(8,128)(2,1)S(1)}, bf16[15,256,768]{2,1,0:T(8,128)(2,1)S(1)}, f32[2,24,128]{2,1,0:T(8,128)S(1)}) custom-call(s32[2,348]{1,0:T(2,128)S(1)} %shard_map.56.refs_0_, bf16[2,40,128]{2,1,0:T(8,128)(2,1)S(1)} %get-tuple-element.35.refs_1_, bf16[4,40,128]{2,1,0:T(8,128)(2,1)S(1)} %bitcast.60), custom_call_target="tpu_custom_call" | custom-call | flops 100000000 | bytes 10000000 | tf_op jit(solution)/shard_map/pallas_call | solution.py:452
  11.5 0.0 collective-permute-done.2
  11.5 0.0 collective-permute-done.1
  11.6 2.4 %collective-permute-start.3 = (bf16[6,40,128]{2,1,0:T(8,128)(2,1)S(1)}, bf16[6,40,128]{2,1,0:T(8,128)(2,1)S(1)}, u32[]{:S(2)}, u32[]{:S(2)}) collective-permute-start(bf16[6,40,128]{2,1,0:T(8,128)(2,1)S(1)} %get-tuple-element.43), channel_id=1, source_target_pairs={{0,1},{1,0},{2,3},{3,2},{4,5},{5,4},{6,7},{7,6},{8,9},{9,8},{10,11... | collective-permute-start | bytes 184328 | tf_op jit(solution)/shard_map/ppermute | solution.py:36
  14.0 0.7 collective-permute-start.4
  14.7 1.4 %shard_map.58 = (bf16[15,256,768]{2,1,0:T(8,128)(2,1)S(1)}, bf16[15,256,768]{2,1,0:T(8,128)(2,1)S(1)}, f32[2,24,128]{2,1,0:T(8,128)S(1)}) custom-call(s32[2,348]{1,0:T(2,128)S(1)} %shard_map.56.refs_0_, bf16[2,40,128]{2,1,0:T(8,128)(2,1)S(1)} %get-tuple-element.35.refs_1_, f32[2,24,128]{2,1,0:T(8,128)S(1)} %get-tuple-element.39.refs_2_, ...), custom_call_target="tpu_custom_call" | custom-call | flops 100000000 | bytes 10000000 | tf_op jit(solution)/shard_map/pallas_call | solution.py:452
  16.1 0.1 collective-permute-done.3.refs_5_
  16.2 0.0 collective-permute-done.4.refs_6_
  16.2 1.4 %shard_map.59 = (bf16[15,256,768]{2,1,0:T(8,128)(2,1)S(1)}, bf16[15,256,768]{2,1,0:T(8,128)(2,1)S(1)}, f32[2,24,128]{2,1,0:T(8,128)S(1)}, bf16[2,24,128]{2,1,0:T(8,128)(2,1)S(1)}) custom-call(s32[2,348]{1,0:T(2,128)S(1)} %shard_map.56.refs_0_, bf16[2,40,128]{2,1,0:T(8,128)(2,1)S(1)} %get-tuple-element.35.refs_1_, ...), custom_call_target="tpu_custom_call" | custom-call | tf_op jit(solution)/shard_map/pallas_call | solution.py:452
  17.6 1.4 %collective-permute-start.5 = (bf16[2,24,128]{2,1,0:T(8,128)(2,1)S(1)}, bf16[2,24,128]{2,1,0:T(8,128)(2,1)S(1)}, u32[]{:S(2)}, u32[]{:S(2)}) collective-permute-start(bf16[2,24,128]{2,1,0:T(8,128)(2,1)S(1)} %get-tuple-element.45), channel_id=1, source_target_pairs={{0,16},{16,0},{1,17},{17,1},{2,18},{18,2},{3,19},{19,3},{4,20},{20... | collective-permute-start | bytes 36872 | tf_op jit(solution)/shard_map/ppermute | solution.py:36
  19.0 2.3 %collective-permute-done.5 = bf16[2,24,128]{2,1,0:T(8,128)(2,1)S(1)} collective-permute-done((bf16[2,24,128]{2,1,0:T(8,128)(2,1)S(1)}, bf16[2,24,128]{2,1,0:T(8,128)(2,1)S(1)}, u32[]{:S(2)}, u32[]{:S(2)}) %collective-permute-start.5) | collective-permute-done | bytes 12320 | tf_op jit(solution)/shard_map/ppermute | solution.py:36
  21.4 0.7 collective-permute-start.7
  22.1 3.2 %collective-permute-start.6 = (bf16[2,2,24,128]{3,2,0,1:T(8,128)(2,1)S(1)}, bf16[2,2,24,128]{3,2,0,1:T(8,128)(2,1)S(1)}, u32[]{:S(2)}, u32[]{:S(2)}) collective-permute-start(bf16[2,2,24,128]{3,2,0,1:T(8,128)(2,1)S(1)} %pad_maximum_fusion.7), channel_id=1, source_target_pairs={{0,4},{4,0},{8,12},{12,8},{1,5},{5,1},{9,13},{13,9},{2,6},{6,2},{1... | collective-permute-start | bytes 73736 | tf_op jit(solution)/shard_map/ppermute | solution.py:36
  25.3 0.8 %shard_map.60.refs_3_ = f32[2,24,128]{2,1,0:T(8,128)S(1)} custom-call(s32[2,348]{1,0:T(2,128)S(1)} %shard_map.56.refs_0_, bf16[15,256,768]{2,1,0:T(8,128)(2,1)S(1)} %get-tuple-element.52.refs_1_, bf16[15,256,768]{2,1,0:T(8,128)(2,1)S(1)} %get-tuple-element.53.refs_2_, bf16[4,24,128]{2,1,0:T(8,128)(2,1)S(1)} %bitcast.55), custom_call_target="tpu_custom_call" | custom-call | flops 100000000 | bytes 10000000 | tf_op jit(solution)/shard_map/pallas_call | solution.py:452
  26.1 0.0 collective-permute-done.7
  26.1 0.0 collective-permute-done.6
  26.2 6.9 %collective-permute-start.8 = (bf16[6,24,128]{2,1,0:T(8,128)(2,1)S(1)}, bf16[6,24,128]{2,1,0:T(8,128)(2,1)S(1)}, u32[]{:S(2)}, u32[]{:S(2)}) collective-permute-start(bf16[6,24,128]{2,1,0:T(8,128)(2,1)S(1)} %get-tuple-element.56), channel_id=1, source_target_pairs={{0,1},{1,0},{2,3},{3,2},{4,5},{5,4},{6,7},{7,6},{8,9},{9,8},{10,11... | collective-permute-start | bytes 110600 | tf_op jit(solution)/shard_map/ppermute | solution.py:36
  33.1 0.7 collective-permute-start.9
  33.8 0.8 %shard_map.61.refs_3_ = f32[2,24,128]{2,1,0:T(8,128)S(1)} custom-call(s32[2,348]{1,0:T(2,128)S(1)} %shard_map.56.refs_0_, bf16[15,256,768]{2,1,0:T(8,128)(2,1)S(1)} %get-tuple-element.49.refs_1_, bf16[15,256,768]{2,1,0:T(8,128)(2,1)S(1)} %get-tuple-element.50.refs_2_, f32[2,24,128]{2,1,0:T(8,128)S(1)} %shard_map.60.refs_3_, ...), custom_call_target="tpu_custom_call" | custom-call | flops 100000000 | bytes 10000000 | tf_op jit(solution)/shard_map/pallas_call | solution.py:452
  34.6 0.5 collective-permute-done.8.refs_6_
  35.0 0.0 collective-permute-done.9.refs_7_
  35.0 0.8 %shard_map.62 = (f32[2,24,128]{2,1,0:T(8,128)S(1)}, bf16[2,24,128]{2,1,0:T(8,128)(2,1)S(1)}) custom-call(s32[2,348]{1,0:T(2,128)S(1)} %shard_map.56.refs_0_, bf16[15,256,768]{2,1,0:T(8,128)(2,1)S(1)} %get-tuple-element.47.refs_1_, bf16[15,256,768]{2,1,0:T(8,128)(2,1)S(1)} %get-tuple-element.48.refs_2_, f32[2,24,128]{2,1,0:T(8,128)S(1)} %shard_map.61.refs_3_, ...), custom_call_target="tpu_custom_call" | custom-call | tf_op jit(solution)/shard_map/pallas_call | solution.py:452
  35.9 0.1 collective-permute-start.10
  35.9 3.7 %collective-permute-done.10 = bf16[2,24,128]{2,1,0:T(8,128)(2,1)S(1)} collective-permute-done((bf16[2,24,128]{2,1,0:T(8,128)(2,1)S(1)}, bf16[2,24,128]{2,1,0:T(8,128)(2,1)S(1)}, u32[]{:S(2)}, u32[]{:S(2)}) %collective-permute-start.10) | collective-permute-done | bytes 12320 | tf_op jit(solution)/shard_map/ppermute | solution.py:36
  39.6 0.7 collective-permute-start.12
  40.3 3.3 %collective-permute-start.11 = (bf16[2,2,24,128]{3,2,0,1:T(8,128)(2,1)S(1)}, bf16[2,2,24,128]{3,2,0,1:T(8,128)(2,1)S(1)}, u32[]{:S(2)}, u32[]{:S(2)}) collective-permute-start(bf16[2,2,24,128]{3,2,0,1:T(8,128)(2,1)S(1)} %pad_maximum_fusion.8), channel_id=1, source_target_pairs={{0,4},{4,0},{8,12},{12,8},{1,5},{5,1},{9,13},{13,9},{2,6},{6,2},{1... | collective-permute-start | bytes 73736 | tf_op jit(solution)/shard_map/ppermute | solution.py:36
  43.7 0.8 %shard_map.63.refs_3_ = f32[2,24,128]{2,1,0:T(8,128)S(1)} custom-call(s32[2,348]{1,0:T(2,128)S(1)} %shard_map.56.refs_0_, bf16[15,256,768]{2,1,0:T(8,128)(2,1)S(1)} %get-tuple-element.52.refs_1_, bf16[15,256,768]{2,1,0:T(8,128)(2,1)S(1)} %get-tuple-element.53.refs_2_, bf16[4,24,128]{2,1,0:T(8,128)(2,1)S(1)} %bitcast.53), custom_call_target="tpu_custom_call" | custom-call | flops 100000000 | bytes 10000000 | tf_op jit(solution)/shard_map/pallas_call | solution.py:452
  44.5 0.0 collective-permute-done.12
  44.5 0.0 collective-permute-done.11
  44.6 4.7 %collective-permute-start.13 = (bf16[6,24,128]{2,1,0:T(8,128)(2,1)S(1)}, bf16[6,24,128]{2,1,0:T(8,128)(2,1)S(1)}, u32[]{:S(2)}, u32[]{:S(2)}) collective-permute-start(bf16[6,24,128]{2,1,0:T(8,128)(2,1)S(1)} %get-tuple-element.63), channel_id=1, source_target_pairs={{0,1},{1,0},{2,3},{3,2},{4,5},{5,4},{6,7},{7,6},{8,9},{9,8},{10,11... | collective-permute-start | bytes 110600 | tf_op jit(solution)/shard_map/ppermute | solution.py:36
  49.3 0.7 collective-permute-start.14
  50.0 0.8 %shard_map.64.refs_3_ = f32[2,24,128]{2,1,0:T(8,128)S(1)} custom-call(s32[2,348]{1,0:T(2,128)S(1)} %shard_map.56.refs_0_, bf16[15,256,768]{2,1,0:T(8,128)(2,1)S(1)} %get-tuple-element.49.refs_1_, bf16[15,256,768]{2,1,0:T(8,128)(2,1)S(1)} %get-tuple-element.50.refs_2_, f32[2,24,128]{2,1,0:T(8,128)S(1)} %shard_map.63.refs_3_, ...), custom_call_target="tpu_custom_call" | custom-call | flops 100000000 | bytes 10000000 | tf_op jit(solution)/shard_map/pallas_call | solution.py:452
  50.8 0.5 collective-permute-done.13.refs_8_
  51.2 0.0 collective-permute-done.14.refs_9_
  51.2 0.9 %shard_map.65 = f32[32,1,128]{2,1,0:T(1,128)S(1)} custom-call(s32[2,348]{1,0:T(2,128)S(1)} %shard_map.56.refs_0_, bf16[15,256,768]{2,1,0:T(8,128)(2,1)S(1)} %get-tuple-element.47.refs_1_, bf16[15,256,768]{2,1,0:T(8,128)(2,1)S(1)} %get-tuple-element.48.refs_2_, f32[2,24,128]{2,1,0:T(8,128)S(1)} %shard_map.64.refs_3_, ...), custom_call_target="tpu_custom_call" | custom-call | tf_op jit(solution)/shard_map/pallas_call | solution.py:452
  52.2 14.0 %all_to_all.5.moment_ref = f32[32,1,128]{2,1,0:T(1,128)S(1)} all-to-all(f32[32,1,128]{2,1,0:T(1,128)S(1)} %shard_map.65), channel_id=1, replica_groups=mesh['gx'=2,'gy'=4,'gz'=4] {'gx','gy','gz'}, dimensions={0} | all-to-all | bytes 32768 | tf_op jit(solution)/shard_map/all_to_all | solution.py:471
  66.2 1.0 %shard_map.66 = f32[1,1,2,8,384]{4,3,2,1,0:T(8,128)} custom-call(f32[32,1,128]{2,1,0:T(1,128)S(1)} %all_to_all.5.moment_ref, f32[2,24,128]{2,1,0:T(8,128)S(1)} %get-tuple-element.42.refs_4_.refs_5_.x0_ref, f32[2,24,128]{2,1,0:T(8,128)S(1)} %get-tuple-element.55.refs_5_.refs_6_.x1_ref, f32[2,24,128]{2,1,0:T(8,128)S(1)} %get-tuple-element.62.refs_7_.x2_ref), custom_call_target="tpu_custom_call" | custom-call | tf_op jit(solution)/shard_map/pallas_call | solution.py:472
  (24 shorter events, 0.2 us)
Async XLA Ops:
  0.8 5.3 %collective-permute-start = (bf16[2,40,128]{2,1,0:T(8,128)(2,1)S(1)}, bf16[2,40,128]{2,1,0:T(8,128)(2,1)S(1)}, u32[]{:S(2)}, u32[]{:S(2)}) collective-permute-start(bf16[2,40,128]{2,1,0:T(8,128)(2,1)S(1)} %get-tuple-element.35.refs_1_), channel_id=1, source_target_pairs={{0,16},{16,0},{1,17},{17,1},{2,18},{18,2},{3,19},{19,3},{4,20},{20... | collective-permute-start | bytes 61448 | tf_op jit(solution)/shard_map/ppermute | solution.py:36
  6.1 5.4 %collective-permute-start.2 = (bf16[2,2,40,128]{3,2,0,1:T(8,128)(2,1)S(1)}, bf16[2,2,40,128]{3,2,0,1:T(8,128)(2,1)S(1)}, u32[]{:S(2)}, u32[]{:S(2)}) collective-permute-start(bf16[2,2,40,128]{3,2,0,1:T(8,128)(2,1)S(1)} %pad_maximum_fusion.2), channel_id=1, source_target_pairs={{4,8},{8,4},{5,9},{9,5},{6,10},{10,6},{7,11},{11,7},{20,24},{24,20... | collective-permute-start | bytes 122888 | tf_op jit(solution)/shard_map/ppermute | solution.py:38
  6.8 4.7 %collective-permute-start.1 = (bf16[2,2,40,128]{3,2,0,1:T(8,128)(2,1)S(1)}, bf16[2,2,40,128]{3,2,0,1:T(8,128)(2,1)S(1)}, u32[]{:S(2)}, u32[]{:S(2)}) collective-permute-start(bf16[2,2,40,128]{3,2,0,1:T(8,128)(2,1)S(1)} %pad_maximum_fusion.2), channel_id=1, source_target_pairs={{0,4},{4,0},{8,12},{12,8},{1,5},{5,1},{9,13},{13,9},{2,6},{6,2},{1... | collective-permute-start | bytes 122888 | tf_op jit(solution)/shard_map/ppermute | solution.py:36
  11.6 4.6 %collective-permute-start.3 = (bf16[6,40,128]{2,1,0:T(8,128)(2,1)S(1)}, bf16[6,40,128]{2,1,0:T(8,128)(2,1)S(1)}, u32[]{:S(2)}, u32[]{:S(2)}) collective-permute-start(bf16[6,40,128]{2,1,0:T(8,128)(2,1)S(1)} %get-tuple-element.43), channel_id=1, source_target_pairs={{0,1},{1,0},{2,3},{3,2},{4,5},{5,4},{6,7},{7,6},{8,9},{9,8},{10,11... | collective-permute-start | bytes 184328 | tf_op jit(solution)/shard_map/ppermute | solution.py:36
  14.0 2.2 %collective-permute-start.4 = (bf16[6,40,128]{2,1,0:T(8,128)(2,1)S(1)}, bf16[6,40,128]{2,1,0:T(8,128)(2,1)S(1)}, u32[]{:S(2)}, u32[]{:S(2)}) collective-permute-start(bf16[6,40,128]{2,1,0:T(8,128)(2,1)S(1)} %get-tuple-element.44), channel_id=1, source_target_pairs={{1,2},{2,1},{5,6},{6,5},{9,10},{10,9},{13,14},{14,13},{17,18},{18,... | collective-permute-start | bytes 184328 | tf_op jit(solution)/shard_map/ppermute | solution.py:38
  17.6 3.8 %collective-permute-start.5 = (bf16[2,24,128]{2,1,0:T(8,128)(2,1)S(1)}, bf16[2,24,128]{2,1,0:T(8,128)(2,1)S(1)}, u32[]{:S(2)}, u32[]{:S(2)}) collective-permute-start(bf16[2,24,128]{2,1,0:T(8,128)(2,1)S(1)} %get-tuple-element.45), channel_id=1, source_target_pairs={{0,16},{16,0},{1,17},{17,1},{2,18},{18,2},{3,19},{19,3},{4,20},{20... | collective-permute-start | bytes 36872 | tf_op jit(solution)/shard_map/ppermute | solution.py:36
  21.4 4.7 %collective-permute-start.7 = (bf16[2,2,24,128]{3,2,0,1:T(8,128)(2,1)S(1)}, bf16[2,2,24,128]{3,2,0,1:T(8,128)(2,1)S(1)}, u32[]{:S(2)}, u32[]{:S(2)}) collective-permute-start(bf16[2,2,24,128]{3,2,0,1:T(8,128)(2,1)S(1)} %pad_maximum_fusion.7), channel_id=1, source_target_pairs={{4,8},{8,4},{5,9},{9,5},{6,10},{10,6},{7,11},{11,7},{20,24},{24,20... | collective-permute-start | bytes 73736 | tf_op jit(solution)/shard_map/ppermute | solution.py:38
  22.1 4.1 %collective-permute-start.6 = (bf16[2,2,24,128]{3,2,0,1:T(8,128)(2,1)S(1)}, bf16[2,2,24,128]{3,2,0,1:T(8,128)(2,1)S(1)}, u32[]{:S(2)}, u32[]{:S(2)}) collective-permute-start(bf16[2,2,24,128]{3,2,0,1:T(8,128)(2,1)S(1)} %pad_maximum_fusion.7), channel_id=1, source_target_pairs={{0,4},{4,0},{8,12},{12,8},{1,5},{5,1},{9,13},{13,9},{2,6},{6,2},{1... | collective-permute-start | bytes 73736 | tf_op jit(solution)/shard_map/ppermute | solution.py:36
  26.2 8.8 %collective-permute-start.8 = (bf16[6,24,128]{2,1,0:T(8,128)(2,1)S(1)}, bf16[6,24,128]{2,1,0:T(8,128)(2,1)S(1)}, u32[]{:S(2)}, u32[]{:S(2)}) collective-permute-start(bf16[6,24,128]{2,1,0:T(8,128)(2,1)S(1)} %get-tuple-element.56), channel_id=1, source_target_pairs={{0,1},{1,0},{2,3},{3,2},{4,5},{5,4},{6,7},{7,6},{8,9},{9,8},{10,11... | collective-permute-start | bytes 110600 | tf_op jit(solution)/shard_map/ppermute | solution.py:36
  33.1 1.9 %collective-permute-start.9 = (bf16[6,24,128]{2,1,0:T(8,128)(2,1)S(1)}, bf16[6,24,128]{2,1,0:T(8,128)(2,1)S(1)}, u32[]{:S(2)}, u32[]{:S(2)}) collective-permute-start(bf16[6,24,128]{2,1,0:T(8,128)(2,1)S(1)} %get-tuple-element.57), channel_id=1, source_target_pairs={{1,2},{2,1},{5,6},{6,5},{9,10},{10,9},{13,14},{14,13},{17,18},{18,... | collective-permute-start | bytes 110600 | tf_op jit(solution)/shard_map/ppermute | solution.py:38
  35.9 3.8 %collective-permute-start.10 = (bf16[2,24,128]{2,1,0:T(8,128)(2,1)S(1)}, bf16[2,24,128]{2,1,0:T(8,128)(2,1)S(1)}, u32[]{:S(2)}, u32[]{:S(2)}) collective-permute-start(bf16[2,24,128]{2,1,0:T(8,128)(2,1)S(1)} %get-tuple-element.58), channel_id=1, source_target_pairs={{0,16},{16,0},{1,17},{17,1},{2,18},{18,2},{3,19},{19,3},{4,20},{20... | collective-permute-start | bytes 36872 | tf_op jit(solution)/shard_map/ppermute | solution.py:36
  39.6 4.9 %collective-permute-start.12 = (bf16[2,2,24,128]{3,2,0,1:T(8,128)(2,1)S(1)}, bf16[2,2,24,128]{3,2,0,1:T(8,128)(2,1)S(1)}, u32[]{:S(2)}, u32[]{:S(2)}) collective-permute-start(bf16[2,2,24,128]{3,2,0,1:T(8,128)(2,1)S(1)} %pad_maximum_fusion.8), channel_id=1, source_target_pairs={{4,8},{8,4},{5,9},{9,5},{6,10},{10,6},{7,11},{11,7},{20,24},{24,20... | collective-permute-start | bytes 73736 | tf_op jit(solution)/shard_map/ppermute | solution.py:38
  40.3 4.2 %collective-permute-start.11 = (bf16[2,2,24,128]{3,2,0,1:T(8,128)(2,1)S(1)}, bf16[2,2,24,128]{3,2,0,1:T(8,128)(2,1)S(1)}, u32[]{:S(2)}, u32[]{:S(2)}) collective-permute-start(bf16[2,2,24,128]{3,2,0,1:T(8,128)(2,1)S(1)} %pad_maximum_fusion.8), channel_id=1, source_target_pairs={{0,4},{4,0},{8,12},{12,8},{1,5},{5,1},{9,13},{13,9},{2,6},{6,2},{1... | collective-permute-start | bytes 73736 | tf_op jit(solution)/shard_map/ppermute | solution.py:36
  44.6 6.7 %collective-permute-start.13 = (bf16[6,24,128]{2,1,0:T(8,128)(2,1)S(1)}, bf16[6,24,128]{2,1,0:T(8,128)(2,1)S(1)}, u32[]{:S(2)}, u32[]{:S(2)}) collective-permute-start(bf16[6,24,128]{2,1,0:T(8,128)(2,1)S(1)} %get-tuple-element.63), channel_id=1, source_target_pairs={{0,1},{1,0},{2,3},{3,2},{4,5},{5,4},{6,7},{7,6},{8,9},{9,8},{10,11... | collective-permute-start | bytes 110600 | tf_op jit(solution)/shard_map/ppermute | solution.py:36
  49.3 1.9 %collective-permute-start.14 = (bf16[6,24,128]{2,1,0:T(8,128)(2,1)S(1)}, bf16[6,24,128]{2,1,0:T(8,128)(2,1)S(1)}, u32[]{:S(2)}, u32[]{:S(2)}) collective-permute-start(bf16[6,24,128]{2,1,0:T(8,128)(2,1)S(1)} %get-tuple-element.64), channel_id=1, source_target_pairs={{1,2},{2,1},{5,6},{6,5},{9,10},{10,9},{13,14},{14,13},{17,18},{18,... | collective-permute-start | bytes 110600 | tf_op jit(solution)/shard_map/ppermute | solution.py:38

commit v5 on v4

--- a/solution.py
+++ b/solution.py
@@ -39,16 +39,38 @@
     return got
 
 
-def spread(field, table, stage):
+def plane_exchange(field):
+    plane = ("gx", "gy")
+    size_x, size_y = [lax.axis_size(axis) for axis in plane]
+    got = lax.all_to_all(jnp.broadcast_to(field[None], (size_x * size_y,) + field.shape), plane, 0, 0)
+    x, y = [lax.axis_index(axis) for axis in plane]
+
+    def partners(index, count):
+        even, odd = index + 1 - 2 * (index % 2), index - 1 + 2 * (index % 2)
+        return [index, jnp.minimum(even, count - 1)] + [jnp.clip(odd, 0, count - 1)] * (count > 2)
+
+    rows = [
+        jnp.stack([lax.dynamic_index_in_dim(got, i * size_y + j, 0, False) for i in partners(x, size_x)])
+        for j in partners(y, size_y)
+    ]
+    return rows[0], rows[1:]
+
+
+def spread(field, table, stage, at_once):
     shape = (-1,) + field.shape[1:]
-    columns = jnp.stack([field] + swaps("gx", field, field))
-    columns, table = lax.optimization_barrier((columns, table))
-    others = swaps("gy", columns, columns)
+    if at_once:
+        columns, others = plane_exchange(field)
+    else:
+        columns = jnp.stack([field] + swaps("gx", field, field))
+        columns, table = lax.optimization_barrier((columns, table))
+        others = swaps("gy", columns, columns)
     result = stage(table, 0, [columns.reshape(shape)], None)
     odd = lax.axis_index("gz") % 2 == 1
     low = jnp.concatenate([part[:, 0] for part in [columns] + others])
     high = jnp.concatenate([part[:, field.shape[0] - 1] for part in [columns] + others])
-    low, high, result = lax.optimization_barrier((jnp.where(odd, low, high), jnp.where(odd, high, low), result))
+    low, high = jnp.where(odd, low, high), jnp.where(odd, high, low)
+    if not at_once:
+        low, high, result = lax.optimization_barrier((low, high, result))
     far = swaps("gz", low, high)
     result = stage(table, 1, [part.reshape(shape) for part in others], result)
     return stage(table, 2, far, result)
@@ -462,7 +484,8 @@
                 result = result[2:]
             return result if last and not moments else result[0]
 
-        return spread(vector, table, stage)
+        at_once = lax.axis_size(("gx", "gy")) <= 8
+        return spread(vector, table, stage, at_once)
 
     tiles = []
     x1, send = apply(packed, tiles, [x0])

time: 67.5 us -> 65.2 us (0.966)
  starting transfers between devices: 32.2 us -> 18.7 us
  blocking collectives: 14 us -> 26.2 us
  waiting for transfers between devices: 7.07 us -> 3.12 us
  Pallas kernels: 12.6 us -> 14.8 us
  local copies, waits for them, and re-layouts: 0.11 us -> 0.79 us
    ppermute x9 -> x3, starting transfers between devices: 28.3 us -> 11.5 us  [swaps(): got = [lax.ppermute(first, axis, matching(count, 0))]]
    all_to_all x0 -> x2, blocking collectives: none -> 15.1 us  [plane_exchange(): lax.all_to_all(jnp.broadcast_to(field[None], (size_x * size_y,) + field.s...]
    ppermute x9 -> x3, waiting for transfers between devices: 7 us -> 0.03 us  [swaps(): got = [lax.ppermute(first, axis, matching(count, 0))]]
    all_to_all x0 -> x1, starting transfers between devices: none -> 5.2 us  [plane_exchange(): lax.all_to_all(jnp.broadcast_to(field[None], (size_x * size_y,) + field.s...]
    all_to_all x0 -> x1, waiting for transfers between devices: none -> 3.02 us  [plane_exchange(): lax.all_to_all(jnp.broadcast_to(field[None], (size_x * size_y,) + field.s...]
    all_to_all x1, blocking collectives: 14 us -> 11 us  [body(): moments = lax.all_to_all(moments, AXES, 0, 0)]
    pallas_call x9, Pallas kernels: 9.25 us -> 11.3 us  [stage(): call(functools.partial(stage_kernel, index, building, last and moments),...]
    ppermute x6 -> x3, starting transfers between devices: 3.92 us -> 1.99 us  [swaps(): got.append(lax.ppermute(second, axis, matching(count, 1)))]
  transfers between devices with their start and end apart: 15 -> 7, of which waited for: 5 -> 1; matrix products, arithmetic and copies ran while one was open for 0% -> 0% of each run, Pallas kernels for 11% -> 15%
where the time goes in v5:
time: 65.2 us; the launch traced here: 64.8 us
  blocking collectives  26.2 us (40%)
  starting transfers between devices  18.7 us (29%)
  Pallas kernels  14.8 us (23%)
  waiting for transfers between devices  3.12 us (5%)
  between operations  1.02 us (2%)
  local copies, waits for them, and re-layouts  0.79 us (1%)
    all_to_all x2, blocking collectives, plane_exchange(): lax.all_to_all(jnp.broadcast_to(field[None], (size_x * size_y,) + field.s...  15.1 us
    ppermute x3, starting transfers between devices, swaps(): got = [lax.ppermute(first, axis, matching(count, 0))]  11.5 us
    pallas_call x9, Pallas kernels, stage(): call(functools.partial(stage_kernel, index, building, last and moments),...  11.3 us
    all_to_all x1, blocking collectives, body(): moments = lax.all_to_all(moments, AXES, 0, 0)  11 us
    all_to_all x1, starting transfers between devices, plane_exchange(): lax.all_to_all(jnp.broadcast_to(field[None], (size_x * size_y,) + field.s...  5.2 us
    all_to_all x1, waiting for transfers between devices, plane_exchange(): lax.all_to_all(jnp.broadcast_to(field[None], (size_x * size_y,) + field.s...  3.02 us
    ppermute x3, starting transfers between devices, swaps(): got.append(lax.ppermute(second, axis, matching(count, 1)))  1.99 us
    pallas_call x1, Pallas kernels, pair_table(): pl.pallas_call(functools.partial(table_kernel, sizes, slots, blocks), out...  1.72 us
  transfers between devices with their start and end apart: 7, of which 1 were waited for; matrix products, arithmetic and copies ran while one was open for 0% of the time, Pallas kernels for 15%

profile of v5, /device:TPU:0, one launch (start us, length us, event | category | flops | bytes accessed | tf_op | source)
XLA Modules:
  0.0 64.8 jit_solution(17156706435827208566)
XLA Ops:
  0.0 0.8 %shard_map.56 = (f32[2,24,128]{2,1,0:T(8,128)S(1)}, f32[2,8,128]{2,1,0:T(8,128)S(1)}, bf16[2,40,128]{2,1,0:T(8,128)(2,1)S(1)}) custom-call(s32[1,1,2]{2,1,0:T(1,128)} %fill_hbm.1, f32[1,1,2,8,384]{4,3,2,1,0:T(8,128)} %noise_hbm.1, f32[1,1,3,2,128]{4,3,2,1,0:T(2,128)} %bitcast.92), custom_call_target="tpu_custom_call" | custom-call | tf_op jit(solution)/shard_map/pallas_call | solution.py:440
  0.8 0.7 %broadcast_in_dim.6 = bf16[8,2,40,128]{3,2,1,0:T(8,128)(2,1)} broadcast(bf16[2,40,128]{2,1,0:T(8,128)(2,1)S(1)} %get-tuple-element.20.refs_1_), dimensions={1,2,3} | broadcast | bytes 184320 | tf_op jit(solution)/shard_map/broadcast_in_dim | solution.py:45
  1.5 5.2 %all-to-all-start = ((bf16[8,2,40,128]{3,2,1,0:T(8,128)(2,1)}), bf16[8,2,40,128]{3,2,1,0:T(8,128)(2,1)S(1)}, u32[]{:S(2)}, u32[]{:S(2)}) async-start(bf16[8,2,40,128]{3,2,1,0:T(8,128)(2,1)} %broadcast_in_dim.6), calls=%async_computation | async-start | bytes 327680 | tf_op jit(solution)/shard_map/all_to_all | solution.py:45
  7.3 1.7 %shard_map.55.refs_0_ = s32[2,348]{1,0:T(2,128)S(1)} custom-call(s32[1,1,1]{2,1,0:T(1,128)S(6)} %copy.60.count_ref, s32[1,1,3,1,54]{4,3,2,1,0:T(1,128)} %bitcast.93), custom_call_target="tpu_custom_call" | custom-call | flops 1000000 | bytes 1000000 | tf_op jit(solution)/shard_map/pallas_call | solution.py:123
  9.1 3.0 %all-to-all-done = bf16[8,2,40,128]{3,2,1,0:T(8,128)(2,1)S(1)} async-done(((bf16[8,2,40,128]{3,2,1,0:T(8,128)(2,1)}), bf16[8,2,40,128]{3,2,1,0:T(8,128)(2,1)S(1)}, u32[]{:S(2)}, u32[]{:S(2)}) %all-to-all-start) | async-done | bytes 163872 | tf_op jit(solution)/shard_map/all_to_all | solution.py:45
  12.2 0.7 %collective-permute-start.1 = (bf16[6,40,128]{2,1,0:T(8,128)(2,1)S(1)}, bf16[6,40,128]{2,1,0:T(8,128)(2,1)S(1)}, u32[]{:S(2)}, u32[]{:S(2)}) collective-permute-start(bf16[6,40,128]{2,1,0:T(8,128)(2,1)S(1)} %get-tuple-element.41), channel_id=1, source_target_pairs={{1,2},{2,1},{5,6},{6,5},{9,10},{10,9},{13,14},{14,13},{17,18},{18,... | collective-permute-start | bytes 184328 | tf_op jit(solution)/shard_map/ppermute | solution.py:38
  12.9 4.5 %collective-permute-start = (bf16[6,40,128]{2,1,0:T(8,128)(2,1)S(1)}, bf16[6,40,128]{2,1,0:T(8,128)(2,1)S(1)}, u32[]{:S(2)}, u32[]{:S(2)}) collective-permute-start(bf16[6,40,128]{2,1,0:T(8,128)(2,1)S(1)} %get-tuple-element.42), channel_id=1, source_target_pairs={{0,1},{1,0},{2,3},{3,2},{4,5},{5,4},{6,7},{7,6},{8,9},{9,8},{10,11... | collective-permute-start | bytes 184328 | tf_op jit(solution)/shard_map/ppermute | solution.py:36
  17.4 1.9 %shard_map.57 = (bf16[15,256,768]{2,1,0:T(8,128)(2,1)S(1)}, bf16[15,256,768]{2,1,0:T(8,128)(2,1)S(1)}, f32[2,24,128]{2,1,0:T(8,128)S(1)}) custom-call(s32[2,348]{1,0:T(2,128)S(1)} %shard_map.55.refs_0_, bf16[2,40,128]{2,1,0:T(8,128)(2,1)S(1)} %get-tuple-element.20.refs_1_, bf16[4,40,128]{2,1,0:T(8,128)(2,1)S(1)} %bitcast.91), custom_call_target="tpu_custom_call" | custom-call | flops 100000000 | bytes 10000000 | tf_op jit(solution)/shard_map/pallas_call | solution.py:474
  19.3 2.0 %shard_map.58 = (bf16[15,256,768]{2,1,0:T(8,128)(2,1)S(1)}, bf16[15,256,768]{2,1,0:T(8,128)(2,1)S(1)}, f32[2,24,128]{2,1,0:T(8,128)S(1)}) custom-call(s32[2,348]{1,0:T(2,128)S(1)} %shard_map.55.refs_0_, bf16[2,40,128]{2,1,0:T(8,128)(2,1)S(1)} %get-tuple-element.20.refs_1_, f32[2,24,128]{2,1,0:T(8,128)S(1)} %get-tuple-element.21.refs_2_, ...), custom_call_target="tpu_custom_call" | custom-call | flops 100000000 | bytes 10000000 | tf_op jit(solution)/shard_map/pallas_call | solution.py:474
  21.3 0.0 collective-permute-done.1.refs_6_
  21.3 0.0 collective-permute-done.refs_5_
  21.3 1.4 %shard_map.59 = (bf16[15,256,768]{2,1,0:T(8,128)(2,1)S(1)}, bf16[15,256,768]{2,1,0:T(8,128)(2,1)S(1)}, f32[2,24,128]{2,1,0:T(8,128)S(1)}, bf16[2,24,128]{2,1,0:T(8,128)(2,1)S(1)}) custom-call(s32[2,348]{1,0:T(2,128)S(1)} %shard_map.55.refs_0_, bf16[2,40,128]{2,1,0:T(8,128)(2,1)S(1)} %get-tuple-element.20.refs_1_, ...), custom_call_target="tpu_custom_call" | custom-call | tf_op jit(solution)/shard_map/pallas_call | solution.py:474
  22.7 7.8 %all_to_all.20 = bf16[8,2,24,128]{3,2,1,0:T(8,128)(2,1)S(1)} all-to-all(bf16[8,2,24,128]{3,2,1,0:T(8,128)(2,1)S(1)} %broadcast_in_dim.7), channel_id=1, replica_groups=mesh['gx'=2,'gy'=4,'gz'=4] {'gx','gy'}, dimensions={0} | all-to-all | bytes 196608 | tf_op jit(solution)/shard_map/all_to_all | solution.py:45
  30.7 0.7 %collective-permute-start.3 = (bf16[6,24,128]{2,1,0:T(8,128)(2,1)S(1)}, bf16[6,24,128]{2,1,0:T(8,128)(2,1)S(1)}, u32[]{:S(2)}, u32[]{:S(2)}) collective-permute-start(bf16[6,24,128]{2,1,0:T(8,128)(2,1)S(1)} %get-tuple-element.57), channel_id=1, source_target_pairs={{1,2},{2,1},{5,6},{6,5},{9,10},{10,9},{13,14},{14,13},{17,18},{18,... | collective-permute-start | bytes 110600 | tf_op jit(solution)/shard_map/ppermute | solution.py:38
  31.3 3.5 %collective-permute-start.2 = (bf16[6,24,128]{2,1,0:T(8,128)(2,1)S(1)}, bf16[6,24,128]{2,1,0:T(8,128)(2,1)S(1)}, u32[]{:S(2)}, u32[]{:S(2)}) collective-permute-start(bf16[6,24,128]{2,1,0:T(8,128)(2,1)S(1)} %get-tuple-element.58), channel_id=1, source_target_pairs={{0,1},{1,0},{2,3},{3,2},{4,5},{5,4},{6,7},{7,6},{8,9},{9,8},{10,11... | collective-permute-start | bytes 110600 | tf_op jit(solution)/shard_map/ppermute | solution.py:36
  34.9 1.0 %shard_map.60.refs_3_ = f32[2,24,128]{2,1,0:T(8,128)S(1)} custom-call(s32[2,348]{1,0:T(2,128)S(1)} %shard_map.55.refs_0_, bf16[15,256,768]{2,1,0:T(8,128)(2,1)S(1)} %get-tuple-element.29.refs_1_, bf16[15,256,768]{2,1,0:T(8,128)(2,1)S(1)} %get-tuple-element.30.refs_2_, bf16[4,24,128]{2,1,0:T(8,128)(2,1)S(1)} %bitcast.88), custom_call_target="tpu_custom_call" | custom-call | flops 100000000 | bytes 10000000 | tf_op jit(solution)/shard_map/pallas_call | solution.py:474
  35.9 1.1 %shard_map.61.refs_3_ = f32[2,24,128]{2,1,0:T(8,128)S(1)} custom-call(s32[2,348]{1,0:T(2,128)S(1)} %shard_map.55.refs_0_, bf16[15,256,768]{2,1,0:T(8,128)(2,1)S(1)} %get-tuple-element.27.refs_1_, bf16[15,256,768]{2,1,0:T(8,128)(2,1)S(1)} %get-tuple-element.28.refs_2_, f32[2,24,128]{2,1,0:T(8,128)S(1)} %shard_map.60.refs_3_, ...), custom_call_target="tpu_custom_call" | custom-call | flops 100000000 | bytes 10000000 | tf_op jit(solution)/shard_map/pallas_call | solution.py:474
  37.0 0.0 collective-permute-done.3.refs_7_
  37.0 0.0 collective-permute-done.2.refs_6_
  37.0 0.8 %shard_map.62 = (f32[2,24,128]{2,1,0:T(8,128)S(1)}, bf16[2,24,128]{2,1,0:T(8,128)(2,1)S(1)}) custom-call(s32[2,348]{1,0:T(2,128)S(1)} %shard_map.55.refs_0_, bf16[15,256,768]{2,1,0:T(8,128)(2,1)S(1)} %get-tuple-element.25.refs_1_, bf16[15,256,768]{2,1,0:T(8,128)(2,1)S(1)} %get-tuple-element.26.refs_2_, f32[2,24,128]{2,1,0:T(8,128)S(1)} %shard_map.61.refs_3_, ...), custom_call_target="tpu_custom_call" | custom-call | tf_op jit(solution)/shard_map/pallas_call | solution.py:474
  37.9 7.3 %all_to_all.21 = bf16[8,2,24,128]{3,2,1,0:T(8,128)(2,1)S(1)} all-to-all(bf16[8,2,24,128]{3,2,1,0:T(8,128)(2,1)S(1)} %broadcast_in_dim.8), channel_id=1, replica_groups=mesh['gx'=2,'gy'=4,'gz'=4] {'gx','gy'}, dimensions={0} | all-to-all | bytes 196608 | tf_op jit(solution)/shard_map/all_to_all | solution.py:45
  45.4 0.7 %collective-permute-start.5 = (bf16[6,24,128]{2,1,0:T(8,128)(2,1)S(1)}, bf16[6,24,128]{2,1,0:T(8,128)(2,1)S(1)}, u32[]{:S(2)}, u32[]{:S(2)}) collective-permute-start(bf16[6,24,128]{2,1,0:T(8,128)(2,1)S(1)} %get-tuple-element.55), channel_id=1, source_target_pairs={{1,2},{2,1},{5,6},{6,5},{9,10},{10,9},{13,14},{14,13},{17,18},{18,... | collective-permute-start | bytes 110600 | tf_op jit(solution)/shard_map/ppermute | solution.py:38
  46.0 3.6 %collective-permute-start.4 = (bf16[6,24,128]{2,1,0:T(8,128)(2,1)S(1)}, bf16[6,24,128]{2,1,0:T(8,128)(2,1)S(1)}, u32[]{:S(2)}, u32[]{:S(2)}) collective-permute-start(bf16[6,24,128]{2,1,0:T(8,128)(2,1)S(1)} %get-tuple-element.56), channel_id=1, source_target_pairs={{0,1},{1,0},{2,3},{3,2},{4,5},{5,4},{6,7},{7,6},{8,9},{9,8},{10,11... | collective-permute-start | bytes 110600 | tf_op jit(solution)/shard_map/ppermute | solution.py:36
  49.6 1.0 %shard_map.63.refs_3_ = f32[2,24,128]{2,1,0:T(8,128)S(1)} custom-call(s32[2,348]{1,0:T(2,128)S(1)} %shard_map.55.refs_0_, bf16[15,256,768]{2,1,0:T(8,128)(2,1)S(1)} %get-tuple-element.29.refs_1_, bf16[15,256,768]{2,1,0:T(8,128)(2,1)S(1)} %get-tuple-element.30.refs_2_, bf16[4,24,128]{2,1,0:T(8,128)(2,1)S(1)} %bitcast.87), custom_call_target="tpu_custom_call" | custom-call | flops 100000000 | bytes 10000000 | tf_op jit(solution)/shard_map/pallas_call | solution.py:474
  50.7 1.1 %shard_map.64.refs_3_ = f32[2,24,128]{2,1,0:T(8,128)S(1)} custom-call(s32[2,348]{1,0:T(2,128)S(1)} %shard_map.55.refs_0_, bf16[15,256,768]{2,1,0:T(8,128)(2,1)S(1)} %get-tuple-element.27.refs_1_, bf16[15,256,768]{2,1,0:T(8,128)(2,1)S(1)} %get-tuple-element.28.refs_2_, f32[2,24,128]{2,1,0:T(8,128)S(1)} %shard_map.63.refs_3_, ...), custom_call_target="tpu_custom_call" | custom-call | flops 100000000 | bytes 10000000 | tf_op jit(solution)/shard_map/pallas_call | solution.py:474
  51.8 0.0 collective-permute-done.5.refs_9_
  51.8 0.0 collective-permute-done.4.refs_8_
  51.8 0.9 %shard_map.65 = f32[32,1,128]{2,1,0:T(1,128)S(1)} custom-call(s32[2,348]{1,0:T(2,128)S(1)} %shard_map.55.refs_0_, bf16[15,256,768]{2,1,0:T(8,128)(2,1)S(1)} %get-tuple-element.25.refs_1_, bf16[15,256,768]{2,1,0:T(8,128)(2,1)S(1)} %get-tuple-element.26.refs_2_, f32[2,24,128]{2,1,0:T(8,128)S(1)} %shard_map.64.refs_3_, ...), custom_call_target="tpu_custom_call" | custom-call | tf_op jit(solution)/shard_map/pallas_call | solution.py:474
  52.8 11.0 %all_to_all.22.moment_ref = f32[32,1,128]{2,1,0:T(1,128)S(1)} all-to-all(f32[32,1,128]{2,1,0:T(1,128)S(1)} %shard_map.65), channel_id=1, replica_groups=mesh['gx'=2,'gy'=4,'gz'=4] {'gx','gy','gz'}, dimensions={0} | all-to-all | bytes 32768 | tf_op jit(solution)/shard_map/all_to_all | solution.py:494
  63.8 1.0 %shard_map.66 = f32[1,1,2,8,384]{4,3,2,1,0:T(8,128)} custom-call(f32[32,1,128]{2,1,0:T(1,128)S(1)} %all_to_all.22.moment_ref, f32[2,24,128]{2,1,0:T(8,128)S(1)} %get-tuple-element.24.refs_4_.refs_5_.x0_ref, f32[2,24,128]{2,1,0:T(8,128)S(1)} %get-tuple-element.32.refs_5_.refs_6_.x1_ref, f32[2,24,128]{2,1,0:T(8,128)S(1)} %get-tuple-element.34.refs_7_.x2_ref), custom_call_target="tpu_custom_call" | custom-call | tf_op jit(solution)/shard_map/pallas_call | solution.py:495
  (33 shorter events, 0.3 us)
Async XLA Ops:
  1.5 10.6 %all-to-all-start = ((bf16[8,2,40,128]{3,2,1,0:T(8,128)(2,1)}), bf16[8,2,40,128]{3,2,1,0:T(8,128)(2,1)S(1)}, u32[]{:S(2)}, u32[]{:S(2)}) async-start(bf16[8,2,40,128]{3,2,1,0:T(8,128)(2,1)} %broadcast_in_dim.6), calls=%async_computation | async-start | bytes 327680 | tf_op jit(solution)/shard_map/all_to_all | solution.py:45
  12.2 9.1 %collective-permute-start.1 = (bf16[6,40,128]{2,1,0:T(8,128)(2,1)S(1)}, bf16[6,40,128]{2,1,0:T(8,128)(2,1)S(1)}, u32[]{:S(2)}, u32[]{:S(2)}) collective-permute-start(bf16[6,40,128]{2,1,0:T(8,128)(2,1)S(1)} %get-tuple-element.41), channel_id=1, source_target_pairs={{1,2},{2,1},{5,6},{6,5},{9,10},{10,9},{13,14},{14,13},{17,18},{18,... | collective-permute-start | bytes 184328 | tf_op jit(solution)/shard_map/ppermute | solution.py:38
  12.9 8.4 %collective-permute-start = (bf16[6,40,128]{2,1,0:T(8,128)(2,1)S(1)}, bf16[6,40,128]{2,1,0:T(8,128)(2,1)S(1)}, u32[]{:S(2)}, u32[]{:S(2)}) collective-permute-start(bf16[6,40,128]{2,1,0:T(8,128)(2,1)S(1)} %get-tuple-element.42), channel_id=1, source_target_pairs={{0,1},{1,0},{2,3},{3,2},{4,5},{5,4},{6,7},{7,6},{8,9},{9,8},{10,11... | collective-permute-start | bytes 184328 | tf_op jit(solution)/shard_map/ppermute | solution.py:36
  30.7 6.4 %collective-permute-start.3 = (bf16[6,24,128]{2,1,0:T(8,128)(2,1)S(1)}, bf16[6,24,128]{2,1,0:T(8,128)(2,1)S(1)}, u32[]{:S(2)}, u32[]{:S(2)}) collective-permute-start(bf16[6,24,128]{2,1,0:T(8,128)(2,1)S(1)} %get-tuple-element.57), channel_id=1, source_target_pairs={{1,2},{2,1},{5,6},{6,5},{9,10},{10,9},{13,14},{14,13},{17,18},{18,... | collective-permute-start | bytes 110600 | tf_op jit(solution)/shard_map/ppermute | solution.py:38
  31.3 5.7 %collective-permute-start.2 = (bf16[6,24,128]{2,1,0:T(8,128)(2,1)S(1)}, bf16[6,24,128]{2,1,0:T(8,128)(2,1)S(1)}, u32[]{:S(2)}, u32[]{:S(2)}) collective-permute-start(bf16[6,24,128]{2,1,0:T(8,128)(2,1)S(1)} %get-tuple-element.58), channel_id=1, source_target_pairs={{0,1},{1,0},{2,3},{3,2},{4,5},{5,4},{6,7},{7,6},{8,9},{9,8},{10,11... | collective-permute-start | bytes 110600 | tf_op jit(solution)/shard_map/ppermute | solution.py:36
  45.4 6.4 %collective-permute-start.5 = (bf16[6,24,128]{2,1,0:T(8,128)(2,1)S(1)}, bf16[6,24,128]{2,1,0:T(8,128)(2,1)S(1)}, u32[]{:S(2)}, u32[]{:S(2)}) collective-permute-start(bf16[6,24,128]{2,1,0:T(8,128)(2,1)S(1)} %get-tuple-element.55), channel_id=1, source_target_pairs={{1,2},{2,1},{5,6},{6,5},{9,10},{10,9},{13,14},{14,13},{17,18},{18,... | collective-permute-start | bytes 110600 | tf_op jit(solution)/shard_map/ppermute | solution.py:38
  46.0 5.8 %collective-permute-start.4 = (bf16[6,24,128]{2,1,0:T(8,128)(2,1)S(1)}, bf16[6,24,128]{2,1,0:T(8,128)(2,1)S(1)}, u32[]{:S(2)}, u32[]{:S(2)}) collective-permute-start(bf16[6,24,128]{2,1,0:T(8,128)(2,1)S(1)} %get-tuple-element.56), channel_id=1, source_target_pairs={{0,1},{1,0},{2,3},{3,2},{4,5},{5,4},{6,7},{7,6},{8,9},{9,8},{10,11... | collective-permute-start | bytes 110600 | tf_op jit(solution)/shard_map/ppermute | solution.py:36

commit v6 on v5

--- a/solution.py
+++ b/solution.py
@@ -64,7 +64,8 @@
         columns = jnp.stack([field] + swaps("gx", field, field))
         columns, table = lax.optimization_barrier((columns, table))
         others = swaps("gy", columns, columns)
-    result = stage(table, 0, [columns.reshape(shape)], None)
+    rows = [part.reshape(shape) for part in [columns] + others]
+    result = None if at_once else stage(table, 0, rows[:1], None)
     odd = lax.axis_index("gz") % 2 == 1
     low = jnp.concatenate([part[:, 0] for part in [columns] + others])
     high = jnp.concatenate([part[:, field.shape[0] - 1] for part in [columns] + others])
@@ -72,11 +73,11 @@
     if not at_once:
         low, high, result = lax.optimization_barrier((low, high, result))
     far = swaps("gz", low, high)
-    result = stage(table, 1, [part.reshape(shape) for part in others], result)
+    result = stage(table, 1, rows if at_once else rows[1:], result)
     return stage(table, 2, far, result)
 
 
-def table_kernel(sizes, slots, blocks, count_ref, list_hbm, table_ref, list_ref, sem):
+def table_kernel(sizes, slots, width, at_once, blocks, count_ref, list_hbm, table_ref, list_ref, sem):
     copy = pltpu.make_async_copy(list_hbm, list_ref, sem)
     copy.start()
     sets = len(slots) * blocks
@@ -96,11 +97,11 @@
         x, y = partner(0, plane - 1), partner(1, third - 3 * plane - 1)
         z = home + code - 3 * third - 1
         far = (z < 0) | (z >= blocks)
-        width = slots[0] // blocks
         side = partner(2, jnp.where(z < 0, -1, 1)) - 1
-        slot = (jnp.maximum(y - 1, 0) * width + x) * blocks + z
+        row = y if at_once else jnp.maximum(y - 1, 0)
+        slot = (row * width + x) * blocks + z
         slot = jnp.where(far, side * (slots[2] // (1 if sizes[2] == 2 else 2)) + y * width + x, slot)
-        at = jnp.where(far, 2, jnp.minimum(y, 1)) * blocks + home
+        at = jnp.where(far, 2, 1 if at_once else jnp.minimum(y, 1)) * blocks + home
         place = table_ref[1, at]
         table_ref[1, at] = place + 1
         table_ref[0, at * segment + place] = slot
@@ -116,12 +117,12 @@
                 table_ref[0, end + i] = empty
 
 
-def pair_table(pair_list, pair_count, blocks, slots):
+def pair_table(pair_list, pair_count, blocks, slots, width, at_once):
     segment = -(-(pair_list.shape[4] + 3) // 2) * 2
     sizes = [lax.axis_size(axis) for axis in AXES]
     pair_list = pltpu.with_memory_space_constraint(jnp.swapaxes(pair_list, 2, 3), pltpu.HBM)
     return pl.pallas_call(
-        functools.partial(table_kernel, sizes, slots, blocks),
+        functools.partial(table_kernel, sizes, slots, width, at_once, blocks),
         out_shape=jax.ShapeDtypeStruct((2, len(slots) * blocks * segment), jnp.int32),
         in_specs=[SMEM, HBM],
         out_specs=SMEM,
@@ -298,11 +299,11 @@
     return sum_ref[block] * mask_ref[block, :1] - old_ref[block]
 
 
-def stage_kernel(stage, building, moments, *refs):
+def stage_kernel(stage, begins, building, moments, *refs):
     refs = list(refs)
     table_ref, own_ref = refs.pop(0), refs.pop(0) if building else None
     tiles = None if building else (refs.pop(0), refs.pop(0))
-    before_ref = refs.pop(0) if stage else None
+    before_ref = None if begins else refs.pop(0)
     last = stage == 2
     mask_ref = refs.pop(0) if last else None
     old = [refs.pop(0) for _ in range(3 if moments else 1)] if last else []
@@ -315,7 +316,7 @@
     gather_slots(refs, slots_ref)
     if not last:
         sum_ref = outs[0]
-    sum_ref[...] = before_ref[...] if stage else jnp.zeros_like(sum_ref)
+    sum_ref[...] = jnp.zeros_like(sum_ref) if begins else before_ref[...]
     if building:
         build(table_ref, stage, own_ref, slots_ref, *tiles, sum_ref, *columns)
     else:
@@ -434,7 +435,9 @@
     columns = 2 if lax.axis_size("gx") == 2 else 3
     others = 1 if lax.axis_size("gy") == 2 else 2
     sides = 1 if lax.axis_size("gz") == 2 else 2
-    slots = (columns * blocks, others * columns * blocks, sides * (1 + others) * columns)
+    at_once = lax.axis_size(("gx", "gy")) <= 8
+    middle = others + 1 if at_once else others
+    slots = (columns * blocks, middle * columns * blocks, sides * (1 + others) * columns)
     limit = 8 << 20
 
     x0, mask, packed = call(
@@ -453,7 +456,7 @@
         ),
         4 << 20,
     )(*[pltpu.with_memory_space_constraint(a, pltpu.HBM) for a in (block_fill, noise, jnp.swapaxes(positions, 2, 3))])
-    table = pair_table(pair_list, pair_count, blocks, slots)
+    table = pair_table(pair_list, pair_count, blocks, slots, columns, at_once)
     field, sent = jax.ShapeDtypeStruct(shape, f32), jax.ShapeDtypeStruct(shape, bf16)
     capacity = (pair_list.shape[4] + blocks) // 4 + 1
     tile = jax.ShapeDtypeStruct((capacity, 2 * beads, len(PLACES) * beads), bf16)
@@ -470,9 +473,9 @@
             scratch = [pltpu.VMEM((slots[index] + 1,) + given[0].shape[1:], bf16)]
             scratch += [total] * last + [pltpu.VMEM((beads, 128), f32)] * (2 * building)
             args = [packed] if building else list(tiles[index])
-            args += ([result] if index else []) + ([mask] + olds if last else []) + given
+            args += ([] if result is None else [result]) + ([mask] + olds if last else []) + given
             result = call(
-                functools.partial(stage_kernel, index, building, last and moments),
+                functools.partial(stage_kernel, index, result is None, building, last and moments),
                 (tile, tile) * building + outs,
                 [SMEM] + [VMEM] * len(args),
                 scratch,
@@ -480,14 +483,13 @@
                 None if last else cost,
             )(table, *args)
             if building:
-                tiles.append(result[:2])
+                tiles[index] = result[:2]
                 result = result[2:]
             return result if last and not moments else result[0]
 
-        at_once = lax.axis_size(("gx", "gy")) <= 8
         return spread(vector, table, stage, at_once)
 
-    tiles = []
+    tiles = {}
     x1, send = apply(packed, tiles, [x0])
     x2, send = apply(send, tiles, [x1])
     moments = apply(send, tiles, [x0, x1, x2])

time: 65.2 us -> 64.2 us (0.985)
  Pallas kernels: 14.8 us -> 11.9 us
  waiting for transfers between devices: 3.12 us -> 4.18 us
  blocking collectives: 26.2 us -> 27.1 us
    pallas_call x10 -> x7, Pallas kernels: 13 us -> 10.1 us  [the longest x6 8.34 us: stage(): call(functools.partial(stage_kernel, index, result is None, building, las...]
    all_to_all x2, blocking collectives: 15.1 us -> 16.5 us  [plane_exchange(): lax.all_to_all(jnp.broadcast_to(field[None], (size_x * size_y,) + field.s...]
    ppermute x3, waiting for transfers between devices: 0.03 us -> 1.15 us  [swaps(): got = [lax.ppermute(first, axis, matching(count, 0))]]
  transfers between devices with their start and end apart: 7 -> 7, of which waited for: 1 -> 3; matrix products, arithmetic and copies ran while one was open for 0% -> 0% of each run, Pallas kernels for 15% -> 11%
where the time goes in v6:
time: 64.2 us; the launch traced here: 63.9 us
  blocking collectives  27.1 us (42%)
  starting transfers between devices  18.8 us (29%)
  Pallas kernels  11.9 us (19%)
  waiting for transfers between devices  4.18 us (7%)
  between operations  0.99 us (2%)
  local copies, waits for them, and re-layouts  0.79 us (1%)
    all_to_all x2, blocking collectives, plane_exchange(): lax.all_to_all(jnp.broadcast_to(field[None], (size_x * size_y,) + field.s...  16.5 us
    ppermute x3, starting transfers between devices, swaps(): got = [lax.ppermute(first, axis, matching(count, 0))]  11.6 us
    all_to_all x1, blocking collectives, body(): moments = lax.all_to_all(moments, AXES, 0, 0)  10.6 us
    pallas_call x6, Pallas kernels, stage(): call(functools.partial(stage_kernel, index, result is None, building, las...  8.34 us
    all_to_all x1, starting transfers between devices, plane_exchange(): lax.all_to_all(jnp.broadcast_to(field[None], (size_x * size_y,) + field.s...  5.2 us
    all_to_all x1, waiting for transfers between devices, plane_exchange(): lax.all_to_all(jnp.broadcast_to(field[None], (size_x * size_y,) + field.s...  2.96 us
    ppermute x3, starting transfers between devices, swaps(): got.append(lax.ppermute(second, axis, matching(count, 1)))  1.99 us
    pallas_call x1, Pallas kernels, pair_table(): pl.pallas_call(functools.partial(table_kernel, sizes, slots, width, at_on...  1.78 us
  transfers between devices with their start and end apart: 7, of which 3 were waited for; matrix products, arithmetic and copies ran while one was open for 0% of the time, Pallas kernels for 11%

profile of v6, /device:TPU:0, one launch (start us, length us, event | category | flops | bytes accessed | tf_op | source)
XLA Modules:
  0.0 63.9 jit_solution(1114770489904194089)
XLA Ops:
  0.0 0.8 %shard_map.56 = (f32[2,24,128]{2,1,0:T(8,128)S(1)}, f32[2,8,128]{2,1,0:T(8,128)S(1)}, bf16[2,40,128]{2,1,0:T(8,128)(2,1)S(1)}) custom-call(s32[1,1,2]{2,1,0:T(1,128)} %fill_hbm.1, f32[1,1,2,8,384]{4,3,2,1,0:T(8,128)} %noise_hbm.1, f32[1,1,3,2,128]{4,3,2,1,0:T(2,128)} %bitcast.92), custom_call_target="tpu_custom_call" | custom-call | tf_op jit(solution)/shard_map/pallas_call | solution.py:443
  0.8 0.7 %broadcast_in_dim.6 = bf16[8,2,40,128]{3,2,1,0:T(8,128)(2,1)} broadcast(bf16[2,40,128]{2,1,0:T(8,128)(2,1)S(1)} %get-tuple-element.17.refs_1_), dimensions={1,2,3} | broadcast | bytes 184320 | tf_op jit(solution)/shard_map/broadcast_in_dim | solution.py:45
  1.5 5.2 %all-to-all-start = ((bf16[8,2,40,128]{3,2,1,0:T(8,128)(2,1)}), bf16[8,2,40,128]{3,2,1,0:T(8,128)(2,1)S(1)}, u32[]{:S(2)}, u32[]{:S(2)}) async-start(bf16[8,2,40,128]{3,2,1,0:T(8,128)(2,1)} %broadcast_in_dim.6), calls=%async_computation | async-start | bytes 327680 | tf_op jit(solution)/shard_map/all_to_all | solution.py:45
  7.3 1.8 %shard_map.55.refs_0_ = s32[2,348]{1,0:T(2,128)S(1)} custom-call(s32[1,1,1]{2,1,0:T(1,128)S(6)} %copy.60.count_ref, s32[1,1,3,1,54]{4,3,2,1,0:T(1,128)} %bitcast.93), custom_call_target="tpu_custom_call" | custom-call | flops 1000000 | bytes 1000000 | tf_op jit(solution)/shard_map/pallas_call | solution.py:124
  9.1 3.0 %all-to-all-done = bf16[8,2,40,128]{3,2,1,0:T(8,128)(2,1)S(1)} async-done(((bf16[8,2,40,128]{3,2,1,0:T(8,128)(2,1)}), bf16[8,2,40,128]{3,2,1,0:T(8,128)(2,1)S(1)}, u32[]{:S(2)}, u32[]{:S(2)}) %all-to-all-start) | async-done | bytes 163872 | tf_op jit(solution)/shard_map/all_to_all | solution.py:45
  12.2 0.7 %collective-permute-start.1 = (bf16[6,40,128]{2,1,0:T(8,128)(2,1)S(1)}, bf16[6,40,128]{2,1,0:T(8,128)(2,1)S(1)}, u32[]{:S(2)}, u32[]{:S(2)}) collective-permute-start(bf16[6,40,128]{2,1,0:T(8,128)(2,1)S(1)} %get-tuple-element.35), channel_id=1, source_target_pairs={{1,2},{2,1},{5,6},{6,5},{9,10},{10,9},{13,14},{14,13},{17,18},{18,... | collective-permute-start | bytes 184328 | tf_op jit(solution)/shard_map/ppermute | solution.py:38
  12.9 4.5 %collective-permute-start = (bf16[6,40,128]{2,1,0:T(8,128)(2,1)S(1)}, bf16[6,40,128]{2,1,0:T(8,128)(2,1)S(1)}, u32[]{:S(2)}, u32[]{:S(2)}) collective-permute-start(bf16[6,40,128]{2,1,0:T(8,128)(2,1)S(1)} %get-tuple-element.36), channel_id=1, source_target_pairs={{0,1},{1,0},{2,3},{3,2},{4,5},{5,4},{6,7},{7,6},{8,9},{9,8},{10,11... | collective-permute-start | bytes 184328 | tf_op jit(solution)/shard_map/ppermute | solution.py:36
  17.4 2.5 %shard_map.57 = (bf16[15,256,768]{2,1,0:T(8,128)(2,1)S(1)}, bf16[15,256,768]{2,1,0:T(8,128)(2,1)S(1)}, f32[2,24,128]{2,1,0:T(8,128)S(1)}) custom-call(s32[2,348]{1,0:T(2,128)S(1)} %shard_map.55.refs_0_, bf16[2,40,128]{2,1,0:T(8,128)(2,1)S(1)} %get-tuple-element.17.refs_1_, bf16[4,40,128]{2,1,0:T(8,128)(2,1)S(1)} %bitcast.90, ...), custom_call_target="tpu_custom_call" | custom-call | flops 100000000 | bytes 10000000 | tf_op jit(solution)/shard_map/pallas_call | solution.py:477
  19.9 0.0 collective-permute-done.1.refs_6_
  19.9 0.0 collective-permute-done.refs_5_
  19.9 1.5 %shard_map.58 = (bf16[15,256,768]{2,1,0:T(8,128)(2,1)S(1)}, bf16[15,256,768]{2,1,0:T(8,128)(2,1)S(1)}, f32[2,24,128]{2,1,0:T(8,128)S(1)}, bf16[2,24,128]{2,1,0:T(8,128)(2,1)S(1)}) custom-call(s32[2,348]{1,0:T(2,128)S(1)} %shard_map.55.refs_0_, bf16[2,40,128]{2,1,0:T(8,128)(2,1)S(1)} %get-tuple-element.17.refs_1_, ...), custom_call_target="tpu_custom_call" | custom-call | tf_op jit(solution)/shard_map/pallas_call | solution.py:477
  21.4 9.2 %all_to_all.20 = bf16[8,2,24,128]{3,2,1,0:T(8,128)(2,1)S(1)} all-to-all(bf16[8,2,24,128]{3,2,1,0:T(8,128)(2,1)S(1)} %broadcast_in_dim.7), channel_id=1, replica_groups=mesh['gx'=2,'gy'=4,'gz'=4] {'gx','gy'}, dimensions={0} | all-to-all | bytes 196608 | tf_op jit(solution)/shard_map/all_to_all | solution.py:45
  30.7 0.7 %collective-permute-start.3 = (bf16[6,24,128]{2,1,0:T(8,128)(2,1)S(1)}, bf16[6,24,128]{2,1,0:T(8,128)(2,1)S(1)}, u32[]{:S(2)}, u32[]{:S(2)}) collective-permute-start(bf16[6,24,128]{2,1,0:T(8,128)(2,1)S(1)} %get-tuple-element.51), channel_id=1, source_target_pairs={{1,2},{2,1},{5,6},{6,5},{9,10},{10,9},{13,14},{14,13},{17,18},{18,... | collective-permute-start | bytes 110600 | tf_op jit(solution)/shard_map/ppermute | solution.py:38
  31.4 2.5 %collective-permute-start.2 = (bf16[6,24,128]{2,1,0:T(8,128)(2,1)S(1)}, bf16[6,24,128]{2,1,0:T(8,128)(2,1)S(1)}, u32[]{:S(2)}, u32[]{:S(2)}) collective-permute-start(bf16[6,24,128]{2,1,0:T(8,128)(2,1)S(1)} %get-tuple-element.52), channel_id=1, source_target_pairs={{0,1},{1,0},{2,3},{3,2},{4,5},{5,4},{6,7},{7,6},{8,9},{9,8},{10,11... | collective-permute-start | bytes 110600 | tf_op jit(solution)/shard_map/ppermute | solution.py:36
  34.0 1.3 %shard_map.59.refs_3_ = f32[2,24,128]{2,1,0:T(8,128)S(1)} custom-call(s32[2,348]{1,0:T(2,128)S(1)} %shard_map.55.refs_0_, bf16[15,256,768]{2,1,0:T(8,128)(2,1)S(1)} %get-tuple-element.23.refs_1_, bf16[15,256,768]{2,1,0:T(8,128)(2,1)S(1)} %get-tuple-element.24.refs_2_, bf16[4,24,128]{2,1,0:T(8,128)(2,1)S(1)} %bitcast.88, bf16[4,24,128]{2,1,0:T(8,128)(2,1)S(1)} %bitcast.86, ...), custom_call_target="tpu_custom_call" | custom-call | flops 100000000 | bytes 10000000 | tf_op jit(solution)/shard_map/pallas_call | solution.py:477
  35.3 0.0 collective-permute-done.3.refs_7_
  35.3 0.6 collective-permute-done.2.refs_6_
  35.9 0.8 %shard_map.60 = (f32[2,24,128]{2,1,0:T(8,128)S(1)}, bf16[2,24,128]{2,1,0:T(8,128)(2,1)S(1)}) custom-call(s32[2,348]{1,0:T(2,128)S(1)} %shard_map.55.refs_0_, bf16[15,256,768]{2,1,0:T(8,128)(2,1)S(1)} %get-tuple-element.21.refs_1_, bf16[15,256,768]{2,1,0:T(8,128)(2,1)S(1)} %get-tuple-element.22.refs_2_, f32[2,24,128]{2,1,0:T(8,128)S(1)} %shard_map.59.refs_3_, ...), custom_call_target="tpu_custom_call" | custom-call | tf_op jit(solution)/shard_map/pallas_call | solution.py:477
  36.7 7.3 %all_to_all.21 = bf16[8,2,24,128]{3,2,1,0:T(8,128)(2,1)S(1)} all-to-all(bf16[8,2,24,128]{3,2,1,0:T(8,128)(2,1)S(1)} %broadcast_in_dim.8), channel_id=1, replica_groups=mesh['gx'=2,'gy'=4,'gz'=4] {'gx','gy'}, dimensions={0} | all-to-all | bytes 196608 | tf_op jit(solution)/shard_map/all_to_all | solution.py:45
  44.2 0.7 %collective-permute-start.5 = (bf16[6,24,128]{2,1,0:T(8,128)(2,1)S(1)}, bf16[6,24,128]{2,1,0:T(8,128)(2,1)S(1)}, u32[]{:S(2)}, u32[]{:S(2)}) collective-permute-start(bf16[6,24,128]{2,1,0:T(8,128)(2,1)S(1)} %get-tuple-element.49), channel_id=1, source_target_pairs={{1,2},{2,1},{5,6},{6,5},{9,10},{10,9},{13,14},{14,13},{17,18},{18,... | collective-permute-start | bytes 110600 | tf_op jit(solution)/shard_map/ppermute | solution.py:38
  44.8 4.6 %collective-permute-start.4 = (bf16[6,24,128]{2,1,0:T(8,128)(2,1)S(1)}, bf16[6,24,128]{2,1,0:T(8,128)(2,1)S(1)}, u32[]{:S(2)}, u32[]{:S(2)}) collective-permute-start(bf16[6,24,128]{2,1,0:T(8,128)(2,1)S(1)} %get-tuple-element.50), channel_id=1, source_target_pairs={{0,1},{1,0},{2,3},{3,2},{4,5},{5,4},{6,7},{7,6},{8,9},{9,8},{10,11... | collective-permute-start | bytes 110600 | tf_op jit(solution)/shard_map/ppermute | solution.py:36
  49.5 1.3 %shard_map.61.refs_3_ = f32[2,24,128]{2,1,0:T(8,128)S(1)} custom-call(s32[2,348]{1,0:T(2,128)S(1)} %shard_map.55.refs_0_, bf16[15,256,768]{2,1,0:T(8,128)(2,1)S(1)} %get-tuple-element.23.refs_1_, bf16[15,256,768]{2,1,0:T(8,128)(2,1)S(1)} %get-tuple-element.24.refs_2_, bf16[4,24,128]{2,1,0:T(8,128)(2,1)S(1)} %bitcast.87, bf16[4,24,128]{2,1,0:T(8,128)(2,1)S(1)} %bitcast.85, ...), custom_call_target="tpu_custom_call" | custom-call | flops 100000000 | bytes 10000000 | tf_op jit(solution)/shard_map/pallas_call | solution.py:477
  50.8 0.0 collective-permute-done.5.refs_9_
  50.8 0.6 collective-permute-done.4.refs_8_
  51.4 0.9 %shard_map.62 = f32[32,1,128]{2,1,0:T(1,128)S(1)} custom-call(s32[2,348]{1,0:T(2,128)S(1)} %shard_map.55.refs_0_, bf16[15,256,768]{2,1,0:T(8,128)(2,1)S(1)} %get-tuple-element.21.refs_1_, bf16[15,256,768]{2,1,0:T(8,128)(2,1)S(1)} %get-tuple-element.22.refs_2_, f32[2,24,128]{2,1,0:T(8,128)S(1)} %shard_map.61.refs_3_, ...), custom_call_target="tpu_custom_call" | custom-call | tf_op jit(solution)/shard_map/pallas_call | solution.py:477
  52.4 10.6 %all_to_all.22.moment_ref = f32[32,1,128]{2,1,0:T(1,128)S(1)} all-to-all(f32[32,1,128]{2,1,0:T(1,128)S(1)} %shard_map.62), channel_id=1, replica_groups=mesh['gx'=2,'gy'=4,'gz'=4] {'gx','gy','gz'}, dimensions={0} | all-to-all | bytes 32768 | tf_op jit(solution)/shard_map/all_to_all | solution.py:496
  62.9 1.0 %shard_map.63 = f32[1,1,2,8,384]{4,3,2,1,0:T(8,128)} custom-call(f32[32,1,128]{2,1,0:T(1,128)S(1)} %all_to_all.22.moment_ref, f32[2,24,128]{2,1,0:T(8,128)S(1)} %get-tuple-element.20.refs_4_.refs_5_.x0_ref, f32[2,24,128]{2,1,0:T(8,128)S(1)} %get-tuple-element.26.refs_5_.refs_6_.x1_ref, f32[2,24,128]{2,1,0:T(8,128)S(1)} %get-tuple-element.28.refs_7_.x2_ref), custom_call_target="tpu_custom_call" | custom-call | tf_op jit(solution)/shard_map/pallas_call | solution.py:497
  (33 shorter events, 0.3 us)
Async XLA Ops:
  1.5 10.6 %all-to-all-start = ((bf16[8,2,40,128]{3,2,1,0:T(8,128)(2,1)}), bf16[8,2,40,128]{3,2,1,0:T(8,128)(2,1)S(1)}, u32[]{:S(2)}, u32[]{:S(2)}) async-start(bf16[8,2,40,128]{3,2,1,0:T(8,128)(2,1)} %broadcast_in_dim.6), calls=%async_computation | async-start | bytes 327680 | tf_op jit(solution)/shard_map/all_to_all | solution.py:45
  12.2 7.7 %collective-permute-start.1 = (bf16[6,40,128]{2,1,0:T(8,128)(2,1)S(1)}, bf16[6,40,128]{2,1,0:T(8,128)(2,1)S(1)}, u32[]{:S(2)}, u32[]{:S(2)}) collective-permute-start(bf16[6,40,128]{2,1,0:T(8,128)(2,1)S(1)} %get-tuple-element.35), channel_id=1, source_target_pairs={{1,2},{2,1},{5,6},{6,5},{9,10},{10,9},{13,14},{14,13},{17,18},{18,... | collective-permute-start | bytes 184328 | tf_op jit(solution)/shard_map/ppermute | solution.py:38
  12.9 7.0 %collective-permute-start = (bf16[6,40,128]{2,1,0:T(8,128)(2,1)S(1)}, bf16[6,40,128]{2,1,0:T(8,128)(2,1)S(1)}, u32[]{:S(2)}, u32[]{:S(2)}) collective-permute-start(bf16[6,40,128]{2,1,0:T(8,128)(2,1)S(1)} %get-tuple-element.36), channel_id=1, source_target_pairs={{0,1},{1,0},{2,3},{3,2},{4,5},{5,4},{6,7},{7,6},{8,9},{9,8},{10,11... | collective-permute-start | bytes 184328 | tf_op jit(solution)/shard_map/ppermute | solution.py:36
  30.7 4.6 %collective-permute-start.3 = (bf16[6,24,128]{2,1,0:T(8,128)(2,1)S(1)}, bf16[6,24,128]{2,1,0:T(8,128)(2,1)S(1)}, u32[]{:S(2)}, u32[]{:S(2)}) collective-permute-start(bf16[6,24,128]{2,1,0:T(8,128)(2,1)S(1)} %get-tuple-element.51), channel_id=1, source_target_pairs={{1,2},{2,1},{5,6},{6,5},{9,10},{10,9},{13,14},{14,13},{17,18},{18,... | collective-permute-start | bytes 110600 | tf_op jit(solution)/shard_map/ppermute | solution.py:38
  31.4 4.5 %collective-permute-start.2 = (bf16[6,24,128]{2,1,0:T(8,128)(2,1)S(1)}, bf16[6,24,128]{2,1,0:T(8,128)(2,1)S(1)}, u32[]{:S(2)}, u32[]{:S(2)}) collective-permute-start(bf16[6,24,128]{2,1,0:T(8,128)(2,1)S(1)} %get-tuple-element.52), channel_id=1, source_target_pairs={{0,1},{1,0},{2,3},{3,2},{4,5},{5,4},{6,7},{7,6},{8,9},{9,8},{10,11... | collective-permute-start | bytes 110600 | tf_op jit(solution)/shard_map/ppermute | solution.py:36
  44.2 6.7 %collective-permute-start.5 = (bf16[6,24,128]{2,1,0:T(8,128)(2,1)S(1)}, bf16[6,24,128]{2,1,0:T(8,128)(2,1)S(1)}, u32[]{:S(2)}, u32[]{:S(2)}) collective-permute-start(bf16[6,24,128]{2,1,0:T(8,128)(2,1)S(1)} %get-tuple-element.49), channel_id=1, source_target_pairs={{1,2},{2,1},{5,6},{6,5},{9,10},{10,9},{13,14},{14,13},{17,18},{18,... | collective-permute-start | bytes 110600 | tf_op jit(solution)/shard_map/ppermute | solution.py:38
  44.8 6.6 %collective-permute-start.4 = (bf16[6,24,128]{2,1,0:T(8,128)(2,1)S(1)}, bf16[6,24,128]{2,1,0:T(8,128)(2,1)S(1)}, u32[]{:S(2)}, u32[]{:S(2)}) collective-permute-start(bf16[6,24,128]{2,1,0:T(8,128)(2,1)S(1)} %get-tuple-element.50), channel_id=1, source_target_pairs={{0,1},{1,0},{2,3},{3,2},{4,5},{5,4},{6,7},{7,6},{8,9},{9,8},{10,11... | collective-permute-start | bytes 110600 | tf_op jit(solution)/shard_map/ppermute | solution.py:36

commit v7 on v6

--- a/solution.py
+++ b/solution.py
@@ -171,7 +171,8 @@
             mid = rest.astype(bf16).astype(f32)
             for i, piece in ((0, high), (8, mid), (3, rest - mid)):
                 place = jnp.where(row == i + c, piece, place)
-        pack_ref[block] = jnp.concatenate([start, place], axis=0).astype(bf16)
+        rest = start - start.astype(bf16).astype(f32)
+        pack_ref[block] = jnp.concatenate([start, rest, place], axis=0).astype(bf16)
 
 
 def gather_slots(parts, slots_ref):
@@ -260,14 +261,15 @@
 
     def prepare(duo, columns_ref):
         first = first_of(duo)
-        columns_ref[:, :8] = turn_positions(slots_ref, table_ref[0, first], table_ref[0, first + 1], rows)
+        columns_ref[:, :8] = turn_positions(slots_ref, table_ref[0, first], table_ref[0, first + 1], 2 * rows)
 
     def consume(duo, tile, index):
-        field = field_of(table_ref, slots_ref, first_of(duo), rows)
-        add_product(sum_ref, jnp.minimum(home_of(duo), blocks - 1), product(field, tile[index]))
+        field = field_of(table_ref, slots_ref, first_of(duo), 2 * rows)
+        both_parts = product(field, tile[index])
+        add_product(sum_ref, jnp.minimum(home_of(duo), blocks - 1), both_parts[:rows] + both_parts[rows:])
 
     def make(duo, columns_ref, tile, index):
-        place = position_of(own_ref, home_of(duo), rows)
+        place = position_of(own_ref, home_of(duo), 2 * rows)
         for i in range(2):
             make_tile(place, columns_ref, tile, index, i)
 
@@ -445,7 +447,7 @@
         (
             jax.ShapeDtypeStruct(shape, f32),
             jax.ShapeDtypeStruct((blocks, 8, beads), f32),
-            jax.ShapeDtypeStruct((blocks, rows + 16, beads), bf16),
+            jax.ShapeDtypeStruct((blocks, 2 * rows + 16, beads), bf16),
         ),
         [HBM] * 3,
         (

time: 64.2 us -> 65.7 us (1.023)
  Pallas kernels: 11.9 us -> 9.68 us
  waiting for transfers between devices: 4.18 us -> 6.07 us
  starting transfers between devices: 18.8 us -> 20 us
    pallas_call x6, Pallas kernels: 8.34 us -> 6.35 us  [stage(): call(functools.partial(stage_kernel, index, result is None, building, las...]
    ppermute x3, starting transfers between devices: 11.6 us -> 12.8 us  [swaps(): got = [lax.ppermute(first, axis, matching(count, 0))]]
    ppermute x3, waiting for transfers between devices: 1.15 us -> 2.11 us  [swaps(): got = [lax.ppermute(first, axis, matching(count, 0))]]
    all_to_all x1, waiting for transfers between devices: 2.96 us -> 3.88 us  [plane_exchange(): lax.all_to_all(jnp.broadcast_to(field[None], (size_x * size_y,) + field.s...]
  transfers between devices with their start and end apart: 7 -> 7, of which waited for: 3 -> 4; matrix products, arithmetic and copies ran while one was open for 0% -> 0% of each run, Pallas kernels for 11% -> 9%
where the time goes in v7:
time: 65.7 us; the launch traced here: 65.2 us
  blocking collectives  27.4 us (42%)
  starting transfers between devices  20 us (30%)
  Pallas kernels  9.68 us (15%)
  waiting for transfers between devices  6.07 us (9%)
  between operations  0.99 us (2%)
  local copies, waits for them, and re-layouts  0.86 us (1%)
    all_to_all x2, blocking collectives, plane_exchange(): lax.all_to_all(jnp.broadcast_to(field[None], (size_x * size_y,) + field.s...  17 us
    ppermute x3, starting transfers between devices, swaps(): got = [lax.ppermute(first, axis, matching(count, 0))]  12.8 us
    all_to_all x1, blocking collectives, body(): moments = lax.all_to_all(moments, AXES, 0, 0)  10.4 us
    pallas_call x6, Pallas kernels, stage(): call(functools.partial(stage_kernel, index, result is None, building, las...  6.35 us
    all_to_all x1, starting transfers between devices, plane_exchange(): lax.all_to_all(jnp.broadcast_to(field[None], (size_x * size_y,) + field.s...  5.2 us
    all_to_all x1, waiting for transfers between devices, plane_exchange(): lax.all_to_all(jnp.broadcast_to(field[None], (size_x * size_y,) + field.s...  3.88 us
    ppermute x3, waiting for transfers between devices, swaps(): got = [lax.ppermute(first, axis, matching(count, 0))]  2.11 us
    ppermute x3, starting transfers between devices, swaps(): got.append(lax.ppermute(second, axis, matching(count, 1)))  1.99 us
  transfers between devices with their start and end apart: 7, of which 4 were waited for; matrix products, arithmetic and copies ran while one was open for 0% of the time, Pallas kernels for 9%

profile of v7, /device:TPU:0, one launch (start us, length us, event | category | flops | bytes accessed | tf_op | source)
XLA Modules:
  0.0 65.2 jit_solution(8551605119585737171)
XLA Ops:
  0.0 0.8 %shard_map.56 = (f32[2,24,128]{2,1,0:T(8,128)S(1)}, f32[2,8,128]{2,1,0:T(8,128)S(1)}, bf16[2,64,128]{2,1,0:T(8,128)(2,1)S(1)}) custom-call(s32[1,1,2]{2,1,0:T(1,128)} %fill_hbm.1, f32[1,1,2,8,384]{4,3,2,1,0:T(8,128)} %noise_hbm.1, f32[1,1,3,2,128]{4,3,2,1,0:T(2,128)} %bitcast.92), custom_call_target="tpu_custom_call" | custom-call | tf_op jit(solution)/shard_map/pallas_call | solution.py:445
  0.8 0.8 %broadcast_in_dim.6 = bf16[8,2,64,128]{3,2,1,0:T(8,128)(2,1)} broadcast(bf16[2,64,128]{2,1,0:T(8,128)(2,1)S(1)} %get-tuple-element.17.refs_1_), dimensions={1,2,3} | broadcast | bytes 294912 | tf_op jit(solution)/shard_map/broadcast_in_dim | solution.py:45
  1.6 5.2 %all-to-all-start = ((bf16[8,2,64,128]{3,2,1,0:T(8,128)(2,1)}), bf16[8,2,64,128]{3,2,1,0:T(8,128)(2,1)S(1)}, u32[]{:S(2)}, u32[]{:S(2)}) async-start(bf16[8,2,64,128]{3,2,1,0:T(8,128)(2,1)} %broadcast_in_dim.6), calls=%async_computation | async-start | bytes 524288 | tf_op jit(solution)/shard_map/all_to_all | solution.py:45
  7.4 1.6 %shard_map.55.refs_0_ = s32[2,348]{1,0:T(2,128)S(1)} custom-call(s32[1,1,1]{2,1,0:T(1,128)S(6)} %copy.60.count_ref, s32[1,1,3,1,54]{4,3,2,1,0:T(1,128)} %bitcast.93), custom_call_target="tpu_custom_call" | custom-call | flops 1000000 | bytes 1000000 | tf_op jit(solution)/shard_map/pallas_call | solution.py:124
  9.0 3.9 %all-to-all-done = bf16[8,2,64,128]{3,2,1,0:T(8,128)(2,1)S(1)} async-done(((bf16[8,2,64,128]{3,2,1,0:T(8,128)(2,1)}), bf16[8,2,64,128]{3,2,1,0:T(8,128)(2,1)S(1)}, u32[]{:S(2)}, u32[]{:S(2)}) %all-to-all-start) | async-done | bytes 262176 | tf_op jit(solution)/shard_map/all_to_all | solution.py:45
  13.0 0.7 %collective-permute-start.1 = (bf16[6,64,128]{2,1,0:T(8,128)(2,1)S(1)}, bf16[6,64,128]{2,1,0:T(8,128)(2,1)S(1)}, u32[]{:S(2)}, u32[]{:S(2)}) collective-permute-start(bf16[6,64,128]{2,1,0:T(8,128)(2,1)S(1)} %get-tuple-element.35), channel_id=1, source_target_pairs={{1,2},{2,1},{5,6},{6,5},{9,10},{10,9},{13,14},{14,13},{17,18},{18,... | collective-permute-start | bytes 294920 | tf_op jit(solution)/shard_map/ppermute | solution.py:38
  13.7 4.5 %collective-permute-start = (bf16[6,64,128]{2,1,0:T(8,128)(2,1)S(1)}, bf16[6,64,128]{2,1,0:T(8,128)(2,1)S(1)}, u32[]{:S(2)}, u32[]{:S(2)}) collective-permute-start(bf16[6,64,128]{2,1,0:T(8,128)(2,1)S(1)} %get-tuple-element.36), channel_id=1, source_target_pairs={{0,1},{1,0},{2,3},{3,2},{4,5},{5,4},{6,7},{7,6},{8,9},{9,8},{10,11... | collective-permute-start | bytes 294920 | tf_op jit(solution)/shard_map/ppermute | solution.py:36
  18.2 2.0 %shard_map.57 = (bf16[15,256,768]{2,1,0:T(8,128)(2,1)S(1)}, bf16[15,256,768]{2,1,0:T(8,128)(2,1)S(1)}, f32[2,24,128]{2,1,0:T(8,128)S(1)}) custom-call(s32[2,348]{1,0:T(2,128)S(1)} %shard_map.55.refs_0_, bf16[2,64,128]{2,1,0:T(8,128)(2,1)S(1)} %get-tuple-element.17.refs_1_, bf16[4,64,128]{2,1,0:T(8,128)(2,1)S(1)} %bitcast.90, ...), custom_call_target="tpu_custom_call" | custom-call | flops 100000000 | bytes 10000000 | tf_op jit(solution)/shard_map/pallas_call | solution.py:479
  20.2 0.0 collective-permute-done.1.refs_6_
  20.2 0.5 collective-permute-done.refs_5_
  20.7 0.9 %shard_map.58 = (bf16[15,256,768]{2,1,0:T(8,128)(2,1)S(1)}, bf16[15,256,768]{2,1,0:T(8,128)(2,1)S(1)}, f32[2,24,128]{2,1,0:T(8,128)S(1)}, bf16[2,24,128]{2,1,0:T(8,128)(2,1)S(1)}) custom-call(s32[2,348]{1,0:T(2,128)S(1)} %shard_map.55.refs_0_, bf16[2,64,128]{2,1,0:T(8,128)(2,1)S(1)} %get-tuple-element.17.refs_1_, ...), custom_call_target="tpu_custom_call" | custom-call | tf_op jit(solution)/shard_map/pallas_call | solution.py:479
  21.7 9.7 %all_to_all.20 = bf16[8,2,24,128]{3,2,1,0:T(8,128)(2,1)S(1)} all-to-all(bf16[8,2,24,128]{3,2,1,0:T(8,128)(2,1)S(1)} %broadcast_in_dim.7), channel_id=1, replica_groups=mesh['gx'=2,'gy'=4,'gz'=4] {'gx','gy'}, dimensions={0} | all-to-all | bytes 196608 | tf_op jit(solution)/shard_map/all_to_all | solution.py:45
  31.5 0.7 %collective-permute-start.3 = (bf16[6,24,128]{2,1,0:T(8,128)(2,1)S(1)}, bf16[6,24,128]{2,1,0:T(8,128)(2,1)S(1)}, u32[]{:S(2)}, u32[]{:S(2)}) collective-permute-start(bf16[6,24,128]{2,1,0:T(8,128)(2,1)S(1)} %get-tuple-element.51), channel_id=1, source_target_pairs={{1,2},{2,1},{5,6},{6,5},{9,10},{10,9},{13,14},{14,13},{17,18},{18,... | collective-permute-start | bytes 110600 | tf_op jit(solution)/shard_map/ppermute | solution.py:38
  32.1 3.2 %collective-permute-start.2 = (bf16[6,24,128]{2,1,0:T(8,128)(2,1)S(1)}, bf16[6,24,128]{2,1,0:T(8,128)(2,1)S(1)}, u32[]{:S(2)}, u32[]{:S(2)}) collective-permute-start(bf16[6,24,128]{2,1,0:T(8,128)(2,1)S(1)} %get-tuple-element.52), channel_id=1, source_target_pairs={{0,1},{1,0},{2,3},{3,2},{4,5},{5,4},{6,7},{7,6},{8,9},{9,8},{10,11... | collective-permute-start | bytes 110600 | tf_op jit(solution)/shard_map/ppermute | solution.py:36
  35.4 1.0 %shard_map.59.refs_3_ = f32[2,24,128]{2,1,0:T(8,128)S(1)} custom-call(s32[2,348]{1,0:T(2,128)S(1)} %shard_map.55.refs_0_, bf16[15,256,768]{2,1,0:T(8,128)(2,1)S(1)} %get-tuple-element.23.refs_1_, bf16[15,256,768]{2,1,0:T(8,128)(2,1)S(1)} %get-tuple-element.24.refs_2_, bf16[4,24,128]{2,1,0:T(8,128)(2,1)S(1)} %bitcast.88, bf16[4,24,128]{2,1,0:T(8,128)(2,1)S(1)} %bitcast.86, ...), custom_call_target="tpu_custom_call" | custom-call | flops 100000000 | bytes 10000000 | tf_op jit(solution)/shard_map/pallas_call | solution.py:479
  36.4 0.0 collective-permute-done.3.refs_7_
  36.5 0.8 %collective-permute-done.2.refs_6_ = bf16[6,24,128]{2,1,0:T(8,128)(2,1)S(1)} collective-permute-done((bf16[6,24,128]{2,1,0:T(8,128)(2,1)S(1)}, bf16[6,24,128]{2,1,0:T(8,128)(2,1)S(1)}, u32[]{:S(2)}, u32[]{:S(2)}) %collective-permute-start.2) | collective-permute-done | bytes 36896 | tf_op jit(solution)/shard_map/ppermute | solution.py:36
  37.3 0.6 shard_map.60
  37.9 7.3 %all_to_all.21 = bf16[8,2,24,128]{3,2,1,0:T(8,128)(2,1)S(1)} all-to-all(bf16[8,2,24,128]{3,2,1,0:T(8,128)(2,1)S(1)} %broadcast_in_dim.8), channel_id=1, replica_groups=mesh['gx'=2,'gy'=4,'gz'=4] {'gx','gy'}, dimensions={0} | all-to-all | bytes 196608 | tf_op jit(solution)/shard_map/all_to_all | solution.py:45
  45.3 0.7 %collective-permute-start.5 = (bf16[6,24,128]{2,1,0:T(8,128)(2,1)S(1)}, bf16[6,24,128]{2,1,0:T(8,128)(2,1)S(1)}, u32[]{:S(2)}, u32[]{:S(2)}) collective-permute-start(bf16[6,24,128]{2,1,0:T(8,128)(2,1)S(1)} %get-tuple-element.49), channel_id=1, source_target_pairs={{1,2},{2,1},{5,6},{6,5},{9,10},{10,9},{13,14},{14,13},{17,18},{18,... | collective-permute-start | bytes 110600 | tf_op jit(solution)/shard_map/ppermute | solution.py:38
  46.0 5.2 %collective-permute-start.4 = (bf16[6,24,128]{2,1,0:T(8,128)(2,1)S(1)}, bf16[6,24,128]{2,1,0:T(8,128)(2,1)S(1)}, u32[]{:S(2)}, u32[]{:S(2)}) collective-permute-start(bf16[6,24,128]{2,1,0:T(8,128)(2,1)S(1)} %get-tuple-element.50), channel_id=1, source_target_pairs={{0,1},{1,0},{2,3},{3,2},{4,5},{5,4},{6,7},{7,6},{8,9},{9,8},{10,11... | collective-permute-start | bytes 110600 | tf_op jit(solution)/shard_map/ppermute | solution.py:36
  51.2 1.0 %shard_map.61.refs_3_ = f32[2,24,128]{2,1,0:T(8,128)S(1)} custom-call(s32[2,348]{1,0:T(2,128)S(1)} %shard_map.55.refs_0_, bf16[15,256,768]{2,1,0:T(8,128)(2,1)S(1)} %get-tuple-element.23.refs_1_, bf16[15,256,768]{2,1,0:T(8,128)(2,1)S(1)} %get-tuple-element.24.refs_2_, bf16[4,24,128]{2,1,0:T(8,128)(2,1)S(1)} %bitcast.87, bf16[4,24,128]{2,1,0:T(8,128)(2,1)S(1)} %bitcast.85, ...), custom_call_target="tpu_custom_call" | custom-call | flops 100000000 | bytes 10000000 | tf_op jit(solution)/shard_map/pallas_call | solution.py:479
  52.2 0.0 collective-permute-done.5.refs_9_
  52.3 0.8 %collective-permute-done.4.refs_8_ = bf16[6,24,128]{2,1,0:T(8,128)(2,1)S(1)} collective-permute-done((bf16[6,24,128]{2,1,0:T(8,128)(2,1)S(1)}, bf16[6,24,128]{2,1,0:T(8,128)(2,1)S(1)}, u32[]{:S(2)}, u32[]{:S(2)}) %collective-permute-start.4) | collective-permute-done | bytes 36896 | tf_op jit(solution)/shard_map/ppermute | solution.py:36
  53.1 0.7 %shard_map.62 = f32[32,1,128]{2,1,0:T(1,128)S(1)} custom-call(s32[2,348]{1,0:T(2,128)S(1)} %shard_map.55.refs_0_, bf16[15,256,768]{2,1,0:T(8,128)(2,1)S(1)} %get-tuple-element.21.refs_1_, bf16[15,256,768]{2,1,0:T(8,128)(2,1)S(1)} %get-tuple-element.22.refs_2_, f32[2,24,128]{2,1,0:T(8,128)S(1)} %shard_map.61.refs_3_, ...), custom_call_target="tpu_custom_call" | custom-call | tf_op jit(solution)/shard_map/pallas_call | solution.py:479
  53.8 10.4 %all_to_all.22.moment_ref = f32[32,1,128]{2,1,0:T(1,128)S(1)} all-to-all(f32[32,1,128]{2,1,0:T(1,128)S(1)} %shard_map.62), channel_id=1, replica_groups=mesh['gx'=2,'gy'=4,'gz'=4] {'gx','gy','gz'}, dimensions={0} | all-to-all | bytes 32768 | tf_op jit(solution)/shard_map/all_to_all | solution.py:498
  64.2 1.0 %shard_map.63 = f32[1,1,2,8,384]{4,3,2,1,0:T(8,128)} custom-call(f32[32,1,128]{2,1,0:T(1,128)S(1)} %all_to_all.22.moment_ref, f32[2,24,128]{2,1,0:T(8,128)S(1)} %get-tuple-element.20.refs_4_.refs_5_.x0_ref, f32[2,24,128]{2,1,0:T(8,128)S(1)} %get-tuple-element.26.refs_5_.refs_6_.x1_ref, f32[2,24,128]{2,1,0:T(8,128)S(1)} %get-tuple-element.28.refs_7_.x2_ref), custom_call_target="tpu_custom_call" | custom-call | tf_op jit(solution)/shard_map/pallas_call | solution.py:499
  (33 shorter events, 0.3 us)
Async XLA Ops:
  1.6 11.3 %all-to-all-start = ((bf16[8,2,64,128]{3,2,1,0:T(8,128)(2,1)}), bf16[8,2,64,128]{3,2,1,0:T(8,128)(2,1)S(1)}, u32[]{:S(2)}, u32[]{:S(2)}) async-start(bf16[8,2,64,128]{3,2,1,0:T(8,128)(2,1)} %broadcast_in_dim.6), calls=%async_computation | async-start | bytes 524288 | tf_op jit(solution)/shard_map/all_to_all | solution.py:45
  13.0 7.2 %collective-permute-start.1 = (bf16[6,64,128]{2,1,0:T(8,128)(2,1)S(1)}, bf16[6,64,128]{2,1,0:T(8,128)(2,1)S(1)}, u32[]{:S(2)}, u32[]{:S(2)}) collective-permute-start(bf16[6,64,128]{2,1,0:T(8,128)(2,1)S(1)} %get-tuple-element.35), channel_id=1, source_target_pairs={{1,2},{2,1},{5,6},{6,5},{9,10},{10,9},{13,14},{14,13},{17,18},{18,... | collective-permute-start | bytes 294920 | tf_op jit(solution)/shard_map/ppermute | solution.py:38
  13.7 7.1 %collective-permute-start = (bf16[6,64,128]{2,1,0:T(8,128)(2,1)S(1)}, bf16[6,64,128]{2,1,0:T(8,128)(2,1)S(1)}, u32[]{:S(2)}, u32[]{:S(2)}) collective-permute-start(bf16[6,64,128]{2,1,0:T(8,128)(2,1)S(1)} %get-tuple-element.36), channel_id=1, source_target_pairs={{0,1},{1,0},{2,3},{3,2},{4,5},{5,4},{6,7},{7,6},{8,9},{9,8},{10,11... | collective-permute-start | bytes 294920 | tf_op jit(solution)/shard_map/ppermute | solution.py:36
  31.5 5.0 %collective-permute-start.3 = (bf16[6,24,128]{2,1,0:T(8,128)(2,1)S(1)}, bf16[6,24,128]{2,1,0:T(8,128)(2,1)S(1)}, u32[]{:S(2)}, u32[]{:S(2)}) collective-permute-start(bf16[6,24,128]{2,1,0:T(8,128)(2,1)S(1)} %get-tuple-element.51), channel_id=1, source_target_pairs={{1,2},{2,1},{5,6},{6,5},{9,10},{10,9},{13,14},{14,13},{17,18},{18,... | collective-permute-start | bytes 110600 | tf_op jit(solution)/shard_map/ppermute | solution.py:38
  32.1 5.1 %collective-permute-start.2 = (bf16[6,24,128]{2,1,0:T(8,128)(2,1)S(1)}, bf16[6,24,128]{2,1,0:T(8,128)(2,1)S(1)}, u32[]{:S(2)}, u32[]{:S(2)}) collective-permute-start(bf16[6,24,128]{2,1,0:T(8,128)(2,1)S(1)} %get-tuple-element.52), channel_id=1, source_target_pairs={{0,1},{1,0},{2,3},{3,2},{4,5},{5,4},{6,7},{7,6},{8,9},{9,8},{10,11... | collective-permute-start | bytes 110600 | tf_op jit(solution)/shard_map/ppermute | solution.py:36
  45.3 6.9 %collective-permute-start.5 = (bf16[6,24,128]{2,1,0:T(8,128)(2,1)S(1)}, bf16[6,24,128]{2,1,0:T(8,128)(2,1)S(1)}, u32[]{:S(2)}, u32[]{:S(2)}) collective-permute-start(bf16[6,24,128]{2,1,0:T(8,128)(2,1)S(1)} %get-tuple-element.49), channel_id=1, source_target_pairs={{1,2},{2,1},{5,6},{6,5},{9,10},{10,9},{13,14},{14,13},{17,18},{18,... | collective-permute-start | bytes 110600 | tf_op jit(solution)/shard_map/ppermute | solution.py:38
  46.0 7.1 %collective-permute-start.4 = (bf16[6,24,128]{2,1,0:T(8,128)(2,1)S(1)}, bf16[6,24,128]{2,1,0:T(8,128)(2,1)S(1)}, u32[]{:S(2)}, u32[]{:S(2)}) collective-permute-start(bf16[6,24,128]{2,1,0:T(8,128)(2,1)S(1)} %get-tuple-element.50), channel_id=1, source_target_pairs={{0,1},{1,0},{2,3},{3,2},{4,5},{5,4},{6,7},{7,6},{8,9},{9,8},{10,11... | collective-permute-start | bytes 110600 | tf_op jit(solution)/shard_map/ppermute | solution.py:36

commit v8 on v6

--- a/solution.py
+++ b/solution.py
@@ -39,10 +39,12 @@
     return got
 
 
-def plane_exchange(field):
+def plane_exchange(field, wide):
     plane = ("gx", "gy")
     size_x, size_y = [lax.axis_size(axis) for axis in plane]
-    got = lax.all_to_all(jnp.broadcast_to(field[None], (size_x * size_y,) + field.shape), plane, 0, 0)
+    if wide is None:
+        wide = jnp.broadcast_to(field[None], (size_x * size_y,) + field.shape)
+    got = lax.all_to_all(wide, plane, 0, 0)
     x, y = [lax.axis_index(axis) for axis in plane]
 
     def partners(index, count):
@@ -56,10 +58,10 @@
     return rows[0], rows[1:]
 
 
-def spread(field, table, stage, at_once):
+def spread(field, table, stage, at_once, wide):
     shape = (-1,) + field.shape[1:]
     if at_once:
-        columns, others = plane_exchange(field)
+        columns, others = plane_exchange(field, wide)
     else:
         columns = jnp.stack([field] + swaps("gx", field, field))
         columns, table = lax.optimization_barrier((columns, table))
@@ -147,7 +149,7 @@
     return ends[-1], home_of, first_of
 
 
-def pack_kernel(fill_hbm, noise_hbm, pos_hbm, start_ref, mask_ref, pack_ref, fill_ref, noise_ref, pos_ref, sems):
+def pack_kernel(fill_hbm, noise_hbm, pos_hbm, start_ref, mask_ref, pack_ref, wide_ref, fill_ref, noise_ref, pos_ref, sems):
     pairs = ((fill_hbm, fill_ref), (noise_hbm, noise_ref), (pos_hbm, pos_ref))
     copies = [pltpu.make_async_copy(a, b, sems.at[i]) for i, (a, b) in enumerate(pairs)]
     for copy in copies:
@@ -171,7 +173,10 @@
             mid = rest.astype(bf16).astype(f32)
             for i, piece in ((0, high), (8, mid), (3, rest - mid)):
                 place = jnp.where(row == i + c, piece, place)
-        pack_ref[block] = jnp.concatenate([start, place], axis=0).astype(bf16)
+        packed = jnp.concatenate([start, place], axis=0).astype(bf16)
+        pack_ref[block] = packed
+        for copy in range(wide_ref.shape[0]):
+            wide_ref[copy, block] = packed
 
 
 def gather_slots(parts, slots_ref):
@@ -440,12 +445,14 @@
     slots = (columns * blocks, middle * columns * blocks, sides * (1 + others) * columns)
     limit = 8 << 20
 
-    x0, mask, packed = call(
+    wide = lax.axis_size(("gx", "gy")) if at_once else 1
+    x0, mask, packed, packed_wide = call(
         pack_kernel,
         (
             jax.ShapeDtypeStruct(shape, f32),
             jax.ShapeDtypeStruct((blocks, 8, beads), f32),
             jax.ShapeDtypeStruct((blocks, rows + 16, beads), bf16),
+            jax.ShapeDtypeStruct((wide, blocks, rows + 16, beads), bf16),
         ),
         [HBM] * 3,
         (
@@ -487,7 +494,7 @@
                 result = result[2:]
             return result if last and not moments else result[0]
 
-        return spread(vector, table, stage, at_once)
+        return spread(vector, table, stage, at_once, packed_wide if building else None)
 
     tiles = {}
     x1, send = apply(packed, tiles, [x0])

time: 64.2 us -> 64.4 us (level)
  starting transfers between devices: 18.8 us -> 20.5 us
  blocking collectives: 27.1 us -> 25.9 us
  waiting for transfers between devices: 4.18 us -> 5.04 us
  Pallas kernels: 11.9 us -> 11.2 us
  local copies, waits for them, and re-layouts: 0.79 us -> 0.1 us
    ppermute x3, starting transfers between devices: 11.6 us -> 13.3 us  [swaps(): got = [lax.ppermute(first, axis, matching(count, 0))]]
    all_to_all x2, blocking collectives: 16.5 us -> 15.3 us  [plane_exchange(): got = lax.all_to_all(wide, plane, 0, 0)]
    pallas_call x6, Pallas kernels: 8.34 us -> 7.2 us  [stage(): call(functools.partial(stage_kernel, index, result is None, building, las...]
    broadcast_in_dim x3 -> x2, local copies, waits for them, and re-layouts: 0.72 us -> 0.03 us  [plane_exchange(): wide = jnp.broadcast_to(field[None], (size_x * size_y,) + field.shape)]
    ppermute x3, waiting for transfers between devices: 1.15 us -> 1.84 us  [swaps(): got = [lax.ppermute(first, axis, matching(count, 0))]]
    pallas_call x1, Pallas kernels: 0.78 us -> 1.46 us  [body(): call(pack_kernel, (jax.ShapeDtypeStruct(shape, f32), jax.ShapeDtypeStruct...]
  transfers between devices with their start and end apart: 7 -> 7, of which waited for: 3 -> 4; matrix products, arithmetic and copies ran while one was open for 0% -> 0% of each run, Pallas kernels for 11% -> 9%
where the time goes in v8:
time: 64.4 us; the launch traced here: 63.9 us
  blocking collectives  25.9 us (40%)
  starting transfers between devices  20.5 us (32%)
  Pallas kernels  11.2 us (17%)
  waiting for transfers between devices  5.04 us (8%)
  between operations  0.98 us (2%)
    all_to_all x2, blocking collectives, plane_exchange(): got = lax.all_to_all(wide, plane, 0, 0)  15.3 us
    ppermute x3, starting transfers between devices, swaps(): got = [lax.ppermute(first, axis, matching(count, 0))]  13.3 us
    all_to_all x1, blocking collectives, body(): moments = lax.all_to_all(moments, AXES, 0, 0)  10.6 us
    pallas_call x6, Pallas kernels, stage(): call(functools.partial(stage_kernel, index, result is None, building, las...  7.2 us
    all_to_all x1, starting transfers between devices, plane_exchange(): got = lax.all_to_all(wide, plane, 0, 0)  5.21 us
    all_to_all x1, waiting for transfers between devices, plane_exchange(): got = lax.all_to_all(wide, plane, 0, 0)  3.14 us
    ppermute x3, starting transfers between devices, swaps(): got.append(lax.ppermute(second, axis, matching(count, 1)))  1.99 us
    ppermute x3, waiting for transfers between devices, swaps(): got = [lax.ppermute(first, axis, matching(count, 0))]  1.84 us
  transfers between devices with their start and end apart: 7, of which 4 were waited for; matrix products, arithmetic and copies ran while one was open for 0% of the time, Pallas kernels for 9%

profile of v8, /device:TPU:0, one launch (start us, length us, event | category | flops | bytes accessed | tf_op | source)
XLA Modules:
  0.0 63.9 jit_solution(6892757186461979297)
XLA Ops:
  0.0 1.5 %shard_map.56 = (f32[2,24,128]{2,1,0:T(8,128)S(1)}, f32[2,8,128]{2,1,0:T(8,128)S(1)}, bf16[2,40,128]{2,1,0:T(8,128)(2,1)S(1)}, bf16[8,2,40,128]{3,2,1,0:T(8,128)(2,1)}) custom-call(s32[1,1,2]{2,1,0:T(1,128)} %fill_hbm.1, f32[1,1,2,8,384]{4,3,2,1,0:T(8,128)} %noise_hbm.1, f32[1,1,3,2,128]{4,3,2,1,0:T(2,128)} %bitcast.92), custom_call_target="tpu_custom_call" | custom-call | tf_op jit(solution)/shard_map/pallas_call | solution.py:449
  1.5 5.2 %all-to-all-start = ((bf16[8,2,40,128]{3,2,1,0:T(8,128)(2,1)}), bf16[8,2,40,128]{3,2,1,0:T(8,128)(2,1)S(1)}, u32[]{:S(2)}, u32[]{:S(2)}) async-start(bf16[8,2,40,128]{3,2,1,0:T(8,128)(2,1)} %get-tuple-element.19), calls=%async_computation | async-start | bytes 327680 | tf_op jit(solution)/shard_map/all_to_all | solution.py:47
  7.3 1.6 %shard_map.55.refs_0_ = s32[2,348]{1,0:T(2,128)S(1)} custom-call(s32[1,1,1]{2,1,0:T(1,128)S(6)} %copy.62.count_ref, s32[1,1,3,1,54]{4,3,2,1,0:T(1,128)} %bitcast.93), custom_call_target="tpu_custom_call" | custom-call | flops 1000000 | bytes 1000000 | tf_op jit(solution)/shard_map/pallas_call | solution.py:126
  8.9 3.1 %all-to-all-done = bf16[8,2,40,128]{3,2,1,0:T(8,128)(2,1)S(1)} async-done(((bf16[8,2,40,128]{3,2,1,0:T(8,128)(2,1)}), bf16[8,2,40,128]{3,2,1,0:T(8,128)(2,1)S(1)}, u32[]{:S(2)}, u32[]{:S(2)}) %all-to-all-start) | async-done | bytes 163872 | tf_op jit(solution)/shard_map/all_to_all | solution.py:47
  12.2 0.7 %collective-permute-start.1 = (bf16[6,40,128]{2,1,0:T(8,128)(2,1)S(1)}, bf16[6,40,128]{2,1,0:T(8,128)(2,1)S(1)}, u32[]{:S(2)}, u32[]{:S(2)}) collective-permute-start(bf16[6,40,128]{2,1,0:T(8,128)(2,1)S(1)} %get-tuple-element.37), channel_id=1, source_target_pairs={{1,2},{2,1},{5,6},{6,5},{9,10},{10,9},{13,14},{14,13},{17,18},{18,... | collective-permute-start | bytes 184328 | tf_op jit(solution)/shard_map/ppermute | solution.py:38
  12.9 4.5 %collective-permute-start = (bf16[6,40,128]{2,1,0:T(8,128)(2,1)S(1)}, bf16[6,40,128]{2,1,0:T(8,128)(2,1)S(1)}, u32[]{:S(2)}, u32[]{:S(2)}) collective-permute-start(bf16[6,40,128]{2,1,0:T(8,128)(2,1)S(1)} %get-tuple-element.38), channel_id=1, source_target_pairs={{0,1},{1,0},{2,3},{3,2},{4,5},{5,4},{6,7},{7,6},{8,9},{9,8},{10,11... | collective-permute-start | bytes 184328 | tf_op jit(solution)/shard_map/ppermute | solution.py:36
  17.4 1.9 %shard_map.57 = (bf16[15,256,768]{2,1,0:T(8,128)(2,1)S(1)}, bf16[15,256,768]{2,1,0:T(8,128)(2,1)S(1)}, f32[2,24,128]{2,1,0:T(8,128)S(1)}) custom-call(s32[2,348]{1,0:T(2,128)S(1)} %shard_map.55.refs_0_, bf16[2,40,128]{2,1,0:T(8,128)(2,1)S(1)} %get-tuple-element.18.refs_1_, bf16[4,40,128]{2,1,0:T(8,128)(2,1)S(1)} %bitcast.90, ...), custom_call_target="tpu_custom_call" | custom-call | flops 100000000 | bytes 10000000 | tf_op jit(solution)/shard_map/pallas_call | solution.py:484
  19.3 0.0 collective-permute-done.1.refs_6_
  19.3 0.2 collective-permute-done.refs_5_
  19.5 1.4 %shard_map.58 = (bf16[15,256,768]{2,1,0:T(8,128)(2,1)S(1)}, bf16[15,256,768]{2,1,0:T(8,128)(2,1)S(1)}, f32[2,24,128]{2,1,0:T(8,128)S(1)}, bf16[2,24,128]{2,1,0:T(8,128)(2,1)S(1)}) custom-call(s32[2,348]{1,0:T(2,128)S(1)} %shard_map.55.refs_0_, bf16[2,40,128]{2,1,0:T(8,128)(2,1)S(1)} %get-tuple-element.18.refs_1_, ...), custom_call_target="tpu_custom_call" | custom-call | tf_op jit(solution)/shard_map/pallas_call | solution.py:484
  20.9 8.0 %all_to_all.20 = bf16[8,2,24,128]{3,2,1,0:T(8,128)(2,1)S(1)} all-to-all(bf16[8,2,24,128]{3,2,1,0:T(8,128)(2,1)S(1)} %broadcast_in_dim.4), channel_id=1, replica_groups=mesh['gx'=2,'gy'=4,'gz'=4] {'gx','gy'}, dimensions={0} | all-to-all | bytes 196608 | tf_op jit(solution)/shard_map/all_to_all | solution.py:47
  29.0 0.7 %collective-permute-start.3 = (bf16[6,24,128]{2,1,0:T(8,128)(2,1)S(1)}, bf16[6,24,128]{2,1,0:T(8,128)(2,1)S(1)}, u32[]{:S(2)}, u32[]{:S(2)}) collective-permute-start(bf16[6,24,128]{2,1,0:T(8,128)(2,1)S(1)} %get-tuple-element.53), channel_id=1, source_target_pairs={{1,2},{2,1},{5,6},{6,5},{9,10},{10,9},{13,14},{14,13},{17,18},{18,... | collective-permute-start | bytes 110600 | tf_op jit(solution)/shard_map/ppermute | solution.py:38
  29.7 4.2 %collective-permute-start.2 = (bf16[6,24,128]{2,1,0:T(8,128)(2,1)S(1)}, bf16[6,24,128]{2,1,0:T(8,128)(2,1)S(1)}, u32[]{:S(2)}, u32[]{:S(2)}) collective-permute-start(bf16[6,24,128]{2,1,0:T(8,128)(2,1)S(1)} %get-tuple-element.54), channel_id=1, source_target_pairs={{0,1},{1,0},{2,3},{3,2},{4,5},{5,4},{6,7},{7,6},{8,9},{9,8},{10,11... | collective-permute-start | bytes 110600 | tf_op jit(solution)/shard_map/ppermute | solution.py:36
  34.0 1.0 %shard_map.59.refs_3_ = f32[2,24,128]{2,1,0:T(8,128)S(1)} custom-call(s32[2,348]{1,0:T(2,128)S(1)} %shard_map.55.refs_0_, bf16[15,256,768]{2,1,0:T(8,128)(2,1)S(1)} %get-tuple-element.25.refs_1_, bf16[15,256,768]{2,1,0:T(8,128)(2,1)S(1)} %get-tuple-element.26.refs_2_, bf16[4,24,128]{2,1,0:T(8,128)(2,1)S(1)} %bitcast.88, bf16[4,24,128]{2,1,0:T(8,128)(2,1)S(1)} %bitcast.86, ...), custom_call_target="tpu_custom_call" | custom-call | flops 100000000 | bytes 10000000 | tf_op jit(solution)/shard_map/pallas_call | solution.py:484
  35.0 0.0 collective-permute-done.3.refs_7_
  35.1 0.8 %collective-permute-done.2.refs_6_ = bf16[6,24,128]{2,1,0:T(8,128)(2,1)S(1)} collective-permute-done((bf16[6,24,128]{2,1,0:T(8,128)(2,1)S(1)}, bf16[6,24,128]{2,1,0:T(8,128)(2,1)S(1)}, u32[]{:S(2)}, u32[]{:S(2)}) %collective-permute-start.2) | collective-permute-done | bytes 36896 | tf_op jit(solution)/shard_map/ppermute | solution.py:36
  35.9 0.8 %shard_map.60 = (f32[2,24,128]{2,1,0:T(8,128)S(1)}, bf16[2,24,128]{2,1,0:T(8,128)(2,1)S(1)}) custom-call(s32[2,348]{1,0:T(2,128)S(1)} %shard_map.55.refs_0_, bf16[15,256,768]{2,1,0:T(8,128)(2,1)S(1)} %get-tuple-element.23.refs_1_, bf16[15,256,768]{2,1,0:T(8,128)(2,1)S(1)} %get-tuple-element.24.refs_2_, f32[2,24,128]{2,1,0:T(8,128)S(1)} %shard_map.59.refs_3_, ...), custom_call_target="tpu_custom_call" | custom-call | tf_op jit(solution)/shard_map/pallas_call | solution.py:484
  36.7 7.3 %all_to_all.21 = bf16[8,2,24,128]{3,2,1,0:T(8,128)(2,1)S(1)} all-to-all(bf16[8,2,24,128]{3,2,1,0:T(8,128)(2,1)S(1)} %broadcast_in_dim.5), channel_id=1, replica_groups=mesh['gx'=2,'gy'=4,'gz'=4] {'gx','gy'}, dimensions={0} | all-to-all | bytes 196608 | tf_op jit(solution)/shard_map/all_to_all | solution.py:47
  44.2 0.7 %collective-permute-start.5 = (bf16[6,24,128]{2,1,0:T(8,128)(2,1)S(1)}, bf16[6,24,128]{2,1,0:T(8,128)(2,1)S(1)}, u32[]{:S(2)}, u32[]{:S(2)}) collective-permute-start(bf16[6,24,128]{2,1,0:T(8,128)(2,1)S(1)} %get-tuple-element.51), channel_id=1, source_target_pairs={{1,2},{2,1},{5,6},{6,5},{9,10},{10,9},{13,14},{14,13},{17,18},{18,... | collective-permute-start | bytes 110600 | tf_op jit(solution)/shard_map/ppermute | solution.py:38
  44.8 4.6 %collective-permute-start.4 = (bf16[6,24,128]{2,1,0:T(8,128)(2,1)S(1)}, bf16[6,24,128]{2,1,0:T(8,128)(2,1)S(1)}, u32[]{:S(2)}, u32[]{:S(2)}) collective-permute-start(bf16[6,24,128]{2,1,0:T(8,128)(2,1)S(1)} %get-tuple-element.52), channel_id=1, source_target_pairs={{0,1},{1,0},{2,3},{3,2},{4,5},{5,4},{6,7},{7,6},{8,9},{9,8},{10,11... | collective-permute-start | bytes 110600 | tf_op jit(solution)/shard_map/ppermute | solution.py:36
  49.5 1.0 %shard_map.61.refs_3_ = f32[2,24,128]{2,1,0:T(8,128)S(1)} custom-call(s32[2,348]{1,0:T(2,128)S(1)} %shard_map.55.refs_0_, bf16[15,256,768]{2,1,0:T(8,128)(2,1)S(1)} %get-tuple-element.25.refs_1_, bf16[15,256,768]{2,1,0:T(8,128)(2,1)S(1)} %get-tuple-element.26.refs_2_, bf16[4,24,128]{2,1,0:T(8,128)(2,1)S(1)} %bitcast.87, bf16[4,24,128]{2,1,0:T(8,128)(2,1)S(1)} %bitcast.85, ...), custom_call_target="tpu_custom_call" | custom-call | flops 100000000 | bytes 10000000 | tf_op jit(solution)/shard_map/pallas_call | solution.py:484
  50.5 0.0 collective-permute-done.5.refs_9_
  50.6 0.8 %collective-permute-done.4.refs_8_ = bf16[6,24,128]{2,1,0:T(8,128)(2,1)S(1)} collective-permute-done((bf16[6,24,128]{2,1,0:T(8,128)(2,1)S(1)}, bf16[6,24,128]{2,1,0:T(8,128)(2,1)S(1)}, u32[]{:S(2)}, u32[]{:S(2)}) %collective-permute-start.4) | collective-permute-done | bytes 36896 | tf_op jit(solution)/shard_map/ppermute | solution.py:36
  51.4 0.9 %shard_map.62 = f32[32,1,128]{2,1,0:T(1,128)S(1)} custom-call(s32[2,348]{1,0:T(2,128)S(1)} %shard_map.55.refs_0_, bf16[15,256,768]{2,1,0:T(8,128)(2,1)S(1)} %get-tuple-element.23.refs_1_, bf16[15,256,768]{2,1,0:T(8,128)(2,1)S(1)} %get-tuple-element.24.refs_2_, f32[2,24,128]{2,1,0:T(8,128)S(1)} %shard_map.61.refs_3_, ...), custom_call_target="tpu_custom_call" | custom-call | tf_op jit(solution)/shard_map/pallas_call | solution.py:484
  52.3 10.6 %all_to_all.22.moment_ref = f32[32,1,128]{2,1,0:T(1,128)S(1)} all-to-all(f32[32,1,128]{2,1,0:T(1,128)S(1)} %shard_map.62), channel_id=1, replica_groups=mesh['gx'=2,'gy'=4,'gz'=4] {'gx','gy','gz'}, dimensions={0} | all-to-all | bytes 32768 | tf_op jit(solution)/shard_map/all_to_all | solution.py:503
  62.9 1.0 %shard_map.63 = f32[1,1,2,8,384]{4,3,2,1,0:T(8,128)} custom-call(f32[32,1,128]{2,1,0:T(1,128)S(1)} %all_to_all.22.moment_ref, f32[2,24,128]{2,1,0:T(8,128)S(1)} %get-tuple-element.22.refs_4_.refs_5_.x0_ref, f32[2,24,128]{2,1,0:T(8,128)S(1)} %get-tuple-element.28.refs_5_.refs_6_.x1_ref, f32[2,24,128]{2,1,0:T(8,128)S(1)} %get-tuple-element.30.refs_7_.x2_ref), custom_call_target="tpu_custom_call" | custom-call | tf_op jit(solution)/shard_map/pallas_call | solution.py:504
  (33 shorter events, 0.3 us)
Async XLA Ops:
  1.5 10.6 %all-to-all-start = ((bf16[8,2,40,128]{3,2,1,0:T(8,128)(2,1)}), bf16[8,2,40,128]{3,2,1,0:T(8,128)(2,1)S(1)}, u32[]{:S(2)}, u32[]{:S(2)}) async-start(bf16[8,2,40,128]{3,2,1,0:T(8,128)(2,1)} %get-tuple-element.19), calls=%async_computation | async-start | bytes 327680 | tf_op jit(solution)/shard_map/all_to_all | solution.py:47
  12.2 7.1 %collective-permute-start.1 = (bf16[6,40,128]{2,1,0:T(8,128)(2,1)S(1)}, bf16[6,40,128]{2,1,0:T(8,128)(2,1)S(1)}, u32[]{:S(2)}, u32[]{:S(2)}) collective-permute-start(bf16[6,40,128]{2,1,0:T(8,128)(2,1)S(1)} %get-tuple-element.37), channel_id=1, source_target_pairs={{1,2},{2,1},{5,6},{6,5},{9,10},{10,9},{13,14},{14,13},{17,18},{18,... | collective-permute-start | bytes 184328 | tf_op jit(solution)/shard_map/ppermute | solution.py:38
  12.9 6.7 %collective-permute-start = (bf16[6,40,128]{2,1,0:T(8,128)(2,1)S(1)}, bf16[6,40,128]{2,1,0:T(8,128)(2,1)S(1)}, u32[]{:S(2)}, u32[]{:S(2)}) collective-permute-start(bf16[6,40,128]{2,1,0:T(8,128)(2,1)S(1)} %get-tuple-element.38), channel_id=1, source_target_pairs={{0,1},{1,0},{2,3},{3,2},{4,5},{5,4},{6,7},{7,6},{8,9},{9,8},{10,11... | collective-permute-start | bytes 184328 | tf_op jit(solution)/shard_map/ppermute | solution.py:36
  29.0 6.0 %collective-permute-start.3 = (bf16[6,24,128]{2,1,0:T(8,128)(2,1)S(1)}, bf16[6,24,128]{2,1,0:T(8,128)(2,1)S(1)}, u32[]{:S(2)}, u32[]{:S(2)}) collective-permute-start(bf16[6,24,128]{2,1,0:T(8,128)(2,1)S(1)} %get-tuple-element.53), channel_id=1, source_target_pairs={{1,2},{2,1},{5,6},{6,5},{9,10},{10,9},{13,14},{14,13},{17,18},{18,... | collective-permute-start | bytes 110600 | tf_op jit(solution)/shard_map/ppermute | solution.py:38
  29.7 6.2 %collective-permute-start.2 = (bf16[6,24,128]{2,1,0:T(8,128)(2,1)S(1)}, bf16[6,24,128]{2,1,0:T(8,128)(2,1)S(1)}, u32[]{:S(2)}, u32[]{:S(2)}) collective-permute-start(bf16[6,24,128]{2,1,0:T(8,128)(2,1)S(1)} %get-tuple-element.54), channel_id=1, source_target_pairs={{0,1},{1,0},{2,3},{3,2},{4,5},{5,4},{6,7},{7,6},{8,9},{9,8},{10,11... | collective-permute-start | bytes 110600 | tf_op jit(solution)/shard_map/ppermute | solution.py:36
  44.2 6.4 %collective-permute-start.5 = (bf16[6,24,128]{2,1,0:T(8,128)(2,1)S(1)}, bf16[6,24,128]{2,1,0:T(8,128)(2,1)S(1)}, u32[]{:S(2)}, u32[]{:S(2)}) collective-permute-start(bf16[6,24,128]{2,1,0:T(8,128)(2,1)S(1)} %get-tuple-element.51), channel_id=1, source_target_pairs={{1,2},{2,1},{5,6},{6,5},{9,10},{10,9},{13,14},{14,13},{17,18},{18,... | collective-permute-start | bytes 110600 | tf_op jit(solution)/shard_map/ppermute | solution.py:38
  44.8 6.5 %collective-permute-start.4 = (bf16[6,24,128]{2,1,0:T(8,128)(2,1)S(1)}, bf16[6,24,128]{2,1,0:T(8,128)(2,1)S(1)}, u32[]{:S(2)}, u32[]{:S(2)}) collective-permute-start(bf16[6,24,128]{2,1,0:T(8,128)(2,1)S(1)} %get-tuple-element.52), channel_id=1, source_target_pairs={{0,1},{1,0},{2,3},{3,2},{4,5},{5,4},{6,7},{7,6},{8,9},{9,8},{10,11... | collective-permute-start | bytes 110600 | tf_op jit(solution)/shard_map/ppermute | solution.py:36
